TPU v7x, 32 devices: a whole 2x2x4 slice. The times are simulated.
32 devices in a mesh: dp: 8 (over y, x, core), tensor: 4 (over z).
Axes of the slice: x: 2, y: 2, z: 4, core: 2. Of those that a mesh axis runs over, the one named last changes fastest.
Arguments:
- tokens: bfloat16 [16384, 1536], P('dp'), may hold values from -6 to 6
- cotangent: bfloat16 [16384, 1536], P('dp'), may hold values from -6 to 6
- destination: int32 [16384], P('dp'), may hold values from 0 to 16383, as said below
- lengths: int32 [8, 4], P('dp'), may hold values from 1 to 1024, 2048 in all within a row
- norm_gain: float32 [1536], replicated, may hold values from 0.1 to 1.9
- inner_weight: float32 [1536, 2, 3072], P('dp', None, 'tensor'), may hold values from -0.15625 to 0.15625
- shared_weight: float32 [1536, 256], P('dp'), may hold values from -0.15625 to 0.15625
- step_weight: float32 [1536, 48], P('dp', 'tensor'), may hold values from -0.15625 to 0.15625
- filter_weight: float32 [4, 3072], P(None, 'tensor'), may hold values from -3 to 3
- filter_bias: float32 [3072], P('tensor'), may hold values from -3 to 3
- shared_filter: float32 [4, 256], replicated, may hold values from -3 to 3
- shared_filter_bias: float32 [256], replicated, may hold values from -3 to 3
- step_bias: float32 [48], P('tensor'), may hold values from -6 to -2
- decay_log: float32 [48], P('tensor'), may hold values from 0 to 2.77
- skip_gain: float32 [48], P('tensor'), may hold values from 0.5 to 1.5
- gate_gain: float32 [3072], P('tensor'), may hold values from 0.1 to 1.9
- out_weight: float32 [1536, 3072], P('dp', 'tensor'), may hold values from -0.109375 to 0.109375
Outputs:
- layer_out: bfloat16 [16384, 1536], P('dp')
- input_grad: bfloat16 [16384, 1536], P('dp')
- norm_gain_grad: float32 [1536], replicated
- inner_weight_grad: float32 [1536, 2, 3072], P('dp', None, 'tensor')
- shared_weight_grad: float32 [1536, 256], P('dp')
- step_weight_grad: float32 [1536, 48], P('dp', 'tensor')
- filter_weight_grad: float32 [4, 3072], P(None, 'tensor')
- filter_bias_grad: float32 [3072], P('tensor')
- shared_filter_grad: float32 [4, 256], replicated
- shared_filter_bias_grad: float32 [256], replicated
- step_bias_grad: float32 [48], P('tensor')
- decay_log_grad: float32 [48], P('tensor')
- skip_gain_grad: float32 [48], P('tensor')
- gate_gain_grad: float32 [3072], P('tensor')
- out_weight_grad: float32 [1536, 3072], P('dp', 'tensor')
Inputs may be any that keep to these rules, and one draw needn't show every extreme that they name: destination is a permutation. The tokens at given positions s * 2048 to (s + 1) * 2048 - 1 that go to work block w take exactly the work positions w * 2048 + s * 256 to w * 2048 + (s + 1) * 256 - 1. `lengths`: each row sums to 2048, and its longest sequence has exactly 1024 tokens.
All inputs are finite; a program needn't handle non-finite values.
Results may differ from a plain program's by a relative error of at most 0.012.
Values may be sent and summed in bfloat16 or wider, within the bound.
No kernel may reach another device: no remote copies, remote signals or barrier semaphores. Data moves between devices by JAX's collectives and lax.ppermute only.
A program may use at most 256 MiB of HBM per device.

v0:
```python
import jax
import jax.numpy as jnp
from jax import lax
from jax.sharding import PartitionSpec as P

INNER = 3072
SPAN = 256


EPSILON = 1e-05
PRECISE = lax.Precision.HIGHEST


def segments_of(lengths, row_count):
    seq_ends = jnp.cumsum(lengths)
    seq_starts = seq_ends - lengths
    places = jnp.arange(row_count, dtype=jnp.int32)
    segment = jnp.sum((places[:, None] >= seq_ends[None, :]).astype(jnp.int32), axis=1)
    belongs = segment[:, None] == jnp.arange(lengths.shape[0], dtype=jnp.int32)[None, :]
    position = places - jnp.sum(jnp.where(belongs, seq_starts[None, :], 0), axis=1)
    return (segment, position)


def causal_filter(signal, kernel, offset_bias, position):
    result = offset_bias + kernel[0] * signal
    for offset in range(1, kernel.shape[0]):
        shifted = jnp.pad(signal, ((offset, 0), (0, 0)))[: signal.shape[0]]
        allowed = (position >= offset).astype(signal.dtype)
        result = result + kernel[offset] * shifted * allowed[:, None]
    return result


def mixer(
    inputs,
    shared,
    step_raw,
    filter_weight,
    filter_bias,
    shared_filter,
    shared_filter_bias,
    step_bias,
    decay_log,
    skip_gain,
    segment,
    position,
):
    row_count = inputs.shape[0]
    heads_here = step_bias.shape[0]
    state_size = shared.shape[1] // 2
    values = jax.nn.silu(causal_filter(inputs, filter_weight, filter_bias, position)).reshape(
        row_count, heads_here, -1
    )
    factors = jax.nn.silu(causal_filter(shared, shared_filter, shared_filter_bias, position))
    writes = factors[:, :state_size]
    read_vectors = factors[:, state_size:]
    step_size = jax.nn.softplus(step_raw + step_bias)
    log_decay = -step_size * jnp.exp(decay_log)
    blocks = row_count // SPAN
    causal = jnp.arange(SPAN)[:, None] >= jnp.arange(SPAN)[None, :]

    def blocked(whole_array):
        return whole_array.reshape((blocks, SPAN) + whole_array.shape[1:])

    def span_step(state_carry, block_item):
        memory, last_segment = state_carry
        value_blk, write_blk, read_blk, size_blk, decay_blk, segment_blk = block_item
        cumulative = jnp.cumsum(decay_blk, axis=0).T
        inside = causal & (segment_blk[:, None] == segment_blk[None, :])
        spread = cumulative[:, :, None] - cumulative[:, None, :]
        decays = jnp.exp(jnp.where(inside[None], spread, -jnp.inf))
        scores = jnp.dot(read_blk, write_blk.T, precision=PRECISE)
        mixing = scores[None] * decays * size_blk.T[:, None, :]
        local_out = jnp.einsum("hts,shp->thp", mixing, value_blk, precision=PRECISE)
        carried = (segment_blk == last_segment).astype(value_blk.dtype)
        entering = jnp.exp(cumulative).T * carried[:, None]
        remote_out = (
            jnp.einsum("tn,hnp->thp", read_blk, memory, precision=PRECISE) * entering[:, :, None]
        )
        block_out = local_out + remote_out + skip_gain[None, :, None] * value_blk
        end_segment = segment_blk[-1]
        closing = (segment_blk == end_segment).astype(value_blk.dtype)
        weights = jnp.exp(cumulative[:, -1:] - cumulative) * size_blk.T * closing[None, :]
        added_state = jnp.einsum("sn,hs,shp->hnp", write_blk, weights, value_blk, precision=PRECISE)
        keeping = jnp.exp(cumulative[:, -1]) * (last_segment == end_segment).astype(value_blk.dtype)
        memory = memory * keeping[:, None, None] + added_state
        return ((memory, end_segment), block_out)

    initial = (jnp.zeros((heads_here, state_size, values.shape[2]), values.dtype), jnp.int32(-1))
    unused, outputs = lax.scan(
        jax.checkpoint(span_step),
        initial,
        (
            blocked(values),
            blocked(writes),
            blocked(read_vectors),
            blocked(step_size),
            blocked(log_decay),
            blocked(segment),
        ),
    )
    return outputs.reshape(row_count, -1)


def prenorm(hidden_in, norm_gain):
    scale = lax.rsqrt(jnp.mean(hidden_in * hidden_in, axis=1, keepdims=True) + EPSILON)
    return hidden_in * scale * norm_gain


def on_device(
    tokens,
    cotangent,
    destination,
    lengths,
    norm_gain,
    inner_weight,
    shared_weight,
    step_weight,
    filter_weight,
    filter_bias,
    shared_filter,
    shared_filter_bias,
    step_bias,
    decay_log,
    skip_gain,
    gate_gain,
    out_weight,
):
    row_count = tokens.shape[0]
    model_width = tokens.shape[1]
    group_rows = row_count // lax.axis_size("dp")
    my_index = lax.axis_index("dp")
    target_block = destination // row_count
    send_slot = (
        target_block * group_rows + (destination - target_block * row_count) - my_index * group_rows
    )
    send_order = (
        jnp.zeros((row_count,), jnp.int32).at[send_slot].set(jnp.arange(row_count, dtype=jnp.int32))
    )
    send_tokens = tokens[send_order]
    send_cot = cotangent[send_order]
    work_tokens, work_cot = (
        lax.all_to_all(send_tokens, "dp", split_axis=0, concat_axis=0, tiled=True),
        lax.all_to_all(send_cot, "dp", split_axis=0, concat_axis=0, tiled=True),
    )
    inner_full, shared_full, step_full, out_full = (
        lax.all_gather(inner_weight.astype(jnp.bfloat16), "dp", axis=0, tiled=True),
        lax.all_gather(shared_weight.astype(jnp.bfloat16), "dp", axis=0, tiled=True),
        lax.all_gather(step_weight.astype(jnp.bfloat16), "dp", axis=0, tiled=True),
        lax.all_gather(out_weight.astype(jnp.bfloat16), "dp", axis=0, tiled=True),
    )
    col_share = model_width // lax.axis_size("tensor")
    column = lax.axis_index("tensor") * col_share
    hidden_in = work_tokens.astype(jnp.float32)
    segment, position = segments_of(lengths[0], row_count)
    normed, pull_norm = jax.vjp(prenorm, hidden_in, norm_gain)
    normed_low = normed.astype(jnp.bfloat16)
    inner_flat = inner_full.reshape(inner_full.shape[0], -1)
    both = jnp.dot(normed_low, inner_flat, preferred_element_type=jnp.float32)
    half_width = both.shape[1] // 2
    gate_in = both[:, :half_width]
    inputs = both[:, half_width:]
    shared = jnp.dot(normed_low, shared_full, preferred_element_type=jnp.float32)
    step_raw = jnp.dot(normed_low, step_full, preferred_element_type=jnp.float32)

    def local_mixer(
        inputs,
        shared,
        step_raw,
        filter_weight,
        filter_bias,
        shared_filter,
        shared_filter_bias,
        step_bias,
        decay_log,
        skip_gain,
    ):
        return mixer(
            inputs,
            shared,
            step_raw,
            filter_weight,
            filter_bias,
            shared_filter,
            shared_filter_bias,
            step_bias,
            decay_log,
            skip_gain,
            segment,
            position,
        )

    mixed_in, pull_mixer = jax.vjp(
        local_mixer,
        inputs,
        shared,
        step_raw,
        filter_weight,
        filter_bias,
        shared_filter,
        shared_filter_bias,
        step_bias,
        decay_log,
        skip_gain,
    )
    gate_sig = jax.nn.sigmoid(gate_in)
    gate_act = gate_in * gate_sig
    gated = mixed_in * gate_act
    square_sum = lax.psum(jnp.sum(gated * gated, axis=1), "tensor")
    gate_scale = lax.rsqrt(square_sum / INNER + EPSILON)[:, None]
    gate_normed = (gated * gate_scale * gate_gain).astype(jnp.bfloat16)
    partial_out = jnp.einsum("ti,di->td", gate_normed, out_full, preferred_element_type=jnp.float32)
    branch = lax.psum(partial_out, "tensor")
    layer_work = (hidden_in + branch).astype(jnp.bfloat16)
    part_out = lax.dynamic_slice_in_dim(layer_work, column, col_share, 1)
    out_grad = jnp.einsum("td,ti->di", work_cot, gate_normed, preferred_element_type=jnp.float32)
    normed_grad = jnp.einsum("td,di->ti", work_cot, out_full, preferred_element_type=jnp.float32)
    gate_gain_grad = jnp.sum(normed_grad * gated * gate_scale, axis=0)
    scaled_grad = normed_grad * gate_gain
    cross_sum = lax.psum(jnp.sum(scaled_grad * gated, axis=1), "tensor")
    gated_grad = gate_scale * scaled_grad - gated * gate_scale**3 * (cross_sum / INNER)[:, None]
    mixed_grad = gated_grad * gate_act
    gate_in_grad = gated_grad * mixed_in * gate_sig * (1.0 + gate_in * (1.0 - gate_sig))
    (
        inputs_grad,
        shared_part,
        step_raw_grad,
        filter_weight_grad,
        filter_bias_grad,
        shared_filter_part,
        shared_bias_part,
        step_bias_grad,
        decay_log_grad,
        skip_gain_grad,
    ) = pull_mixer(mixed_grad)
    shared_grad, shared_filter_grad, shared_filter_bias_grad = lax.psum(
        (shared_part, shared_filter_part, shared_bias_part), "tensor"
    )
    both_low = jnp.concatenate([gate_in_grad, inputs_grad], axis=1).astype(jnp.bfloat16)
    shared_low = shared_grad.astype(jnp.bfloat16)
    step_low = step_raw_grad.astype(jnp.bfloat16)
    input_part = jnp.einsum("tk,dk->td", both_low, inner_flat, preferred_element_type=jnp.float32)
    input_part = input_part + jnp.einsum(
        "tk,dk->td", step_low, step_full, preferred_element_type=jnp.float32
    )
    normed_back = lax.psum(input_part, "tensor")
    normed_back = normed_back + jnp.einsum(
        "tk,dk->td", shared_low, shared_full, preferred_element_type=jnp.float32
    )
    input_norm_grad, norm_gain_grad = pull_norm(normed_back)
    input_work = (input_norm_grad + work_cot.astype(jnp.float32)).astype(jnp.bfloat16)
    part_grad = lax.dynamic_slice_in_dim(input_work, column, col_share, 1)
    inner_grad = jnp.einsum(
        "td,tk->dk", normed_low, both_low, preferred_element_type=jnp.float32
    ).reshape(inner_full.shape)
    shared_weight_grad = jnp.einsum(
        "td,tk->dk", normed_low, shared_low, preferred_element_type=jnp.float32
    )
    step_weight_grad = jnp.einsum(
        "td,tk->dk", normed_low, step_low, preferred_element_type=jnp.float32
    )
    inner_grad, shared_weight_grad, step_weight_grad, out_grad = (
        lax.psum_scatter(inner_grad, "dp", scatter_dimension=0, tiled=True),
        lax.psum_scatter(shared_weight_grad, "dp", scatter_dimension=0, tiled=True),
        lax.psum_scatter(step_weight_grad, "dp", scatter_dimension=0, tiled=True),
        lax.psum_scatter(out_grad, "dp", scatter_dimension=0, tiled=True),
    )
    (
        norm_gain_grad,
        filter_weight_grad,
        filter_bias_grad,
        shared_filter_grad,
        shared_filter_bias_grad,
        step_bias_grad,
        decay_log_grad,
        skip_gain_grad,
        gate_gain_grad,
    ) = lax.psum(
        (
            norm_gain_grad,
            filter_weight_grad,
            filter_bias_grad,
            shared_filter_grad,
            shared_filter_bias_grad,
            step_bias_grad,
            decay_log_grad,
            skip_gain_grad,
            gate_gain_grad,
        ),
        "dp",
    )
    part_out, part_grad = (
        lax.all_to_all(part_out, "dp", split_axis=0, concat_axis=0, tiled=True),
        lax.all_to_all(part_grad, "dp", split_axis=0, concat_axis=0, tiled=True),
    )
    back_out, back_grad = (
        lax.all_gather(part_out, "tensor", axis=1, tiled=True),
        lax.all_gather(part_grad, "tensor", axis=1, tiled=True),
    )
    layer_out = back_out[send_slot]
    input_grad = back_grad[send_slot]
    return (
        layer_out,
        input_grad,
        norm_gain_grad,
        inner_grad,
        shared_weight_grad,
        step_weight_grad,
        filter_weight_grad,
        filter_bias_grad,
        shared_filter_grad,
        shared_filter_bias_grad,
        step_bias_grad,
        decay_log_grad,
        skip_gain_grad,
        gate_gain_grad,
        out_grad,
    )


def solution(mesh):
    in_specs = (
        P("dp", None),
        P("dp", None),
        P("dp"),
        P("dp", None),
        P(),
        P("dp", None, "tensor"),
        P("dp", None),
        P("dp", "tensor"),
        P(None, "tensor"),
        P("tensor"),
        P(),
        P(),
        P("tensor"),
        P("tensor"),
        P("tensor"),
        P("tensor"),
        P("dp", "tensor"),
    )
    out_specs = (
        P("dp", None),
        P("dp", None),
        P(),
        P("dp", None, "tensor"),
        P("dp", None),
        P("dp", "tensor"),
        P(None, "tensor"),
        P("tensor"),
        P(),
        P(),
        P("tensor"),
        P("tensor"),
        P("tensor"),
        P("tensor"),
        P("dp", "tensor"),
    )
    return jax.shard_map(
        on_device, mesh=mesh, in_specs=in_specs, out_specs=out_specs, check_vma=False
    )
```

profile of v0, /device:TPU:1, one launch (start us, length us, event | category | flops | bytes accessed | tf_op | source)
XLA Modules:
  0.0 2526.7 jit_solution(8638867920375196014)
XLA Ops:
  42.6 88.7 %all-gather = bf16[8,192,12]{1,2,0:T(8,128)(2,1)S(1)} all-gather(bf16[1,192,12]{1,2,0:T(8,128)(2,1)S(1)} %convert_bitcast_fusion), channel_id=1, replica_groups=mesh['dp'=8,'tensor'=4] {'dp'}, dimensions={0}, use_global_device_ids=true | all-gather | bytes 41472 | tf_op jit(solution)/shard_map/all_gather | solution.py:148
  240.0 294.4 %while.47 = (s32[]{:T(128)}, f32[12,128,64]{1,2,0:T(8,128)S(1)}, s32[]{:T(128)}, f32[8,256,12,64]{1,0,3,2:T(8,128)}, f32[8,12,128,64]{2,3,1,0:T(8,128)}, /*index...) while((s32[]{:T(128)}, f32[12,128,64]{1,2,0:T(8,128)S(1)}, ...), condition=%wide.region_8.9_spmd.clone, body=%wide.region_5.8_spmd.clone.sunk | while | flops 1313649664 | bytes 11765497 | solution.py:89
  290.6 18.5 dynamic_update_slice.85
  327.4 18.5 dynamic_update_slice.85
  364.2 18.5 dynamic_update_slice.85
  401.0 18.5 dynamic_update_slice.85
  474.6 18.5 dynamic_update_slice.85
  511.4 18.5 dynamic_update_slice.85
  620.6 466.0 %while.48 = (s32[]{:T(128)}, f32[12]{0:T(128)}, f32[12,128,64]{1,2,0:T(8,128)S(1)}, f32[8,256,12,64]{1,0,3,2:T(8,128)}, f32[8,256,128]{2,1,0:T(8,128)}, /*index=...) while((s32[]{:T(128)}, f32[12]{0:T(128)}, ...), condition=%wide.region_27.28_spmd.clone, body=%wide.region_14.27_spmd.clone.sunk | while | flops 3037355008 | bytes 28656244 | solution.py:89
  711.3 18.5 dynamic_update_slice.89
  769.5 18.5 dynamic_update_slice.89
  944.0 18.5 dynamic_update_slice.89
  1002.1 18.5 dynamic_update_slice.89
  1060.3 18.5 dynamic_update_slice.89
  1214.8 149.8 %all-reduce.31 = (bf16[2048,256]{1,0:T(8,128)(2,1)}, f32[4,256]{1,0:T(4,128)S(1)}, f32[256]{0:T(256)S(1)}) all-reduce(f32[2048,256]{1,0:T(8,128)S(1)} %fusion.111, f32[4,256]{1,0:T(4,128)S(1)} %pad_add_fusion.1, f32[256]{0:T(256)S(1)} %get-tuple-element.895), channel_id=1, replica_groups=mesh['dp'=8,'tensor'=4] {'tensor'}, use_global_device_ids=true, to_apply=%region_29.30 | all-reduce | flops 525568 | bytes 3155968 | tf_op jit(solution)/shard_map/psum | solution.py:235
  1364.6 703.4 %all-reduce.30.cloned.1.call-done = (f32[2048,1536]{1,0:T(8,128)}, f32[2048,1536]{1,0:T(8,128)}) async-done(((f32[2048,1536]{1,0:T(8,128)}, f32[2048,1536]{1,0:T(8,128)}), (f32[2048,1536]{1,0:T(8,128)}, f32[2048,1536]{1,0:T(8,128)})) %all-reduce.30.cloned.1.call-update) | async-done | bytes 25165840 | tf_op jit(solution)/shard_map/psum | solution.py:212
  2081.2 26.4 %all_to_all.45 = bf16[8,256,384]{2,1,0:T(8,128)(2,1)} all-to-all(bf16[8,256,384]{2,1,0:T(8,128)(2,1)S(1)} %bitcast.451), channel_id=1, replica_groups=mesh['dp'=8,'tensor'=4] {'dp'}, dimensions={0} | all-to-all | bytes 3145728 | tf_op jit(solution)/shard_map/all_to_all | solution.py:293
  2107.7 24.2 all_to_all.46
  2151.3 38.5 %reduce-scatter.7.cloned.1.call-done = f32[192,2,768]{2,0,1:T(8,128)} async-done(((f32[1536,2,768]{2,0,1:T(8,128)}), f32[192,2,768]{2,0,1:T(8,128)}) %reduce-scatter.7.cloned.1.call-update) | async-done | bytes 1179664 | tf_op jit(solution)/shard_map/reduce_scatter | solution.py:262
  2192.9 22.7 all-reduce.24
  2215.6 91.3 %all-gather.12.cloned.1.call-done = bf16[2048,1536]{1,0:T(8,128)(2,1)} async-done(((bf16[2048,384]{1,0:T(8,128)(2,1)}), bf16[2048,1536]{1,0:T(8,128)(2,1)}) %all-gather.12.cloned.1.call-update) | async-done | bytes 6291472 | tf_op jit(solution)/shard_map/all_gather | solution.py:297
  2323.7 98.3 %all-gather.10.cloned.1.call-done = bf16[2048,1536]{1,0:T(8,128)(2,1)} async-done(((bf16[2048,384]{1,0:T(8,128)(2,1)}), bf16[2048,1536]{1,0:T(8,128)(2,1)}) %all-gather.10.cloned.1.call-update) | async-done | bytes 6291472 | tf_op jit(solution)/shard_map/all_gather | solution.py:296
  2438.8 23.2 reduce-scatter.9.cloned.1.call-done
  2462.0 57.9 %reduce-scatter.11.cloned.1.call-done = f32[192,768]{1,0:T(8,128)} async-done(((f32[1536,768]{1,0:T(8,128)}), f32[192,768]{1,0:T(8,128)}) %reduce-scatter.11.cloned.1.call-update) | async-done | bytes 589840 | tf_op jit(solution)/shard_map/reduce_scatter | solution.py:265
  (1043 shorter events, 959.7 us)
Async XLA Ops:
  7.2 182.0 %all-gather.6.cloned.1.call-start = ((), (), s32[]{:S(2)}) async-start(), calls=%async_computation.8 | async-start | bytes 5308416 | tf_op jit(solution)/shard_map/all_gather | solution.py:146
  36.5 95.0 %copy-start.73 = (f32[12]{0:T(128)S(1)}, f32[12]{0:T(128)}, u32[]{:S(2)}) copy-start(f32[12]{0:T(128)} %param.34) | copy-start | bytes 148
  36.5 121.8 %all-to-all-start = ((bf16[8,256,1536]{2,1,0:T(8,128)(2,1)}), bf16[8,256,1536]{2,1,0:T(8,128)(2,1)}, u32[]{:S(2)}, u32[]{:S(2)}) async-start(bf16[8,256,1536]{2,1,0:T(8,128)(2,1)} %bitcast.442), calls=%async_computation | async-start | bytes 12582912 | tf_op jit(solution)/shard_map/all_to_all | solution.py:142
  41.6 525.0 %all-gather.8.cloned.1.call-start = ((), (), s32[]{:S(2)}) async-start(), calls=%async_computation.9 | async-start | bytes 2654208 | tf_op jit(solution)/shard_map/all_gather | solution.py:149
  148.6 62.8 %copy-start.37 = (f32[768]{0:T(1024)}, f32[768]{0:T(1024)S(1)}, u32[]{:S(2)}) copy-start(f32[768]{0:T(1024)S(1)} %get-tuple-element.897) | copy-start | bytes 9220
  148.7 62.8 %copy-start.39 = (f32[768]{0:T(1024)}, f32[768]{0:T(1024)S(1)}, u32[]{:S(2)}) copy-start(f32[768]{0:T(1024)S(1)} %get-tuple-element.898) | copy-start | bytes 9220
  148.7 62.8 %copy-start.41 = (f32[768]{0:T(1024)}, f32[768]{0:T(1024)S(1)}, u32[]{:S(2)}) copy-start(f32[768]{0:T(1024)S(1)} %get-tuple-element.899) | copy-start | bytes 9220
  148.7 62.8 %copy-start.43 = (f32[768]{0:T(1024)}, f32[768]{0:T(1024)S(1)}, u32[]{:S(2)}) copy-start(f32[768]{0:T(1024)S(1)} %get-tuple-element.896) | copy-start | bytes 9220
  158.3 53.2 %copy-start.17 = (f32[2048]{0:T(1024)}, f32[2048]{0:T(1024)S(1)}, u32[]{:S(2)}) copy-start(f32[2048]{0:T(1024)S(1)} %get-tuple-element.1029) | copy-start | bytes 24580
  158.3 53.2 %copy-start.19 = (f32[2048]{0:T(1024)}, f32[2048]{0:T(1024)S(1)}, u32[]{:S(2)}) copy-start(f32[2048]{0:T(1024)S(1)} %get-tuple-element.1030) | copy-start | bytes 24580
  158.3 53.2 %copy-start.21 = (f32[2048]{0:T(1024)}, f32[2048]{0:T(1024)S(1)}, u32[]{:S(2)}) copy-start(f32[2048]{0:T(1024)S(1)} %get-tuple-element.1031) | copy-start | bytes 24580
  158.3 408.3 %all-to-all-start.2 = ((bf16[8,256,1536]{2,1,0:T(8,128)(2,1)}), bf16[8,256,1536]{2,1,0:T(8,128)(2,1)}, u32[]{:S(2)}, u32[]{:S(2)}) async-start(bf16[8,256,1536]{2,1,0:T(8,128)(2,1)} %bitcast.441), calls=%async_computation.2 | async-start | bytes 12582912 | tf_op jit(solution)/shard_map/all_to_all | solution.py:143
  163.1 1904.9 %all-reduce.30.cloned.1.call-start = ((), (), s32[]{:S(2)}) async-start(), calls=%async_computation.16 | async-start | bytes 50331648 | tf_op jit(solution)/shard_map/psum | solution.py:212
  1164.0 985.7 %reduce-scatter.13.cloned.1.call-start = ((), (), s32[]{:S(2)}) async-start(), calls=%async_computation.15 | async-start | bytes 884736
  1185.1 1004.7 %reduce-scatter.7.cloned.1.call-start = ((), (), s32[]{:S(2)}) async-start(), calls=%async_computation.12 | async-start | bytes 10616832 | tf_op jit(solution)/shard_map/reduce_scatter | solution.py:262
  1200.9 1106.0 %all-gather.12.cloned.1.call-start = ((), (), s32[]{:S(2)}) async-start(), calls=%async_computation.11 | async-start | bytes 7864320 | tf_op jit(solution)/shard_map/all_gather | solution.py:297
  1214.1 854.0 %copy-start.11 = (bf16[1536,256]{1,0:T(8,128)(2,1)S(1)}, bf16[1536,256]{1,0:T(8,128)(2,1)}, u32[]{:S(2)}) copy-start(bf16[1536,256]{1,0:T(8,128)(2,1)} %copy-done.10) | copy-start | bytes 2359300
  1214.1 854.0 %copy-start.29 = (f32[2048]{0:T(1024)S(1)}, f32[2048]{0:T(1024)}, u32[]{:S(2)}) copy-start(f32[2048]{0:T(1024)} %copy-done.28) | copy-start | bytes 24580
  1214.1 854.0 %copy-start.31 = (f32[1536]{0:T(1024)S(1)}, f32[1536]{0:T(1024)}, u32[]{:S(2)}) copy-start(f32[1536]{0:T(1024)} %param.25) | copy-start | bytes 18436
  2081.2 50.7 %copy-start.12 = (bf16[2048,256]{1,0:T(8,128)(2,1)S(1)}, bf16[2048,256]{1,0:T(8,128)(2,1)}, u32[]{:S(2)}) copy-start(bf16[2048,256]{1,0:T(8,128)(2,1)} %get-tuple-element.971) | copy-start | bytes 3145732
  2107.6 314.4 %all-gather.10.cloned.1.call-start = ((), (), s32[]{:S(2)}) async-start(), calls=%async_computation.10 | async-start | bytes 7864320 | tf_op jit(solution)/shard_map/all_gather | solution.py:296
  2131.9 330.2 %reduce-scatter.9.cloned.1.call-start = ((), (), s32[]{:S(2)}) async-start(), calls=%async_computation.13 | async-start | bytes 1769472 | tf_op jit(solution)/shard_map/reduce_scatter | solution.py:263
  2137.8 382.1 %reduce-scatter.11.cloned.1.call-start = ((), (), s32[]{:S(2)}) async-start(), calls=%async_computation.14 | async-start | bytes 5308416 | tf_op jit(solution)/shard_map/reduce_scatter | solution.py:265
  2149.5 157.3 %copy-start.34 = (s32[2048]{0:T(1024)S(1)}, s32[2048]{0:T(1024)}, u32[]{:S(2)}) copy-start(s32[2048]{0:T(1024)} %get-tuple-element.987) | copy-start | bytes 24580
  (113 other events, 1461.7 us)
Sparse Core Ops, SparseCore 0:
  10.4 46.4 all-gather.5
  58.8 70.6 all-gather.7
  1164.1 903.8 all-reduce.29
  2071.6 38.1 reduce-scatter.12
  2113.1 76.5 reduce-scatter.6
  2191.2 115.6 all-gather.11
  2308.4 113.5 all-gather.9
  2425.9 36.1 reduce-scatter.8
  2466.0 53.8 reduce-scatter.10
where the time goes:
time: 2550 us; the launch traced here: 2530 us
  waiting for transfers between devices  1010 us (40%)
  local copies, waits for them, and re-layouts  624 us (24%)
  blocking collectives  338 us (13%)
  matrix products  315 us (12%)
  other arithmetic  187 us (7%)
    psum x1, waiting for transfers between devices, on_device(): branch = lax.psum(partial_out, 'tensor')  703 us
    dynamic_update_slice x72, local copies, waits for them, and re-layouts, mixer(): lax.scan(jax.checkpoint(span_step), initial, (blocked(values), blocked(wr...  344 us
    psum x1, blocking collectives, on_device(): lax.psum((shared_part, shared_filter_part, shared_bias_part), 'tensor')  150 us
    dot_general x24, matrix products, span_step(): local_out = jnp.einsum('hts,shp->thp', mixing, value_blk, precision=PRECISE)  101 us
    all_gather x1, waiting for transfers between devices, on_device(): lax.all_gather(part_out, 'tensor', axis=1, tiled=True)  98.3 us
    all_gather x1, waiting for transfers between devices, on_device(): lax.all_gather(part_grad, 'tensor', axis=1, tiled=True)  91.3 us
    all_gather x1, blocking collectives, on_device(): lax.all_gather(step_weight.astype(jnp.bfloat16), 'dp', axis=0, tiled=True)  88.7 us
    reduce_scatter x1, waiting for transfers between devices, on_device(): lax.psum_scatter(out_grad, 'dp', scatter_dimension=0, tiled=True)  57.9 us
  transfers between devices with their start and end apart: 11, of which 6 were waited for; matrix products, arithmetic and copies ran while one was open for 21% of the time, Pallas kernels for 0%

commit v1 on v0

v1 whole, which is shorter than its diff:
```python
import jax
import jax.numpy as jnp
from jax import lax
from jax.experimental import pallas as pl
from jax.experimental.pallas import tpu as pltpu
from jax.sharding import PartitionSpec as P

SPAN = 128
HALO = 8
LANES = 128
F32 = jnp.float32
BF16 = jnp.bfloat16
EPSILON = 1e-05


def mm(a, b):
    return jnp.dot(a, b, preferred_element_type=F32)


def mm_t(a, b):
    return lax.dot_general(a, b, (((1,), (1,)), ((), ())), preferred_element_type=F32)


def halves(v):
    high = v.astype(BF16)
    return high, (v - high.astype(F32)).astype(BF16)


def widen(v, spread):
    high, rest = halves(v)
    return mm(high, spread) + mm(rest, spread)


def head_sum(v, spread):
    high, rest = halves(v)
    return mm_t(high, spread) + mm_t(rest, spread)


def start_of(place, lens_ref):
    end, start = jnp.int32(0), jnp.zeros_like(place)
    for i in range(lens_ref.shape[0]):
        start = jnp.where(place >= end, end, start)
        end = end + lens_ref[i]
    return start


def taps(current, before, reach):
    whole = jnp.concatenate([before, current], axis=0)
    rows = current.shape[0]
    return [whole[HALO - k : HALO - k + rows] for k in range(reach)]


def filtered(shifted, allowed, kernel, bias):
    result = bias + kernel[0:1] * shifted[0]
    for k in range(1, len(shifted)):
        result = result + kernel[k : k + 1] * shifted[k] * allowed[k]
    return result


def permitted(place, start, reach, width):
    flags = [None]
    for k in range(1, reach):
        flags.append(jnp.where(place - k >= start, 1.0, 0.0)[:, :1])
    return flags


def softplus(v):
    return jnp.maximum(v, 0.0) + jnp.log1p(jnp.exp(-jnp.abs(v)))


def chunk_setup(base, lens_ref, span):
    place = base + lax.broadcasted_iota(jnp.int32, (span, LANES), 0)
    start = start_of(place, lens_ref)
    last_start = start_of(jnp.full((1, LANES), base + span - 1, jnp.int32), lens_ref)
    return place, start, last_start


def stacked(pair, low_lanes):
    zero = jnp.zeros_like(pair)
    return jnp.concatenate([jnp.where(low_lanes, pair, zero), jnp.where(low_lanes, zero, pair)], axis=0)


def forward_kernel(
    lens_ref, proj_ref, shared_ref, fw_ref, fb_ref, sf_ref, sb_ref, head_ref, skip_ref, spread_ref,
    out_ref, kept_ref, memory, before, shared_before,
):
    step = pl.program_id(0)
    span = proj_ref.shape[0]
    width = out_ref.shape[1]
    reach = fw_ref.shape[0]
    pairs = width // LANES
    base = step * span

    @pl.when(step == 0)
    def _():
        memory[...] = jnp.zeros_like(memory)
        before[...] = jnp.zeros_like(before)
        shared_before[...] = jnp.zeros_like(shared_before)

    place, start, last_start = chunk_setup(base, lens_ref, span)
    allowed = permitted(place, start, reach, width)
    inputs = proj_ref[:, :width]
    shared = shared_ref[...]
    conv = filtered(taps(inputs, before[...], reach), allowed, fw_ref, fb_ref[...])
    values = conv * jax.nn.sigmoid(conv)
    conv = filtered(taps(shared, shared_before[...], reach), allowed, sf_ref, sb_ref[...])
    factors = conv * jax.nn.sigmoid(conv)
    before[...] = inputs[span - HALO :]
    shared_before[...] = shared[span - HALO :]
    writes = factors[:, :LANES].astype(BF16)
    reads = factors[:, LANES:].astype(BF16)
    size = softplus(proj_ref[:, width:] + head_ref[0:1])
    decay = -size * head_ref[1:2]
    row = lax.broadcasted_iota(jnp.int32, (span, span), 0)
    col = lax.broadcasted_iota(jnp.int32, (span, span), 1)
    lower = jnp.where(row >= col, 1.0, 0.0)
    total = jnp.dot(lower, decay, precision=lax.Precision.HIGHEST, preferred_element_type=F32)
    total_t = total.T
    inside = (col <= row) & (col + base >= start)
    scores = jnp.where(inside, mm_t(reads, writes), 0.0)
    spread = spread_ref[...]
    scaled = values * widen(size, spread)
    scaled_low = scaled.astype(BF16)
    entering = jnp.exp(total) * jnp.where(start < base, 1.0, 0.0)
    state = memory[...]
    state_low = state.astype(BF16)
    kept_ref[0] = state_low
    remote = mm(reads, state_low) * widen(entering, spread) + skip_ref[...] * values
    low_lanes = lax.broadcasted_iota(jnp.int32, (span, LANES), 1) < LANES // 2
    for pair in range(pairs):
        lanes = slice(pair * LANES, (pair + 1) * LANES)
        mixing = []
        for head in (2 * pair, 2 * pair + 1):
            fade = jnp.exp(jnp.minimum(total[:, head : head + 1] - total_t[head : head + 1, :], 0.0))
            mixing.append((scores * fade).astype(BF16))
        local = mm(jnp.concatenate(mixing, axis=1), stacked(scaled_low[:, lanes], low_lanes))
        out_ref[:, lanes] = (local + remote[:, lanes]).astype(out_ref.dtype)
    end = total[span - 1 : span]
    closing = jnp.exp(end - total) * jnp.where(place >= last_start, 1.0, 0.0)
    added = mm(writes.T, (scaled * widen(closing, spread)).astype(BF16))
    keeping = jnp.exp(end) * jnp.where(last_start < base, 1.0, 0.0)
    memory[...] = state * widen(jnp.broadcast_to(keeping, (8, LANES)), spread)[0:1] + added


def backward_kernel(
    lens_ref, proj_ref, proj_before_ref, shared_ref, shared_before_ref, grad_ref, out_ref, kept_ref,
    fw_ref, fb_ref, sf_ref, sb_ref, head_ref, skip_ref, spread_ref,
    inputs_grad_ref, shared_grad_ref, raw_grad_ref, fsum_ref, ssum_ref, hsum_ref,
    memory_grad, after, shared_after,
):
    step = pl.program_id(0)
    steps = pl.num_programs(0)
    span = proj_ref.shape[0]
    width = out_ref.shape[1]
    reach = fw_ref.shape[0]
    pairs = width // LANES
    chunk = steps - 1 - step
    base = chunk * span

    @pl.when(step == 0)
    def _():
        memory_grad[...] = jnp.zeros_like(memory_grad)
        after[...] = jnp.zeros_like(after)
        shared_after[...] = jnp.zeros_like(shared_after)
        fsum_ref[...] = jnp.zeros_like(fsum_ref)
        ssum_ref[...] = jnp.zeros_like(ssum_ref)
        hsum_ref[...] = jnp.zeros_like(hsum_ref)

    place, start, last_start = chunk_setup(base, lens_ref, span)
    allowed = permitted(place, start, reach, width)
    first = jnp.where(chunk > 0, 1.0, 0.0)
    inputs = proj_ref[:, :width]
    shifted = taps(inputs, proj_before_ref[:, :width] * first, reach)
    conv = filtered(shifted, allowed, fw_ref, fb_ref[...])
    gate = jax.nn.sigmoid(conv)
    values = conv * gate
    slope = gate * (1.0 + conv * (1.0 - gate))
    shared_shifted = taps(shared_ref[...], shared_before_ref[...] * first, reach)
    conv = filtered(shared_shifted, allowed, sf_ref, sb_ref[...])
    gate = jax.nn.sigmoid(conv)
    factors = conv * gate
    shared_slope = gate * (1.0 + conv * (1.0 - gate))
    writes = factors[:, :LANES].astype(BF16)
    reads = factors[:, LANES:].astype(BF16)
    raw = proj_ref[:, width:] + head_ref[0:1]
    size = softplus(raw)
    decay = -size * head_ref[1:2]
    row = lax.broadcasted_iota(jnp.int32, (span, span), 0)
    col = lax.broadcasted_iota(jnp.int32, (span, span), 1)
    lower = jnp.where(row >= col, 1.0, 0.0)
    upper = jnp.where(row <= col, 1.0, 0.0)
    total = jnp.dot(lower, decay, precision=lax.Precision.HIGHEST, preferred_element_type=F32)
    total_t = total.T
    start_t = start_of(base + col[0:1], lens_ref)
    inside_t = (row <= col) & (row + base >= start_t)
    scores_t = jnp.where(inside_t, mm_t(writes, reads), 0.0)
    spread = spread_ref[...]
    size_wide = widen(size, spread)
    scaled = values * size_wide
    scaled_low = scaled.astype(BF16)
    grad = grad_ref[...].astype(F32)
    grad_low = grad.astype(BF16)
    state_low = kept_ref[0]
    later = memory_grad[...]
    later_low = later.astype(BF16)
    entering = jnp.exp(total) * jnp.where(start < base, 1.0, 0.0)
    entered = (grad * widen(entering, spread)).astype(BF16)
    end = total[span - 1 : span]
    closing = jnp.exp(end - total) * jnp.where(place >= last_start, 1.0, 0.0)
    closing_wide = widen(closing, spread)
    keeping = jnp.exp(end) * jnp.where(last_start < base, 1.0, 0.0)
    keeping_wide = widen(jnp.broadcast_to(keeping, (8, LANES)), spread)[0:1]
    closed = mm(writes, later_low) * closing_wide
    low_lanes = lax.broadcasted_iota(jnp.int32, (span, LANES), 1) < LANES // 2
    scores_grad_t = jnp.zeros((span, span), F32)
    local = []
    for pair in range(pairs):
        lanes = slice(pair * LANES, (pair + 1) * LANES)
        halved = stacked(grad_low[:, lanes], low_lanes)
        mixing_grad = mm_t(scaled_low[:, lanes], halved)
        mixing = []
        for which, head in enumerate((2 * pair, 2 * pair + 1)):
            fade = jnp.exp(jnp.minimum(total_t[head : head + 1, :] - total[:, head : head + 1], 0.0))
            mixing.append((scores_t * fade).astype(BF16))
            scores_grad_t = scores_grad_t + mixing_grad[:, which * span : (which + 1) * span] * fade
        local.append(mm(jnp.concatenate(mixing, axis=1), halved))
    scaled_grad = jnp.concatenate(local, axis=1) + closed
    scores_grad_t = jnp.where(inside_t, scores_grad_t, 0.0).astype(BF16)
    kept_closing = (scaled * closing_wide).astype(BF16)
    reads_grad = mm(scores_grad_t.T, writes) + mm_t(entered, state_low)
    writes_grad = mm(scores_grad_t, reads) + mm_t(kept_closing, later_low)
    memory_grad[...] = later * keeping_wide + mm(reads.T, entered)
    skip = skip_ref[...]
    size_grad = head_sum(values * scaled_grad, spread)
    paid = head_sum(
        grad_low.astype(F32) * (out_ref[...] - skip * values) - scaled_low.astype(F32) * scaled_grad, spread
    )
    tail = jnp.sum(scaled_low.astype(F32) * closed, axis=0, keepdims=True) + keeping_wide * jnp.sum(
        later * state_low.astype(F32), axis=0, keepdims=True
    )
    tail = head_sum(jnp.broadcast_to(tail, (8, width)), spread)[0:1]
    total_grad = paid + jnp.where(place == base + span - 1, tail, 0.0)
    decay_grad = jnp.dot(upper, total_grad, precision=lax.Precision.HIGHEST, preferred_element_type=F32)
    raw_grad = (size_grad - decay_grad * head_ref[1:2]) * jax.nn.sigmoid(raw)
    raw_grad_ref[...] = raw_grad.astype(raw_grad_ref.dtype)
    hsum_ref[0:1] += jnp.sum(raw_grad, axis=0, keepdims=True)
    hsum_ref[1:2] += jnp.sum(decay_grad * decay, axis=0, keepdims=True)
    conv_grad = (size_wide * scaled_grad + skip * grad) * slope
    shared_conv_grad = jnp.concatenate([writes_grad, reads_grad], axis=1) * shared_slope
    fsum_ref[reach : reach + 1] += jnp.sum(conv_grad, axis=0, keepdims=True)
    fsum_ref[reach + 1 : reach + 2] += jnp.sum(grad * values, axis=0, keepdims=True)
    ssum_ref[reach : reach + 1] += jnp.sum(shared_conv_grad, axis=0, keepdims=True)
    late = base + lax.broadcasted_iota(jnp.int32, (span + HALO, LANES), 0)
    late_allowed = permitted(late, start_of(late, lens_ref), reach, width)
    whole = jnp.concatenate([conv_grad, after[...]], axis=0)
    shared_whole = jnp.concatenate([shared_conv_grad, shared_after[...]], axis=0)
    result = fw_ref[0:1] * conv_grad
    shared_result = sf_ref[0:1] * shared_conv_grad
    fsum_ref[0:1] += jnp.sum(conv_grad * shifted[0], axis=0, keepdims=True)
    ssum_ref[0:1] += jnp.sum(shared_conv_grad * shared_shifted[0], axis=0, keepdims=True)
    for k in range(1, reach):
        masked = whole * late_allowed[k]
        fsum_ref[k : k + 1] += jnp.sum(masked[:span] * shifted[k], axis=0, keepdims=True)
        result = result + fw_ref[k : k + 1] * masked[k : k + span]
        masked = shared_whole * late_allowed[k]
        ssum_ref[k : k + 1] += jnp.sum(masked[:span] * shared_shifted[k], axis=0, keepdims=True)
        shared_result = shared_result + sf_ref[k : k + 1] * masked[k : k + span]
    after[...] = conv_grad[:HALO]
    shared_after[...] = shared_conv_grad[:HALO]
    inputs_grad_ref[...] = result.astype(inputs_grad_ref.dtype)
    shared_grad_ref[...] = shared_result.astype(shared_grad_ref.dtype)


def head_rows(step_bias, decay_log, skip_gain, width):
    heads = step_bias.shape[0]
    table = jnp.zeros((8, LANES), F32)
    table = table.at[0, :heads].set(step_bias).at[1, :heads].set(jnp.exp(decay_log))
    skip = jnp.repeat(skip_gain, width // heads)[None, :]
    spread = (jnp.arange(LANES)[:, None] == (jnp.arange(width) // (width // heads))[None, :]).astype(BF16)
    return table, skip, spread


def fixed(shape):
    return pl.BlockSpec(shape, lambda *_: (0,) * len(shape))


def mixer_forward(lens, proj, shared, fw, fb, sf, sb, table, skip, spread):
    rows = proj.shape[0]
    width = fw.shape[1]
    steps = rows // SPAN
    block = lambda cols: pl.BlockSpec((SPAN, cols), lambda i, *_: (i, 0))
    return pl.pallas_call(
        forward_kernel,
        grid_spec=pltpu.PrefetchScalarGridSpec(
            num_scalar_prefetch=1,
            grid=(steps,),
            in_specs=[
                block(proj.shape[1]), block(shared.shape[1]), fixed(fw.shape), fixed(fb.shape), fixed(sf.shape),
                fixed(sb.shape), fixed(table.shape), fixed(skip.shape), fixed(spread.shape),
            ],
            out_specs=[block(width), pl.BlockSpec((1, LANES, width), lambda i, *_: (i, 0, 0))],
            scratch_shapes=[
                pltpu.VMEM((LANES, width), F32),
                pltpu.VMEM((HALO, width), F32),
                pltpu.VMEM((HALO, shared.shape[1]), F32),
            ],
        ),
        out_shape=[
            jax.ShapeDtypeStruct((rows, width), F32),
            jax.ShapeDtypeStruct((steps, LANES, width), BF16),
        ],
        cost_estimate=pl.CostEstimate(flops=20 * 10**9, bytes_accessed=30 * 10**6, transcendentals=0),
        name="mixer_forward",
    )(lens, proj, shared, fw, fb, sf, sb, table, skip, spread)


def mixer_backward(lens, proj, shared, grad, out, kept, fw, fb, sf, sb, table, skip, spread):
    rows = proj.shape[0]
    width = fw.shape[1]
    steps = rows // SPAN
    lead = SPAN // HALO
    block = lambda cols: pl.BlockSpec((SPAN, cols), lambda i, *_: (steps - 1 - i, 0))
    ahead = lambda cols: pl.BlockSpec((HALO, cols), lambda i, *_: (jnp.maximum((steps - 1 - i) * lead - 1, 0), 0))
    return pl.pallas_call(
        backward_kernel,
        grid_spec=pltpu.PrefetchScalarGridSpec(
            num_scalar_prefetch=1,
            grid=(steps,),
            in_specs=[
                block(proj.shape[1]), ahead(proj.shape[1]), block(shared.shape[1]), ahead(shared.shape[1]),
                block(width), block(width), pl.BlockSpec((1, LANES, width), lambda i, *_: (steps - 1 - i, 0, 0)),
                fixed(fw.shape), fixed(fb.shape), fixed(sf.shape),
                fixed(sb.shape), fixed(table.shape), fixed(skip.shape), fixed(spread.shape),
            ],
            out_specs=[
                block(width), block(shared.shape[1]), block(LANES),
                fixed((8, width)), fixed((8, shared.shape[1])), fixed((8, LANES)),
            ],
            scratch_shapes=[
                pltpu.VMEM((LANES, width), F32),
                pltpu.VMEM((HALO, width), F32),
                pltpu.VMEM((HALO, shared.shape[1]), F32),
            ],
        ),
        out_shape=[
            jax.ShapeDtypeStruct((rows, width), BF16),
            jax.ShapeDtypeStruct((rows, shared.shape[1]), F32),
            jax.ShapeDtypeStruct((rows, LANES), BF16),
            jax.ShapeDtypeStruct((8, width), F32),
            jax.ShapeDtypeStruct((8, shared.shape[1]), F32),
            jax.ShapeDtypeStruct((8, LANES), F32),
        ],
        cost_estimate=pl.CostEstimate(flops=40 * 10**9, bytes_accessed=60 * 10**6, transcendentals=0),
        name="mixer_backward",
    )(lens, proj, proj, shared, shared, grad, out, kept, fw, fb, sf, sb, table, skip, spread)


def swap(v, axis, mask=1):
    count = lax.axis_size(axis)
    return lax.ppermute(v, axis, [(i, i ^ mask) for i in range(count)])


def diagonal(v):
    return lax.ppermute(v, ("side", "core"), [(i, i ^ 3) for i in range(4)])


def pick(stack, index, axis=0):
    return lax.dynamic_index_in_dim(stack, index, axis, keepdims=False)


def placed(pieces, spots, shape):
    lead = len(shape)
    tail = pieces[0].shape
    whole = jnp.zeros(shape + tail, pieces[0].dtype)
    for piece, spot in zip(pieces, spots):
        whole = lax.dynamic_update_slice(whole, piece.reshape((1,) * lead + tail), tuple(spot) + (0,) * len(tail))
    return whole


def row_doubling(v):
    pieces = [v]
    count = lax.axis_size("row")
    while len(pieces) < count:
        reach = len(pieces)
        pieces = pieces + [swap(p, "row", reach) for p in pieces]
    return pieces


def row_halving(pieces):
    while len(pieces) > 1:
        reach = len(pieces) // 2
        kept = pieces[:reach]
        pieces = [a + swap(b.astype(BF16), "row", reach).astype(F32) for a, b in zip(kept, pieces[reach:])]
    return pieces[0]


def line_gather(v):
    count = lax.axis_size("tensor")
    left, right = [v], [v]
    for j in range(1, count):
        left.append(lax.ppermute(left[-1], "tensor", [(i, i + 1) for i in range(j - 1, count - 1)]))
        right.append(lax.ppermute(right[-1], "tensor", [(i + 1, i) for i in range(0, count - j)]))
    return jnp.stack(left[:0:-1] + right)


def line_scatter(stack):
    count = lax.axis_size("tensor")
    plane = lax.axis_index("tensor")
    from_left = from_right = None
    for t in range(1, count):
        send_right = pick(stack, jnp.clip(count - t + plane, 0, count - 1))
        send_left = pick(stack, jnp.clip(plane - count + t, 0, count - 1))
        if t > 1:
            send_right = (send_right.astype(F32) + from_left.astype(F32)).astype(BF16)
            send_left = (send_left.astype(F32) + from_right.astype(F32)).astype(BF16)
        from_left = lax.ppermute(send_right, "tensor", [(i, i + 1) for i in range(t)])
        from_right = lax.ppermute(send_left, "tensor", [(count - 1 - i, count - 2 - i) for i in range(t)])
    return pick(stack, plane).astype(F32) + from_left.astype(F32) + from_right.astype(F32)


def whole_weight(piece, row, side, core):
    planes = line_gather(piece)
    plane = lax.axis_index("tensor")
    count = lax.axis_size("tensor")

    def shard(dx, dk):
        return pick(planes, (side ^ dx) * 2 + (core ^ dk) - plane + count - 1)

    pieces = [
        shard(0, 0),
        swap(shard(0, 1), "core"),
        swap(shard(1, 0), "side"),
        diagonal(shard(1, 1)),
    ]
    spots = [(side, core), (side, 1 - core), (1 - side, core), (1 - side, 1 - core)]
    return rows_joined(placed(pieces, spots, (2, 2)), row)


def rows_joined(block, row):
    blocks = row_doubling(block)
    count = len(blocks)
    whole = placed(blocks, [(row ^ d,) for d in range(count)], (count,))
    return whole.reshape(-1, whole.shape[-1])


def scattered_weight(grad, row, side, core):
    count = lax.axis_size("row")
    blocks = grad.reshape(count, 2, 2, -1, grad.shape[-1])
    mine = row_halving([pick(blocks, row ^ d) for d in range(count)]).astype(BF16)

    def part(dx, dk):
        return pick(pick(mine, side ^ dx), core ^ dk)

    pieces = [
        part(0, 0),
        swap(part(0, 1), "core"),
        swap(part(1, 0), "side"),
        diagonal(part(1, 1)),
    ]
    spots = [
        (side * 2 + core,),
        (side * 2 + 1 - core,),
        ((1 - side) * 2 + core,),
        ((1 - side) * 2 + 1 - core,),
    ]
    return line_scatter(placed(pieces, spots, (4,)))


def everywhere(v):
    for mask in (1, 2):
        v = v + swap(v, "tensor", mask)
    return v


def on_device(
    tokens, cotangent, destination, lengths, norm_gain, inner_weight, shared_weight, step_weight, filter_weight,
    filter_bias, shared_filter, shared_filter_bias, step_bias, decay_log, skip_gain, gate_gain, out_weight,
):
    row_count, model_width = tokens.shape
    width = filter_weight.shape[1]
    heads = step_bias.shape[0]
    rows_n, planes = lax.axis_size("row"), lax.axis_size("tensor")
    row, side, core, plane = (lax.axis_index(a) for a in ("row", "side", "core", "tensor"))
    group_rows = row_count // (rows_n * 4)
    source = (row * 2 + side) * 2 + core

    step_low = jnp.pad(step_weight.astype(BF16), ((0, 0), (0, LANES - heads)))
    in_piece = jnp.concatenate([inner_weight[:, 1].astype(BF16), step_low], axis=1)
    in_full = whole_weight(in_piece, row, side, core)
    shared_piece = shared_weight.astype(BF16)
    shared_pair = jnp.stack([shared_piece, swap(shared_piece, "core")])
    shared_side = swap(shared_pair, "side")
    shared_full = rows_joined(
        placed(
            [shared_pair[0], shared_pair[1], shared_side[0], shared_side[1]],
            [(side, core), (side, 1 - core), (1 - side, core), (1 - side, 1 - core)],
            (2, 2),
        ),
        row,
    )
    gate_full = whole_weight(inner_weight[:, 0].astype(BF16), row, side, core)
    out_full = whole_weight(out_weight.astype(BF16), row, side, core)

    params = jnp.concatenate(
        [
            filter_weight,
            filter_bias[None],
            gate_gain[None],
            jnp.pad(jnp.concatenate([step_bias, decay_log, skip_gain]), (0, width - 3 * heads))[None],
            jnp.zeros((1, width), F32),
        ],
        axis=0,
    )
    shards = line_gather(params)
    params = pick(shards, side * 2 + core - plane + planes - 1)
    fw, fb, gain = params[:4], params[4:5], params[5:6]
    bias_here, decay_here, skip_here = (params[6, i * heads : (i + 1) * heads] for i in range(3))
    sf, sb = shared_filter, shared_filter_bias[None]
    table, skip, spread = head_rows(bias_here, decay_here, skip_here, width)

    pair = jnp.stack([lengths[0], swap(lengths, "core")[0]])
    four = jnp.stack([pair, swap(pair, "side")])
    lens = pick(pick(four, (plane // 2) ^ side), (plane % 2) ^ core)

    block_of = lambda r: r * planes + plane
    wanted = jnp.concatenate(
        [
            block_of(row ^ d) * row_count + source * group_rows + jnp.arange(group_rows, dtype=jnp.int32)
            for d in range(rows_n)
        ]
    )
    chosen = (wanted[:, None] == destination[None, :]).astype(BF16)
    sent_tokens = jnp.dot(chosen, tokens, preferred_element_type=F32).astype(BF16).reshape(rows_n, group_rows, -1)
    sent_cot = jnp.dot(chosen, cotangent, preferred_element_type=F32).astype(BF16).reshape(rows_n, group_rows, -1)

    def exchanged(sent):
        pieces = [sent[0]] + [swap(sent[d], "row", d) for d in range(1, rows_n)]
        return placed(pieces, [(row ^ d,) for d in range(rows_n)], (rows_n,))

    def gathered(own):
        beside = swap(own, "side")
        pairs = [own, beside]
        others = [swap(p, "core") for p in pairs]
        whole = jnp.zeros((rows_n, 2, 2) + own.shape[1:], own.dtype)
        for dx in range(2):
            for dk, p in ((0, pairs[dx]), (1, others[dx])):
                whole = lax.dynamic_update_slice(whole, p[:, None, None], (0, side ^ dx, core ^ dk, 0, 0))
        return whole.reshape(-1, own.shape[-1])

    own_tokens = exchanged(sent_tokens)
    hidden = own_tokens.astype(F32)
    scale = lax.rsqrt(jnp.mean(hidden * hidden, axis=-1, keepdims=True) + EPSILON)
    own_normed = (hidden * scale * norm_gain).astype(BF16)
    normed = gathered(own_normed)
    own_cot = exchanged(sent_cot)
    cot = gathered(own_cot)

    proj = jnp.dot(normed, in_full, preferred_element_type=F32)
    shared = jnp.dot(normed, shared_full, preferred_element_type=F32)
    mixed, kept = mixer_forward(lens, proj, shared, fw, fb, sf, sb, table, skip, spread)
    gate_in = jnp.dot(normed, gate_full, preferred_element_type=F32)
    gate_sig = jax.nn.sigmoid(gate_in)
    gate_act = gate_in * gate_sig
    gated = mixed * gate_act
    square_sum = jnp.sum(gated * gated, axis=1)
    square_sum = square_sum + swap(square_sum, "core")
    square_sum = square_sum + swap(square_sum, "side")
    gate_scale = lax.rsqrt(square_sum / (4 * width) + EPSILON)[:, None]
    gate_normed = (gated * gate_scale * gain).astype(BF16)

    def part_rows(v, dx, dk):
        v = v.reshape(rows_n, 2, 2, group_rows, v.shape[-1])
        return pick(pick(v, side ^ dx, 1), core ^ dk, 1).reshape(rows_n * group_rows, v.shape[-1])

    def summed_rows(part):
        far = swap(part(1, 1).astype(BF16), "core")
        beside = swap((part(1, 0) + far.astype(F32)).astype(BF16), "side")
        near = swap(part(0, 1).astype(BF16), "core")
        return part(0, 0) + near.astype(F32) + beside.astype(F32)

    branch = summed_rows(lambda dx, dk: lax.dot_general(
        part_rows(gate_normed, dx, dk), out_full, (((1,), (1,)), ((), ())), preferred_element_type=F32))
    flat = lambda v: v.reshape(rows_n * group_rows, -1)

    lines = target_slots(destination, row_count, source, group_rows, planes, rows_n, plane)

    def returned(rows):
        rows = rows.reshape(rows_n, group_rows, -1)
        back = exchanged(jnp.stack([pick(rows, row ^ d) for d in range(rows_n)]))
        return line_gather(flat(back)).reshape(-1, rows.shape[-1])[lines]

    layer_out = returned((flat(hidden) + branch).astype(BF16))

    normed_grad = jnp.dot(cot, out_full, preferred_element_type=F32)
    out_grad = lax.dot_general(cot, gate_normed, (((0,), (0,)), ((), ())), preferred_element_type=F32)
    out_grad = scattered_weight(out_grad, row, side, core)
    gate_gain_grad = jnp.sum(normed_grad * gated * gate_scale, axis=0)
    scaled_grad = normed_grad * gain
    cross_sum = jnp.sum(scaled_grad * gated, axis=1)
    cross_sum = cross_sum + swap(cross_sum, "core")
    cross_sum = cross_sum + swap(cross_sum, "side")
    gated_grad = gate_scale * scaled_grad - gated * gate_scale**3 * (cross_sum / (4 * width))[:, None]
    mixed_grad = gated_grad * gate_act
    gate_in_grad = (gated_grad * mixed * gate_sig * (1.0 + gate_in * (1.0 - gate_sig))).astype(BF16)
    gate_grad = lax.dot_general(normed, gate_in_grad, (((0,), (0,)), ((), ())), preferred_element_type=F32)
    gate_grad = scattered_weight(gate_grad, row, side, core)
    inputs_grad, shared_part, raw_grad, fsum, ssum, hsum = mixer_backward(
        lens, proj, shared, mixed_grad, mixed, kept, fw, fb, sf, sb, table, skip, spread
    )
    proj_grad = jnp.concatenate([inputs_grad, raw_grad], axis=1)
    shared_grad = summed_rows(lambda dx, dk: part_rows(shared_part, dx, dk)).astype(BF16)
    normed_back = summed_rows(lambda dx, dk: (
        lax.dot_general(part_rows(gate_in_grad, dx, dk), gate_full, (((1,), (1,)), ((), ())), preferred_element_type=F32)
        + lax.dot_general(part_rows(proj_grad, dx, dk), in_full, (((1,), (1,)), ((), ())), preferred_element_type=F32)
    ))
    normed_back = normed_back + lax.dot_general(
        shared_grad, shared_full, (((1,), (1,)), ((), ())), preferred_element_type=F32
    )
    x, s = flat(hidden), flat(scale)
    norm_gain_grad = jnp.sum(normed_back * x * s, axis=0)
    gained = normed_back * norm_gain
    along = jnp.mean(gained * x, axis=1, keepdims=True)
    input_work = flat(own_cot).astype(F32) + s * gained - x * (s**3 * along)
    input_grad = returned(input_work.astype(BF16))

    proj_weight_grad = lax.dot_general(normed, proj_grad, (((0,), (0,)), ((), ())), preferred_element_type=F32)
    proj_weight_grad = scattered_weight(proj_weight_grad, row, side, core)
    inner_grad = jnp.stack([gate_grad, proj_weight_grad[:, :width]], axis=1)
    step_weight_grad = proj_weight_grad[:, width : width + heads]
    shared_weight_grad = lax.dot_general(
        flat(own_normed), shared_grad, (((0,), (0,)), ((), ())), preferred_element_type=F32
    ).reshape(rows_n, 2, 2, -1, shared.shape[1])
    shared_weight_grad = row_halving([pick(shared_weight_grad, row ^ d) for d in range(rows_n)])
    mine = pick(shared_weight_grad, core, 1) + swap(pick(shared_weight_grad, 1 - core, 1), "core")
    mine = pick(mine, side) + swap(pick(mine, 1 - side), "side")
    shared_weight_grad = everywhere(mine)

    line = lambda v: jnp.pad(v, (0, -v.shape[0] % width)).reshape(-1, width)
    skip_grad = fsum[5].reshape(heads, -1).sum(axis=1)
    small = jnp.concatenate(
        [
            fsum[:5],
            gate_gain_grad[None],
            jnp.pad(jnp.concatenate([hsum[0, :heads], hsum[1, :heads], skip_grad]), (0, width - 3 * heads))[None],
            jnp.zeros((1, width), F32),
            line(norm_gain_grad),
            line(ssum[:5].reshape(-1)),
        ],
        axis=0,
    )
    reach = 1
    while reach < rows_n:
        small = small + swap(small, "row", reach)
        reach = reach * 2
    small = everywhere(small)
    small = jnp.stack([small, swap(small, "core")])
    small = jnp.stack([small, swap(small, "side")])
    common = (small[0, 0, 8:] + small[0, 1, 8:]) + (small[1, 0, 8:] + small[1, 1, 8:])
    mine = pick(pick(small[:, :, :8], (plane // 2) ^ side), (plane % 2) ^ core)
    lines_n = line(norm_gain_grad).shape[0]
    norm_gain_grad = common[:lines_n].reshape(-1)[:model_width]
    shared_sums = common[lines_n:].reshape(-1)[: 5 * shared.shape[1]].reshape(5, -1)
    return (
        layer_out, input_grad, norm_gain_grad, inner_grad, shared_weight_grad, step_weight_grad,
        mine[:4], mine[4], shared_sums[:4], shared_sums[4],
        mine[6, :heads], mine[6, heads : 2 * heads], mine[6, 2 * heads : 3 * heads], mine[5], out_grad,
    )


def target_slots(destination, row_count, source, group_rows, planes, rows_n, plane):
    block = destination // row_count
    row_of, plane_of = block // planes, block % planes
    place = destination - block * row_count - source * group_rows
    return ((plane_of - plane + planes - 1) * rows_n + row_of) * group_rows + place


def solution(mesh):
    count, planes = mesh.devices.shape
    names = ("row", "side", "core", "tensor")
    inner = jax.sharding.Mesh(mesh.devices.reshape(count // 4, 2, 2, planes), names)
    dp = ("row", "side", "core")
    in_specs = (
        P(dp, None), P(dp, None), P(dp), P(dp, None), P(), P(dp, None, "tensor"), P(dp, None), P(dp, "tensor"),
        P(None, "tensor"), P("tensor"), P(), P(), P("tensor"), P("tensor"), P("tensor"), P("tensor"), P(dp, "tensor"),
    )
    out_specs = (
        P(dp, None), P(dp, None), P(), P(dp, None, "tensor"), P(dp, None), P(dp, "tensor"),
        P(None, "tensor"), P("tensor"), P(), P(), P("tensor"), P("tensor"), P("tensor"), P("tensor"), P(dp, "tensor"),
    )
    return jax.shard_map(on_device, mesh=inner, in_specs=in_specs, out_specs=out_specs, check_vma=False)
```

time: 2550 us -> 1070 us (0.42)
  waiting for transfers between devices: 1010 us -> 442 us
  local copies, waits for them, and re-layouts: 624 us -> 156 us
  blocking collectives: 338 us -> 0 us
  starting transfers between devices: 10.4 us -> 239 us
  matrix products: 315 us -> 110 us
  other arithmetic: 187 us -> 31.1 us
  Pallas kernels: 0 us -> 76.6 us
    psum x1 -> x0, waiting for transfers between devices: 703 us -> none  [on_device(): branch = lax.psum(partial_out, 'tensor')]
    ppermute x0 -> x116, waiting for transfers between devices: none -> 442 us  [the longest x56 257 us: swap(): return lax.ppermute(v, axis, [(i, i ^ mask) for i in range(count)])]
    dynamic_update_slice x72 -> x48, local copies, waits for them, and re-layouts: 344 us -> 14.6 us  [the longest x41 10 us: placed(): lax.dynamic_update_slice(whole, piece.reshape((1,) * lead + tail), tuple(...]
    ppermute x0 -> x116, starting transfers between devices: none -> 239 us  [the longest x56 106 us: swap(): return lax.ppermute(v, axis, [(i, i ^ mask) for i in range(count)])]
    all_gather x4 -> x0, waiting for transfers between devices: 190 us -> none  [the longest x1 98.3 us: on_device(): lax.all_gather(part_out, 'tensor', axis=1, tiled=True)]
    psum x4 -> x0, blocking collectives: 189 us -> none  [the longest x1 150 us: on_device(): lax.psum((shared_part, shared_filter_part, shared_bias_part), 'tensor')]
    dot_general x107 -> x23, matrix products: 290 us -> 110 us  [the longest x1 23.3 us: on_device(): gate_in = jnp.dot(normed, gate_full, preferred_element_type=F32)]
    reduce_scatter x3 -> x0, waiting for transfers between devices: 120 us -> none  [the longest x1 57.9 us: on_device(): lax.psum_scatter(out_grad, 'dp', scatter_dimension=0, tiled=True)]
  transfers between devices with their start and end apart: 11 -> 116, of which waited for: 6 -> 50; matrix products, arithmetic and copies ran while one was open for 21% -> 22% of each run, Pallas kernels for 0% -> 7%
where the time goes in v1:
time: 1070 us; the launch traced here: 1060 us
  waiting for transfers between devices  442 us (41%)
  starting transfers between devices  239 us (22%)
  local copies, waits for them, and re-layouts  156 us (15%)
  matrix products  110 us (10%)
  Pallas kernels  76.6 us (7%)
  other arithmetic  31.1 us (3%)
    ppermute x56, waiting for transfers between devices, swap(): return lax.ppermute(v, axis, [(i, i ^ mask) for i in range(count)])  257 us
    ppermute x56, starting transfers between devices, swap(): return lax.ppermute(v, axis, [(i, i ^ mask) for i in range(count)])  106 us
    ppermute x18, waiting for transfers between devices, line_gather(): lax.ppermute(right[-1], 'tensor', [(i + 1, i) for i in range(0, count - j)])  92 us
    ppermute x9, waiting for transfers between devices, line_scatter(): lax.ppermute(send_right, 'tensor', [(i, i + 1) for i in range(t)])  53.6 us
    ppermute x18, starting transfers between devices, line_gather(): lax.ppermute(left[-1], 'tensor', [(i, i + 1) for i in range(j - 1, count...  52.8 us
    pallas_call x1, Pallas kernels, mixer_backward(): pl.pallas_call(backward_kernel, grid_spec=pltpu.PrefetchScalarGridSpec(nu...  50.9 us
    unnamed x185, local copies, waits for them, and re-layouts  48.5 us
    gather x2, local copies, waits for them, and re-layouts, returned(): return line_gather(flat(back)).reshape(-1, rows.shape[-1])[lines]  37.6 us
  transfers between devices with their start and end apart: 116, of which 50 were waited for; matrix products, arithmetic and copies ran while one was open for 22% of the time, Pallas kernels for 7%

profile of v1, /device:TPU:1, one launch (start us, length us, event | category | flops | bytes accessed | tf_op | source)
XLA Modules:
  0.0 1056.8 jit_solution(13678958744507478489)
XLA Ops:
  29.7 8.0 fusion.29
  131.7 12.8 %collective-permute-start.8 = (bf16[192,896]{1,0:T(8,128)(2,1)S(1)}, bf16[192,896]{1,0:T(8,128)(2,1)S(1)}, u32[]{:S(2)}, u32[]{:S(2)}) collective-permute-start(bf16[192,896]{1,0:T(8,128)(2,1)S(1)} %collective-permute-done.7), channel_id=1, source_target_pairs={{2,3},{6,7},{10,11},{14,15},{18,19},{22,23},{26,27},{30,31}} | collective-permute-start | bytes 1032200 | tf_op jit(solution)/shard_map/ppermute | solution.py:401
  160.5 35.8 %collective-permute-done.44 = bf16[192,768]{1,0:T(8,128)(2,1)S(1)} collective-permute-done((bf16[192,768]{1,0:T(8,128)(2,1)S(1)}, bf16[192,768]{1,0:T(8,128)(2,1)S(1)}, u32[]{:S(2)}, u32[]{:S(2)}) %collective-permute-start.44) | collective-permute-done | bytes 294944 | tf_op jit(solution)/shard_map/ppermute | solution.py:360
  238.3 25.1 %collective-permute-done.34 = bf16[2,2,192,768]{3,2,1,0:T(8,128)(2,1)S(1)} collective-permute-done((bf16[2,2,192,768]{3,2,1,0:T(8,128)(2,1)S(1)}, bf16[2,2,192,768]{3,2,1,0:T(8,128)(2,1)S(1)}, u32[]{:S(2)}, u32[]{:S(2)}) %collective-permute-start.34) | collective-permute-done | bytes 1179680 | tf_op jit(solution)/shard_map/ppermute | solution.py:360
  272.1 46.0 %collective-permute-done.15 = bf16[2,2,192,896]{3,2,1,0:T(8,128)(2,1)S(1)} collective-permute-done((bf16[2,2,192,896]{3,2,1,0:T(8,128)(2,1)S(1)}, bf16[2,2,192,896]{3,2,1,0:T(8,128)(2,1)S(1)}, u32[]{:S(2)}, u32[]{:S(2)}) %collective-permute-start.15) | collective-permute-done | bytes 1376288 | tf_op jit(solution)/shard_map/ppermute | solution.py:360
  318.5 8.7 fusion.110.proj_ref.proj_before_ref
  330.3 25.8 %mixer_forward.1 = (f32[2048,768]{1,0:T(8,128)}, bf16[16,128,768]{2,1,0:T(8,128)(2,1)}) custom-call(s32[4]{0:T(128)} %fusion.102.lens_ref, f32[2048,896]{1,0:T(8,128)} %fusion.110.proj_ref.proj_before_ref, f32[2048,256]{1,0:T(8,128)} %fusion.111.shared_ref.shared_before_ref, f32[4,768]{1,0:T(4,128)} %fusion.81.fw_ref, f32[1,768]{1,0:T(1,128)} %get-tuple-element.200.fb_ref, ...), custom_call_target="tpu_custom_call" | custom-call | flops 20000000000 | bytes 30000000 | tf_op jit(solution)/shard_map/mixer_forward/pallas_call | solution.py:292
  356.1 23.3 %multiply_reduce_fusion.2 = (f32[2048]{0:T(1024)S(1)}, f32[2048,768]{1,0:T(8,128)S(1)}, f32[2048,768]{1,0:T(8,128)}) fusion(f32[2048,768]{1,0:T(8,128)} %get-tuple-element.47.out_ref, bf16[2048,1536]{1,0:T(8,128)(2,1)} %bitcast.515, bf16[1536,768]{1,0:T(8,128)(2,1)S(1)} %bitcast.524), kind=kOutput, calls=%fused_computation.7 | convolution fusion | flops 4842846208 | bytes 27533312 | tf_op jit(solution)/shard_map/dot_general | solution.py:561
  397.2 9.1 copy.89
  406.2 8.7 copy.87
  415.5 14.1 %multiply_convert_fusion = (bf16[2048,768]{1,0:T(8,128)(2,1)}, f32[2048,768]{1,0:T(8,128)}, bf16[2048,768]{1,0:T(8,128)(2,1)S(1)}) fusion(f32[2048,768]{1,0:T(8,128)} %get-tuple-element.217, f32[2048,768]{1,0:T(8,128)} %get-tuple-element.47.out_ref, f32[2048]{0:T(1024)S(1)} %add_multiply_fusion, f32[2048,768]{1,0:T(8,128)} %copy-done.12, ...), kind=kLoop, calls=%fused_computation.3 | loop fusion | flops 31457280 | bytes 37776384 | tf_op jit(solution)/shard_map/convert_element_type | solution.py:604
  438.2 50.9 %mixer_backward.1 = (bf16[2048,768]{1,0:T(8,128)(2,1)}, f32[2048,256]{1,0:T(8,128)}, bf16[2048,128]{1,0:T(8,128)(2,1)}, f32[8,768]{1,0:T(8,128)}, f32[8,256]{1,0:T(8,128)}, /*index=5*/f32[8,128]{1,0:T(8,128)}) custom-call(s32[4]{0:T(128)} %fusion.102.lens_ref, f32[2048,896]{1,0:T(8,128)} %fusion.110.proj_ref.proj_before_ref, ...), custom_call_target="tpu_custom_call" | custom-call | flops 40000000000 | bytes 60000000 | tf_op jit(solution)/shard_map/mixer_backward/pallas_call | solution.py:324
  544.2 26.2 %collective-permute-done.101 = bf16[2,2,192,256]{3,2,1,0:T(8,128)(2,1)S(1)} collective-permute-done((bf16[2,2,192,256]{3,2,1,0:T(8,128)(2,1)S(1)}, bf16[2,2,192,256]{3,2,1,0:T(8,128)(2,1)S(1)}, u32[]{:S(2)}, u32[]{:S(2)}) %collective-permute-start.101) | collective-permute-done | bytes 393248 | tf_op jit(solution)/shard_map/ppermute | solution.py:360
  581.7 18.9 %collective-permute-done.91 = bf16[2,2,192,896]{3,2,1,0:T(8,128)(2,1)S(1)} collective-permute-done((bf16[2,2,192,896]{3,2,1,0:T(8,128)(2,1)S(1)}, bf16[2,2,192,896]{3,2,1,0:T(8,128)(2,1)S(1)}, u32[]{:S(2)}, u32[]{:S(2)}) %collective-permute-start.91) | collective-permute-done | bytes 1376288 | tf_op jit(solution)/shard_map/ppermute | solution.py:360
  676.7 12.0 %collective-permute-done.65 = bf16[512,1536]{1,0:T(8,128)(2,1)S(1)} collective-permute-done((bf16[512,1536]{1,0:T(8,128)(2,1)S(1)}, bf16[512,1536]{1,0:T(8,128)(2,1)S(1)}, u32[]{:S(2)}, u32[]{:S(2)}) %collective-permute-start.65) | collective-permute-done | bytes 1572896 | tf_op jit(solution)/shard_map/ppermute | solution.py:360
  701.0 21.6 %collective-permute-done.49 = bf16[512,1536]{1,0:T(8,128)(2,1)} collective-permute-done((bf16[512,1536]{1,0:T(8,128)(2,1)S(1)}, bf16[512,1536]{1,0:T(8,128)(2,1)}, u32[]{:S(2)}, u32[]{:S(2)}) %collective-permute-start.49) | collective-permute-done | bytes 1572896 | tf_op jit(solution)/shard_map/ppermute | solution.py:360
  741.0 29.6 %collective-permute-done.96 = bf16[192,896]{1,0:T(8,128)(2,1)S(1)} collective-permute-done((bf16[192,896]{1,0:T(8,128)(2,1)S(1)}, bf16[192,896]{1,0:T(8,128)(2,1)S(1)}, u32[]{:S(2)}, u32[]{:S(2)}) %collective-permute-start.96) | collective-permute-done | bytes 344096 | tf_op jit(solution)/shard_map/ppermute | solution.py:416
  814.7 16.1 %collective-permute-done.97 = bf16[192,896]{1,0:T(8,128)(2,1)S(1)} collective-permute-done((bf16[192,896]{1,0:T(8,128)(2,1)S(1)}, bf16[192,896]{1,0:T(8,128)(2,1)S(1)}, u32[]{:S(2)}, u32[]{:S(2)}) %collective-permute-start.97) | collective-permute-done | bytes 344096 | tf_op jit(solution)/shard_map/ppermute | solution.py:416
  830.8 37.1 %collective-permute-start.77 = (f32[12,768]{1,0:T(8,128)S(1)}, f32[12,768]{1,0:T(8,128)S(1)}, u32[]{:S(2)}, u32[]{:S(2)}) collective-permute-start(f32[12,768]{1,0:T(8,128)S(1)} %add.825), channel_id=1, source_target_pairs={{0,1},{1,0},{2,3},{3,2},{4,5},{5,4},{6,7},{7,6},{8,9},{9,8},{10,11... | collective-permute-start | bytes 110600 | tf_op jit(solution)/shard_map/ppermute | solution.py:360
  909.2 24.7 %collective-permute-done.74 = bf16[512,1536]{1,0:T(8,128)(2,1)S(1)} collective-permute-done((bf16[512,1536]{1,0:T(8,128)(2,1)}, bf16[512,1536]{1,0:T(8,128)(2,1)S(1)}, u32[]{:S(2)}, u32[]{:S(2)}) %collective-permute-start.74) | collective-permute-done | bytes 1572896 | tf_op jit(solution)/shard_map/ppermute | solution.py:402
  936.0 31.6 %collective-permute-done.55 = bf16[512,1536]{1,0:T(8,128)(2,1)S(1)} collective-permute-done((bf16[512,1536]{1,0:T(8,128)(2,1)}, bf16[512,1536]{1,0:T(8,128)(2,1)S(1)}, u32[]{:S(2)}, u32[]{:S(2)}) %collective-permute-start.55) | collective-permute-done | bytes 1572896 | tf_op jit(solution)/shard_map/ppermute | solution.py:402
  990.2 11.1 %collective-permute-done.75 = bf16[512,1536]{1,0:T(8,128)(2,1)S(1)} collective-permute-done((bf16[512,1536]{1,0:T(8,128)(2,1)S(1)}, bf16[512,1536]{1,0:T(8,128)(2,1)S(1)}, u32[]{:S(2)}, u32[]{:S(2)}) %collective-permute-start.75) | collective-permute-done | bytes 1572896 | tf_op jit(solution)/shard_map/ppermute | solution.py:402
  1002.6 18.8 %gather_fusion.1 = bf16[2048,1536]{1,0:T(8,128)(2,1)} fusion(bf16[3584,1536]{1,0:T(8,128)(2,1)} %bitcast.144, s32[2048]{0:T(1024)S(1)} %fusion.90), kind=kCustom, calls=%fused_computation.1 | custom fusion | bytes 12591104 | tf_op jit(solution)/shard_map/gather | solution.py:590
  1037.8 18.8 %gather_fusion = bf16[2048,1536]{1,0:T(8,128)(2,1)} fusion(bf16[3584,1536]{1,0:T(8,128)(2,1)} %bitcast.105, s32[2048]{0:T(1024)S(1)} %fusion.90), kind=kCustom, calls=%fused_computation | custom fusion | bytes 12591104 | tf_op jit(solution)/shard_map/gather | solution.py:590
  (613 shorter events, 519.0 us)
Async XLA Ops:
  2.5 92.1 %collective-permute-start.37 = (bf16[192,768]{1,0:T(8,128)(2,1)}, bf16[192,768]{1,0:T(8,128)(2,1)}, u32[]{:S(2)}, u32[]{:S(2)}) collective-permute-start(bf16[192,768]{1,0:T(8,128)(2,1)} %convert_element_type.371), channel_id=1, source_target_pairs={{0,1},{1,2},{2,3},{4,5},{5,6},{6,7},{8,9},{9,10},{10,11},{12,13},{... | collective-permute-start | bytes 884744 | tf_op jit(solution)/shard_map/ppermute | solution.py:401
  7.3 91.8 %collective-permute-start.40 = (bf16[192,768]{1,0:T(8,128)(2,1)}, bf16[192,768]{1,0:T(8,128)(2,1)}, u32[]{:S(2)}, u32[]{:S(2)}) collective-permute-start(bf16[192,768]{1,0:T(8,128)(2,1)} %convert_element_type.371), channel_id=1, source_target_pairs={{1,0},{2,1},{3,2},{5,4},{6,5},{7,6},{9,8},{10,9},{11,10},{13,12},{... | collective-permute-start | bytes 884744 | tf_op jit(solution)/shard_map/ppermute | solution.py:402
  146.9 89.4 %collective-permute-start.3 = (bf16[2,256,1536]{2,1,0:T(8,128)(2,1)S(1)}, bf16[2,256,1536]{2,1,0:T(8,128)(2,1)S(1)}, u32[]{:S(2)}, u32[]{:S(2)}) collective-permute-start(bf16[2,256,1536]{2,1,0:T(8,128)(2,1)S(1)} %get-tuple-element.143), channel_id=1, source_target_pairs={{0,4},{4,0},{1,5},{5,1},{2,6},{6,2},{3,7},{7,3},{8,12},{12,8},{9,1... | collective-permute-start | bytes 4718600 | tf_op jit(solution)/shard_map/ppermute | solution.py:360
  154.0 83.8 %collective-permute-start.4 = (bf16[2,256,1536]{2,1,0:T(8,128)(2,1)S(1)}, bf16[2,256,1536]{2,1,0:T(8,128)(2,1)S(1)}, u32[]{:S(2)}, u32[]{:S(2)}) collective-permute-start(bf16[2,256,1536]{2,1,0:T(8,128)(2,1)S(1)} %get-tuple-element.143), channel_id=1, source_target_pairs={{0,8},{8,0},{1,9},{9,1},{2,10},{10,2},{3,11},{11,3},{4,12},{12,4},... | collective-permute-start | bytes 4718600 | tf_op jit(solution)/shard_map/ppermute | solution.py:360
  155.4 114.2 %collective-permute-start.58 = (bf16[2,256,1536]{2,1,0:T(8,128)(2,1)S(1)}, bf16[2,256,1536]{2,1,0:T(8,128)(2,1)S(1)}, u32[]{:S(2)}, u32[]{:S(2)}) collective-permute-start(bf16[2,256,1536]{2,1,0:T(8,128)(2,1)S(1)} %bitcast_dynamic-update-slice_fusion.29), channel_id=1, source_target_pairs={{0,4},{4,0},{1,5},{5,1},{2,6},{6,2},{3,7},{7,3},{8,12},{12,8},{9,1... | collective-permute-start | bytes 4718600 | tf_op jit(solution)/shard_map/ppermute | solution.py:360
  236.3 143.7 %collective-permute-start.46 = (bf16[2,2,192,768]{3,2,1,0:T(8,128)(2,1)S(1)}, bf16[2,2,192,768]{3,2,1,0:T(8,128)(2,1)}, u32[]{:S(2)}, u32[]{:S(2)}) collective-permute-start(bf16[2,2,192,768]{3,2,1,0:T(8,128)(2,1)S(1)} %bitcast_dynamic-update-slice_fusion.57), channel_id=1, source_target_pairs={{0,16},{16,0},{1,17},{17,1},{2,18},{18,2},{3,19},{19,3},{4,20},{20... | collective-permute-start | bytes 3538952 | tf_op jit(solution)/shard_map/ppermute | solution.py:360
  237.8 80.2 %collective-permute-start.15 = (bf16[2,2,192,896]{3,2,1,0:T(8,128)(2,1)S(1)}, bf16[2,2,192,896]{3,2,1,0:T(8,128)(2,1)S(1)}, u32[]{:S(2)}, u32[]{:S(2)}) collective-permute-start(bf16[2,2,192,896]{3,2,1,0:T(8,128)(2,1)S(1)} %bitcast_dynamic-update-slice_fusion.38), channel_id=1, source_target_pairs={{0,16},{16,0},{1,17},{17,1},{2,18},{18,2},{3,19},{19,3},{4,20},{20... | collective-permute-start | bytes 4128776 | tf_op jit(solution)/shard_map/ppermute | solution.py:360
  263.4 54.9 %collective-permute-start.5 = (bf16[2,256,1536]{2,1,0:T(8,128)(2,1)S(1)}, bf16[2,256,1536]{2,1,0:T(8,128)(2,1)S(1)}, u32[]{:S(2)}, u32[]{:S(2)}) collective-permute-start(bf16[2,256,1536]{2,1,0:T(8,128)(2,1)S(1)} %collective-permute-done.4), channel_id=1, source_target_pairs={{0,4},{4,0},{1,5},{5,1},{2,6},{6,2},{3,7},{7,3},{8,12},{12,8},{9,1... | collective-permute-start | bytes 4718600 | tf_op jit(solution)/shard_map/ppermute | solution.py:360
  268.6 115.0 %collective-permute-start.60 = (bf16[2,256,1536]{2,1,0:T(8,128)(2,1)}, bf16[2,256,1536]{2,1,0:T(8,128)(2,1)}, u32[]{:S(2)}, u32[]{:S(2)}) collective-permute-start(bf16[2,256,1536]{2,1,0:T(8,128)(2,1)} %collective-permute-done.59), channel_id=1, source_target_pairs={{0,4},{4,0},{1,5},{5,1},{2,6},{6,2},{3,7},{7,3},{8,12},{12,8},{9,1... | collective-permute-start | bytes 4718600 | tf_op jit(solution)/shard_map/ppermute | solution.py:360
  438.0 133.8 %collective-permute-start.106 = (bf16[2,2,192,768]{3,2,1,0:T(8,128)(2,1)}, bf16[2,2,192,768]{3,2,1,0:T(8,128)(2,1)}, u32[]{:S(2)}, u32[]{:S(2)}) collective-permute-start(bf16[2,2,192,768]{3,2,1,0:T(8,128)(2,1)} %fusion.46), channel_id=1, source_target_pairs={{0,16},{16,0},{1,17},{17,1},{2,18},{18,2},{3,19},{19,3},{4,20},{20... | collective-permute-start | bytes 3538952 | tf_op jit(solution)/shard_map/ppermute | solution.py:360
  517.4 155.2 %collective-permute-start.63 = (bf16[512,1536]{1,0:T(8,128)(2,1)}, bf16[512,1536]{1,0:T(8,128)(2,1)S(1)}, u32[]{:S(2)}, u32[]{:S(2)}) collective-permute-start(bf16[512,1536]{1,0:T(8,128)(2,1)} %fusion.35), channel_id=1, source_target_pairs={{0,4},{4,0},{1,5},{5,1},{2,6},{6,2},{3,7},{7,3},{8,12},{12,8},{9,1... | collective-permute-start | bytes 4718600 | tf_op jit(solution)/shard_map/ppermute | solution.py:360
  526.2 111.6 %collective-permute-start.64 = (bf16[512,1536]{1,0:T(8,128)(2,1)}, bf16[512,1536]{1,0:T(8,128)(2,1)}, u32[]{:S(2)}, u32[]{:S(2)}) collective-permute-start(bf16[512,1536]{1,0:T(8,128)(2,1)} %fusion.36), channel_id=1, source_target_pairs={{0,4},{4,0},{1,5},{5,1},{2,6},{6,2},{3,7},{7,3},{8,12},{12,8},{9,1... | collective-permute-start | bytes 4718600 | tf_op jit(solution)/shard_map/ppermute | solution.py:360
  571.8 71.2 %collective-permute-start.48 = (bf16[512,1536]{1,0:T(8,128)(2,1)}, bf16[512,1536]{1,0:T(8,128)(2,1)}, u32[]{:S(2)}, u32[]{:S(2)}) collective-permute-start(bf16[512,1536]{1,0:T(8,128)(2,1)} %convolution_convert_fusion), channel_id=1, source_target_pairs={{0,4},{4,0},{1,5},{5,1},{2,6},{6,2},{3,7},{7,3},{8,12},{12,8},{9,1... | collective-permute-start | bytes 4718600 | tf_op jit(solution)/shard_map/ppermute | solution.py:360
  672.0 50.6 %collective-permute-start.49 = (bf16[512,1536]{1,0:T(8,128)(2,1)S(1)}, bf16[512,1536]{1,0:T(8,128)(2,1)}, u32[]{:S(2)}, u32[]{:S(2)}) collective-permute-start(bf16[512,1536]{1,0:T(8,128)(2,1)S(1)} %fusion.32), channel_id=1, source_target_pairs={{0,8},{8,0},{1,9},{9,1},{2,10},{10,2},{3,11},{11,3},{4,12},{12,4},... | collective-permute-start | bytes 4718600 | tf_op jit(solution)/shard_map/ppermute | solution.py:360
  672.6 61.3 %collective-permute-start.95 = (bf16[192,896]{1,0:T(8,128)(2,1)S(1)}, bf16[192,896]{1,0:T(8,128)(2,1)S(1)}, u32[]{:S(2)}, u32[]{:S(2)}) collective-permute-start(bf16[192,896]{1,0:T(8,128)(2,1)S(1)} %get-tuple-element.178), channel_id=1, source_target_pairs={{0,1},{4,5},{8,9},{12,13},{16,17},{20,21},{24,25},{28,29}} | collective-permute-start | bytes 1032200 | tf_op jit(solution)/shard_map/ppermute | solution.py:416
  727.8 72.0 %collective-permute-start.70 = (bf16[512,1536]{1,0:T(8,128)(2,1)}, bf16[512,1536]{1,0:T(8,128)(2,1)}, u32[]{:S(2)}, u32[]{:S(2)}) collective-permute-start(bf16[512,1536]{1,0:T(8,128)(2,1)} %bitcast.136), channel_id=1, source_target_pairs={{0,1},{1,2},{2,3},{4,5},{5,6},{6,7},{8,9},{9,10},{10,11},{12,13},{... | collective-permute-start | bytes 4718600 | tf_op jit(solution)/shard_map/ppermute | solution.py:401
  787.4 107.4 %collective-permute-start.73 = (bf16[512,1536]{1,0:T(8,128)(2,1)}, bf16[512,1536]{1,0:T(8,128)(2,1)}, u32[]{:S(2)}, u32[]{:S(2)}) collective-permute-start(bf16[512,1536]{1,0:T(8,128)(2,1)} %bitcast.136), channel_id=1, source_target_pairs={{1,0},{2,1},{3,2},{5,4},{6,5},{7,6},{9,8},{10,9},{11,10},{13,12},{... | collective-permute-start | bytes 4718600 | tf_op jit(solution)/shard_map/ppermute | solution.py:402
  793.1 103.0 %collective-permute-start.51 = (bf16[512,1536]{1,0:T(8,128)(2,1)}, bf16[512,1536]{1,0:T(8,128)(2,1)}, u32[]{:S(2)}, u32[]{:S(2)}) collective-permute-start(bf16[512,1536]{1,0:T(8,128)(2,1)} %bitcast.97), channel_id=1, source_target_pairs={{0,1},{1,2},{2,3},{4,5},{5,6},{6,7},{8,9},{9,10},{10,11},{12,13},{... | collective-permute-start | bytes 4718600 | tf_op jit(solution)/shard_map/ppermute | solution.py:401
  798.4 99.5 %collective-permute-start.54 = (bf16[512,1536]{1,0:T(8,128)(2,1)}, bf16[512,1536]{1,0:T(8,128)(2,1)}, u32[]{:S(2)}, u32[]{:S(2)}) collective-permute-start(bf16[512,1536]{1,0:T(8,128)(2,1)} %bitcast.97), channel_id=1, source_target_pairs={{1,0},{2,1},{3,2},{5,4},{6,5},{7,6},{9,8},{10,9},{11,10},{13,12},{... | collective-permute-start | bytes 4718600 | tf_op jit(solution)/shard_map/ppermute | solution.py:402
  799.8 99.5 %collective-permute-start.71 = (bf16[512,1536]{1,0:T(8,128)(2,1)}, bf16[512,1536]{1,0:T(8,128)(2,1)}, u32[]{:S(2)}, u32[]{:S(2)}) collective-permute-start(bf16[512,1536]{1,0:T(8,128)(2,1)} %collective-permute-done.70), channel_id=1, source_target_pairs={{1,2},{2,3},{5,6},{6,7},{9,10},{10,11},{13,14},{14,15},{17,18},{18... | collective-permute-start | bytes 4718600 | tf_op jit(solution)/shard_map/ppermute | solution.py:401
  897.9 69.7 %collective-permute-start.55 = (bf16[512,1536]{1,0:T(8,128)(2,1)}, bf16[512,1536]{1,0:T(8,128)(2,1)S(1)}, u32[]{:S(2)}, u32[]{:S(2)}) collective-permute-start(bf16[512,1536]{1,0:T(8,128)(2,1)} %collective-permute-done.54), channel_id=1, source_target_pairs={{1,0},{2,1},{5,4},{6,5},{9,8},{10,9},{13,12},{14,13},{17,16},{18,1... | collective-permute-start | bytes 4718600 | tf_op jit(solution)/shard_map/ppermute | solution.py:402
  899.2 69.7 %collective-permute-start.72 = (bf16[512,1536]{1,0:T(8,128)(2,1)}, bf16[512,1536]{1,0:T(8,128)(2,1)}, u32[]{:S(2)}, u32[]{:S(2)}) collective-permute-start(bf16[512,1536]{1,0:T(8,128)(2,1)} %collective-permute-done.71), channel_id=1, source_target_pairs={{2,3},{6,7},{10,11},{14,15},{18,19},{22,23},{26,27},{30,31}} | collective-permute-start | bytes 4718600 | tf_op jit(solution)/shard_map/ppermute | solution.py:401
  933.9 67.4 %collective-permute-start.75 = (bf16[512,1536]{1,0:T(8,128)(2,1)S(1)}, bf16[512,1536]{1,0:T(8,128)(2,1)S(1)}, u32[]{:S(2)}, u32[]{:S(2)}) collective-permute-start(bf16[512,1536]{1,0:T(8,128)(2,1)S(1)} %collective-permute-done.74), channel_id=1, source_target_pairs={{1,0},{5,4},{9,8},{13,12},{17,16},{21,20},{25,24},{29,28}} | collective-permute-start | bytes 4718600 | tf_op jit(solution)/shard_map/ppermute | solution.py:402
  967.6 67.5 %collective-permute-start.56 = (bf16[512,1536]{1,0:T(8,128)(2,1)S(1)}, bf16[512,1536]{1,0:T(8,128)(2,1)}, u32[]{:S(2)}, u32[]{:S(2)}) collective-permute-start(bf16[512,1536]{1,0:T(8,128)(2,1)S(1)} %collective-permute-done.55), channel_id=1, source_target_pairs={{1,0},{5,4},{9,8},{13,12},{17,16},{21,20},{25,24},{29,28}} | collective-permute-start | bytes 4718600 | tf_op jit(solution)/shard_map/ppermute | solution.py:402
  (164 other events, 3591.7 us)

commit v2 on v1

v2 whole, which is shorter than its diff:
```python
import jax
import jax.numpy as jnp
from jax import lax
from jax.experimental import pallas as pl
from jax.experimental.pallas import tpu as pltpu
from jax.sharding import PartitionSpec as P

SPAN = 128
HALO = 8
LANES = 128
F32 = jnp.float32
BF16 = jnp.bfloat16
EPSILON = 1e-05


def mm(a, b):
    return jnp.dot(a, b, preferred_element_type=F32)


def mm_t(a, b):
    return lax.dot_general(a, b, (((1,), (1,)), ((), ())), preferred_element_type=F32)


def halves(v):
    high = v.astype(BF16)
    return high, (v - high.astype(F32)).astype(BF16)


def widen(v, spread):
    high, rest = halves(v)
    return mm(high, spread) + mm(rest, spread)


def head_sum(v, spread):
    high, rest = halves(v)
    return mm_t(high, spread) + mm_t(rest, spread)


def start_of(place, lens_ref):
    end, start = jnp.int32(0), jnp.zeros_like(place)
    for i in range(lens_ref.shape[0]):
        start = jnp.where(place >= end, end, start)
        end = end + lens_ref[i]
    return start


def taps(current, before, reach):
    whole = jnp.concatenate([before, current], axis=0)
    rows = current.shape[0]
    return [whole[HALO - k : HALO - k + rows] for k in range(reach)]


def filtered(shifted, allowed, kernel, bias):
    result = bias + kernel[0:1] * shifted[0]
    for k in range(1, len(shifted)):
        result = result + kernel[k : k + 1] * shifted[k] * allowed[k]
    return result


def permitted(place, start, reach, width):
    flags = [None]
    for k in range(1, reach):
        flags.append(jnp.where(place - k >= start, 1.0, 0.0)[:, :1])
    return flags


def softplus(v):
    return jnp.maximum(v, 0.0) + jnp.log1p(jnp.exp(-jnp.abs(v)))


def chunk_setup(base, lens_ref, span):
    place = base + lax.broadcasted_iota(jnp.int32, (span, LANES), 0)
    start = start_of(place, lens_ref)
    last_start = start_of(jnp.full((1, LANES), base + span - 1, jnp.int32), lens_ref)
    return place, start, last_start


def stacked(pair, low_lanes):
    zero = jnp.zeros_like(pair)
    return jnp.concatenate([jnp.where(low_lanes, pair, zero), jnp.where(low_lanes, zero, pair)], axis=0)


def forward_kernel(
    lens_ref, order_ref, proj_ref, fw_ref, fb_ref, sf_ref, sb_ref, head_ref, skip_ref, spread_ref,
    out_ref, kept_ref, memory, before, shared_before,
):
    step = pl.program_id(0)
    span = proj_ref.shape[0]
    width = out_ref.shape[1]
    reach = fw_ref.shape[0]
    pairs = width // LANES
    base = step * span

    @pl.when(step == 0)
    def _():
        memory[...] = jnp.zeros_like(memory)
        before[...] = jnp.zeros_like(before)
        shared_before[...] = jnp.zeros_like(shared_before)

    place, start, last_start = chunk_setup(base, lens_ref, span)
    allowed = permitted(place, start, reach, width)
    inputs = proj_ref[:, :width]
    shared = proj_ref[:, width + LANES :]
    conv = filtered(taps(inputs, before[...], reach), allowed, fw_ref, fb_ref[...])
    values = conv * jax.nn.sigmoid(conv)
    conv = filtered(taps(shared, shared_before[...], reach), allowed, sf_ref, sb_ref[...])
    factors = conv * jax.nn.sigmoid(conv)
    before[...] = inputs[span - HALO :]
    shared_before[...] = shared[span - HALO :]
    writes = factors[:, :LANES].astype(BF16)
    reads = factors[:, LANES:].astype(BF16)
    size = softplus(proj_ref[:, width : width + LANES] + head_ref[0:1])
    decay = -size * head_ref[1:2]
    row = lax.broadcasted_iota(jnp.int32, (span, span), 0)
    col = lax.broadcasted_iota(jnp.int32, (span, span), 1)
    lower = jnp.where(row >= col, 1.0, 0.0)
    total = jnp.dot(lower, decay, precision=lax.Precision.HIGHEST, preferred_element_type=F32)
    total_t = total.T
    inside = (col <= row) & (col + base >= start)
    scores = jnp.where(inside, mm_t(reads, writes), 0.0)
    spread = spread_ref[...]
    scaled = values * widen(size, spread)
    scaled_low = scaled.astype(BF16)
    entering = jnp.exp(total) * jnp.where(start < base, 1.0, 0.0)
    state = memory[...]
    state_low = state.astype(BF16)
    kept_ref[0] = state_low
    remote = mm(reads, state_low) * widen(entering, spread) + skip_ref[...] * values
    low_lanes = lax.broadcasted_iota(jnp.int32, (span, LANES), 1) < LANES // 2
    for pair in range(pairs):
        lanes = slice(pair * LANES, (pair + 1) * LANES)
        mixing = []
        for head in (2 * pair, 2 * pair + 1):
            fade = jnp.exp(jnp.minimum(total[:, head : head + 1] - total_t[head : head + 1, :], 0.0))
            mixing.append((scores * fade).astype(BF16))
        local = mm(jnp.concatenate(mixing, axis=1), stacked(scaled_low[:, lanes], low_lanes))
        out_ref[:, lanes] = (local + remote[:, lanes]).astype(out_ref.dtype)
    end = total[span - 1 : span]
    closing = jnp.exp(end - total) * jnp.where(place >= last_start, 1.0, 0.0)
    added = mm(writes.T, (scaled * widen(closing, spread)).astype(BF16))
    keeping = jnp.exp(end) * jnp.where(last_start < base, 1.0, 0.0)
    memory[...] = state * widen(jnp.broadcast_to(keeping, (8, LANES)), spread)[0:1] + added


def backward_kernel(
    lens_ref, order_ref, proj_ref, proj_before_ref, grad_ref, out_ref, kept_ref,
    fw_ref, fb_ref, sf_ref, sb_ref, head_ref, skip_ref, spread_ref,
    proj_grad_ref, shared_grad_ref, fsum_ref, ssum_ref, hsum_ref,
    memory_grad, after, shared_after,
):
    step = pl.program_id(0)
    steps = pl.num_programs(0)
    span = proj_ref.shape[0]
    width = out_ref.shape[1]
    reach = fw_ref.shape[0]
    pairs = width // LANES
    chunk = steps - 1 - step
    base = chunk * span

    @pl.when(step == 0)
    def _():
        memory_grad[...] = jnp.zeros_like(memory_grad)
        after[...] = jnp.zeros_like(after)
        shared_after[...] = jnp.zeros_like(shared_after)
        fsum_ref[...] = jnp.zeros_like(fsum_ref)
        ssum_ref[...] = jnp.zeros_like(ssum_ref)
        hsum_ref[...] = jnp.zeros_like(hsum_ref)

    place, start, last_start = chunk_setup(base, lens_ref, span)
    allowed = permitted(place, start, reach, width)
    first = jnp.where(chunk > 0, 1.0, 0.0)
    inputs = proj_ref[:, :width]
    shifted = taps(inputs, proj_before_ref[:, :width] * first, reach)
    conv = filtered(shifted, allowed, fw_ref, fb_ref[...])
    gate = jax.nn.sigmoid(conv)
    values = conv * gate
    slope = gate * (1.0 + conv * (1.0 - gate))
    shared_shifted = taps(proj_ref[:, width + LANES :], proj_before_ref[:, width + LANES :] * first, reach)
    conv = filtered(shared_shifted, allowed, sf_ref, sb_ref[...])
    gate = jax.nn.sigmoid(conv)
    factors = conv * gate
    shared_slope = gate * (1.0 + conv * (1.0 - gate))
    writes = factors[:, :LANES].astype(BF16)
    reads = factors[:, LANES:].astype(BF16)
    raw = proj_ref[:, width : width + LANES] + head_ref[0:1]
    size = softplus(raw)
    decay = -size * head_ref[1:2]
    row = lax.broadcasted_iota(jnp.int32, (span, span), 0)
    col = lax.broadcasted_iota(jnp.int32, (span, span), 1)
    lower = jnp.where(row >= col, 1.0, 0.0)
    upper = jnp.where(row <= col, 1.0, 0.0)
    total = jnp.dot(lower, decay, precision=lax.Precision.HIGHEST, preferred_element_type=F32)
    total_t = total.T
    start_t = start_of(base + col[0:1], lens_ref)
    inside_t = (row <= col) & (row + base >= start_t)
    scores_t = jnp.where(inside_t, mm_t(writes, reads), 0.0)
    spread = spread_ref[...]
    size_wide = widen(size, spread)
    scaled = values * size_wide
    scaled_low = scaled.astype(BF16)
    grad = grad_ref[...].astype(F32)
    grad_low = grad.astype(BF16)
    state_low = kept_ref[0]
    later = memory_grad[...]
    later_low = later.astype(BF16)
    entering = jnp.exp(total) * jnp.where(start < base, 1.0, 0.0)
    entered = (grad * widen(entering, spread)).astype(BF16)
    end = total[span - 1 : span]
    closing = jnp.exp(end - total) * jnp.where(place >= last_start, 1.0, 0.0)
    closing_wide = widen(closing, spread)
    keeping = jnp.exp(end) * jnp.where(last_start < base, 1.0, 0.0)
    keeping_wide = widen(jnp.broadcast_to(keeping, (8, LANES)), spread)[0:1]
    closed = mm(writes, later_low) * closing_wide
    low_lanes = lax.broadcasted_iota(jnp.int32, (span, LANES), 1) < LANES // 2
    scores_grad_t = jnp.zeros((span, span), F32)
    local = []
    for pair in range(pairs):
        lanes = slice(pair * LANES, (pair + 1) * LANES)
        halved = stacked(grad_low[:, lanes], low_lanes)
        mixing_grad = mm_t(scaled_low[:, lanes], halved)
        mixing = []
        for which, head in enumerate((2 * pair, 2 * pair + 1)):
            fade = jnp.exp(jnp.minimum(total_t[head : head + 1, :] - total[:, head : head + 1], 0.0))
            mixing.append((scores_t * fade).astype(BF16))
            scores_grad_t = scores_grad_t + mixing_grad[:, which * span : (which + 1) * span] * fade
        local.append(mm(jnp.concatenate(mixing, axis=1), halved))
    scaled_grad = jnp.concatenate(local, axis=1) + closed
    scores_grad_t = jnp.where(inside_t, scores_grad_t, 0.0).astype(BF16)
    kept_closing = (scaled * closing_wide).astype(BF16)
    reads_grad = mm(scores_grad_t.T, writes) + mm_t(entered, state_low)
    writes_grad = mm(scores_grad_t, reads) + mm_t(kept_closing, later_low)
    memory_grad[...] = later * keeping_wide + mm(reads.T, entered)
    skip = skip_ref[...]
    size_grad = head_sum(values * scaled_grad, spread)
    paid = head_sum(
        grad_low.astype(F32) * (out_ref[...] - skip * values) - scaled_low.astype(F32) * scaled_grad, spread
    )
    tail = jnp.sum(scaled_low.astype(F32) * closed, axis=0, keepdims=True) + keeping_wide * jnp.sum(
        later * state_low.astype(F32), axis=0, keepdims=True
    )
    tail = head_sum(jnp.broadcast_to(tail, (8, width)), spread)[0:1]
    total_grad = paid + jnp.where(place == base + span - 1, tail, 0.0)
    decay_grad = jnp.dot(upper, total_grad, precision=lax.Precision.HIGHEST, preferred_element_type=F32)
    raw_grad = (size_grad - decay_grad * head_ref[1:2]) * jax.nn.sigmoid(raw)
    proj_grad_ref[:, width:] = raw_grad.astype(proj_grad_ref.dtype)
    hsum_ref[0:1] += jnp.sum(raw_grad, axis=0, keepdims=True)
    hsum_ref[1:2] += jnp.sum(decay_grad * decay, axis=0, keepdims=True)
    conv_grad = (size_wide * scaled_grad + skip * grad) * slope
    shared_conv_grad = jnp.concatenate([writes_grad, reads_grad], axis=1) * shared_slope
    fsum_ref[reach : reach + 1] += jnp.sum(conv_grad, axis=0, keepdims=True)
    fsum_ref[reach + 1 : reach + 2] += jnp.sum(grad * values, axis=0, keepdims=True)
    ssum_ref[reach : reach + 1] += jnp.sum(shared_conv_grad, axis=0, keepdims=True)
    late = base + lax.broadcasted_iota(jnp.int32, (span + HALO, LANES), 0)
    late_allowed = permitted(late, start_of(late, lens_ref), reach, width)
    whole = jnp.concatenate([conv_grad, after[...]], axis=0)
    shared_whole = jnp.concatenate([shared_conv_grad, shared_after[...]], axis=0)
    result = fw_ref[0:1] * conv_grad
    shared_result = sf_ref[0:1] * shared_conv_grad
    fsum_ref[0:1] += jnp.sum(conv_grad * shifted[0], axis=0, keepdims=True)
    ssum_ref[0:1] += jnp.sum(shared_conv_grad * shared_shifted[0], axis=0, keepdims=True)
    for k in range(1, reach):
        masked = whole * late_allowed[k]
        fsum_ref[k : k + 1] += jnp.sum(masked[:span] * shifted[k], axis=0, keepdims=True)
        result = result + fw_ref[k : k + 1] * masked[k : k + span]
        masked = shared_whole * late_allowed[k]
        ssum_ref[k : k + 1] += jnp.sum(masked[:span] * shared_shifted[k], axis=0, keepdims=True)
        shared_result = shared_result + sf_ref[k : k + 1] * masked[k : k + span]
    after[...] = conv_grad[:HALO]
    shared_after[...] = shared_conv_grad[:HALO]
    proj_grad_ref[:, :width] = result.astype(proj_grad_ref.dtype)
    shared_grad_ref[...] = shared_result.astype(shared_grad_ref.dtype)


def head_rows(step_bias, decay_log, skip_gain, width):
    heads = step_bias.shape[0]
    table = jnp.zeros((8, LANES), F32)
    table = table.at[0, :heads].set(step_bias).at[1, :heads].set(jnp.exp(decay_log))
    skip = jnp.repeat(skip_gain, width // heads)[None, :]
    spread = (jnp.arange(LANES)[:, None] == (jnp.arange(width) // (width // heads))[None, :]).astype(BF16)
    return table, skip, spread


def fixed(shape):
    return pl.BlockSpec(shape, lambda *_: (0,) * len(shape))


def mixer_forward(lens, order, proj, fw, fb, sf, sb, table, skip, spread):
    rows = proj.shape[0]
    width = fw.shape[1]
    steps = rows // SPAN
    block = lambda cols: pl.BlockSpec((SPAN, cols), lambda i, lens_ref, order_ref: (order_ref[i], 0))
    return pl.pallas_call(
        forward_kernel,
        grid_spec=pltpu.PrefetchScalarGridSpec(
            num_scalar_prefetch=2,
            grid=(steps,),
            in_specs=[
                block(proj.shape[1]), fixed(fw.shape), fixed(fb.shape), fixed(sf.shape),
                fixed(sb.shape), fixed(table.shape), fixed(skip.shape), fixed(spread.shape),
            ],
            out_specs=[block(width), pl.BlockSpec((1, LANES, width), lambda i, *_: (i, 0, 0))],
            scratch_shapes=[
                pltpu.VMEM((LANES, width), F32),
                pltpu.VMEM((HALO, width), F32),
                pltpu.VMEM((HALO, sf.shape[1]), F32),
            ],
        ),
        out_shape=[
            jax.ShapeDtypeStruct((rows, width), F32),
            jax.ShapeDtypeStruct((steps, LANES, width), BF16),
        ],
        cost_estimate=pl.CostEstimate(flops=20 * 10**9, bytes_accessed=30 * 10**6, transcendentals=0),
        name="mixer_forward",
    )(lens, order, proj, fw, fb, sf, sb, table, skip, spread)


def mixer_backward(lens, order, proj, grad, out, kept, fw, fb, sf, sb, table, skip, spread):
    rows = proj.shape[0]
    width = fw.shape[1]
    steps = rows // SPAN
    lead = SPAN // HALO
    block = lambda cols: pl.BlockSpec((SPAN, cols), lambda i, lens_ref, order_ref: (order_ref[steps - 1 - i], 0))
    ahead = lambda cols: pl.BlockSpec(
        (HALO, cols),
        lambda i, lens_ref, order_ref: (order_ref[jnp.maximum(steps - 2 - i, 0)] * lead + lead - 1, 0),
    )
    return pl.pallas_call(
        backward_kernel,
        grid_spec=pltpu.PrefetchScalarGridSpec(
            num_scalar_prefetch=2,
            grid=(steps,),
            in_specs=[
                block(proj.shape[1]), ahead(proj.shape[1]),
                block(width), block(width), pl.BlockSpec((1, LANES, width), lambda i, *_: (steps - 1 - i, 0, 0)),
                fixed(fw.shape), fixed(fb.shape), fixed(sf.shape),
                fixed(sb.shape), fixed(table.shape), fixed(skip.shape), fixed(spread.shape),
            ],
            out_specs=[
                block(width + LANES), block(sf.shape[1]),
                fixed((8, width)), fixed((8, sf.shape[1])), fixed((8, LANES)),
            ],
            scratch_shapes=[
                pltpu.VMEM((LANES, width), F32),
                pltpu.VMEM((HALO, width), F32),
                pltpu.VMEM((HALO, sf.shape[1]), F32),
            ],
        ),
        out_shape=[
            jax.ShapeDtypeStruct((rows, width + LANES), BF16),
            jax.ShapeDtypeStruct((rows, sf.shape[1]), F32),
            jax.ShapeDtypeStruct((8, width), F32),
            jax.ShapeDtypeStruct((8, sf.shape[1]), F32),
            jax.ShapeDtypeStruct((8, LANES), F32),
        ],
        cost_estimate=pl.CostEstimate(flops=40 * 10**9, bytes_accessed=60 * 10**6, transcendentals=0),
        name="mixer_backward",
    )(lens, order, proj, proj, grad, out, kept, fw, fb, sf, sb, table, skip, spread)


def swap(v, axis, mask=1):
    count = lax.axis_size(axis)
    return lax.ppermute(v, axis, [(i, i ^ mask) for i in range(count)])


def crossed(v):
    pairs = [(a * 4 + b, b * 4 + a) for a in range(4) for b in range(4)]
    return lax.ppermute(v, ("side", "core", "tensor"), pairs)


def pick(stack, index, axis=0):
    return lax.dynamic_index_in_dim(stack, index, axis, keepdims=False)


def in_order(pieces, index):
    if len(pieces) == 2:
        first, second = pieces
        even = index == 0
        return jnp.stack([jnp.where(even, first, second), jnp.where(even, second, first)])
    whole = jnp.stack(pieces)
    return jnp.stack([pick(whole, index ^ i) for i in range(len(pieces))])


def row_doubling(v):
    pieces = [v]
    while len(pieces) < lax.axis_size("row"):
        reach = len(pieces)
        pieces = pieces + [swap(p, "row", reach) for p in pieces]
    return pieces


def line_flood(v):
    count = lax.axis_size("tensor")
    left, right = [v], [v]
    for j in range(1, count):
        left.append(lax.ppermute(left[-1], "tensor", [(i, i + 1) for i in range(j - 1, count - 1)]))
        right.append(lax.ppermute(right[-1], "tensor", [(i + 1, i) for i in range(0, count - j)]))
    return left[1:], right[1:]


def summed(v, axes):
    for axis in axes:
        reach = 1
        while reach < lax.axis_size(axis):
            v = v + swap(v, axis, reach)
            reach = reach * 2
    return v


def contract_rows(a, b):
    return lax.dot_general(a, b, (((0,), (0,)), ((), ())), preferred_element_type=F32)


def contract_columns(a, b):
    return lax.dot_general(a, b, (((1,), (1,)), ((), ())), preferred_element_type=F32)


def on_device(
    tokens, cotangent, destination, lengths, norm_gain, inner_weight, shared_weight, step_weight, filter_weight,
    filter_bias, shared_filter, shared_filter_bias, step_bias, decay_log, skip_gain, gate_gain, out_weight,
):
    row_count, model_width = tokens.shape
    width = filter_weight.shape[1]
    heads = step_bias.shape[0]
    rows_n, planes = lax.axis_size("row"), lax.axis_size("tensor")
    row, side, core, plane = (lax.axis_index(a) for a in ("row", "side", "core", "tensor"))
    group_rows = row_count // (rows_n * 4)
    owned = rows_n * group_rows
    source = (row * 2 + side) * 2 + core

    wanted = jnp.concatenate(
        [
            ((row ^ d) * planes + plane) * row_count + source * group_rows + jnp.arange(group_rows, dtype=jnp.int32)
            for d in range(rows_n)
        ]
    )
    chosen = (wanted[:, None] == destination[None, :]).astype(BF16)

    def exchanged(sent):
        return jnp.concatenate([sent[:group_rows]] + [
            swap(sent[d * group_rows : (d + 1) * group_rows], "row", d) for d in range(1, rows_n)
        ])

    def gathered(own):
        beside = swap(own, "side")
        return jnp.concatenate([own, swap(own, "core"), beside, swap(beside, "core")])

    own_tokens = exchanged(jnp.dot(chosen, tokens, preferred_element_type=F32).astype(BF16))
    hidden = own_tokens.astype(F32)
    scale = lax.rsqrt(jnp.mean(hidden * hidden, axis=-1, keepdims=True) + EPSILON)
    normed = gathered((hidden * scale * norm_gain).astype(BF16))
    own_cot = exchanged(jnp.dot(chosen, cotangent, preferred_element_type=F32).astype(BF16))
    cot = gathered(own_cot)

    step_low = jnp.pad(step_weight.astype(BF16), ((0, 0), (0, LANES - heads)))
    piece = jnp.concatenate([inner_weight[:, 1].astype(BF16), step_low, shared_weight.astype(BF16)], axis=1)
    blocks = in_order(row_doubling(crossed(piece)), row)
    left, right = line_flood(blocks)
    stack = jnp.stack(left[::-1] + [blocks] + right)
    in_full = lax.dynamic_slice_in_dim(stack, planes - 1 - plane, planes, 0)
    in_full = in_full.transpose(1, 0, 2, 3).reshape(model_width, -1)
    piece = jnp.concatenate([inner_weight[:, 0].astype(BF16), out_weight.astype(BF16)], axis=1)
    both_full = lax.all_gather(crossed(piece), ("row", "tensor"), axis=0, tiled=True)
    gate_full, out_full = both_full[:, :width], both_full[:, width:]

    params = jnp.concatenate(
        [
            filter_weight,
            filter_bias[None],
            gate_gain[None],
            jnp.pad(jnp.concatenate([step_bias, decay_log, skip_gain]), (0, width - 3 * heads))[None],
            jnp.pad(lengths.astype(F32), ((0, 0), (0, width - lengths.shape[1]))),
        ],
        axis=0,
    )
    params = crossed(params)
    fw, fb, gain = params[:4], params[4:5], params[5:6]
    bias_here, decay_here, skip_here = (params[6, i * heads : (i + 1) * heads] for i in range(3))
    lens = params[7, : lengths.shape[1]].astype(jnp.int32)
    sf, sb = shared_filter, shared_filter_bias[None]
    table, skip, spread = head_rows(bias_here, decay_here, skip_here, width)

    if group_rows % SPAN == 0:
        spans = jnp.arange(row_count // SPAN, dtype=jnp.int32)
        part = (spans * SPAN // group_rows) ^ source
        order = (((part // 2) % 2 * 2 + part % 2) * rows_n + part // 4) * (group_rows // SPAN)
        order = order + spans % (group_rows // SPAN)
        sequenced = unsequenced = lambda v: v
    else:
        order = jnp.arange(row_count // SPAN, dtype=jnp.int32)
        groups = jnp.arange(4 * rows_n, dtype=jnp.int32)
        part = groups ^ source
        to = ((part // 2) % 2 * 2 + part % 2) * rows_n + part // 4
        fro = (((groups % rows_n) * 4 + groups // rows_n) ^ source)
        sequenced = lambda v: v.reshape(4 * rows_n, group_rows, -1)[to].reshape(v.shape)
        unsequenced = lambda v: v.reshape(4 * rows_n, group_rows, -1)[fro].reshape(v.shape)

    def summed_over_group(v):
        v = v + swap(v, "core").reshape(2, 2, owned)[:, ::-1].reshape(-1)
        return v + swap(v, "side").reshape(2, 2 * owned)[::-1].reshape(-1)

    proj = sequenced(jnp.dot(normed, in_full, preferred_element_type=F32))
    mixed_seq, kept = mixer_forward(lens, order, proj, fw, fb, sf, sb, table, skip, spread)
    mixed = unsequenced(mixed_seq)
    gate_in = lax.optimization_barrier(jnp.dot(normed, gate_full, preferred_element_type=F32))
    gate_sig = jax.nn.sigmoid(gate_in)
    gate_act = gate_in * gate_sig
    gated = mixed * gate_act
    square_sum = summed_over_group(jnp.sum(gated * gated, axis=1))
    gate_scale = lax.rsqrt(square_sum / (4 * width) + EPSILON)[:, None]
    gate_normed = (gated * gate_scale * gain).astype(BF16)

    def rows_of(v, dx, dk):
        return v[(dx * 2 + dk) * owned : (dx * 2 + dk + 1) * owned]

    def summed_rows(part):
        far = swap(part(1, 1).astype(BF16), "core")
        beside = swap((part(1, 0) + far.astype(F32)).astype(BF16), "side")
        near = swap(part(0, 1).astype(BF16), "core")
        return part(0, 0) + near.astype(F32) + beside.astype(F32)

    block_of = destination // row_count
    row_of, plane_of = (block_of // planes) ^ row, block_of % planes
    slot = row_of * group_rows + destination - block_of * row_count - source * group_rows
    steps_down = (plane - plane_of) % planes

    def returned(rows):
        back = exchanged(rows)
        left, right = line_flood(back)
        held = [back] + [jnp.where(plane >= j, left[j - 1], right[planes - 1 - j]) for j in range(1, planes)]

        def settled(which):
            where = jnp.concatenate([jnp.where(steps_down == j, slot, -1)[:, None] == jnp.arange(owned)[None, :]
                                     for j in which], axis=1)
            return jnp.dot(where.astype(BF16), jnp.concatenate([held[j] for j in which]), preferred_element_type=F32)
        return (settled((0, 2)).astype(BF16) + settled((1, 3)).astype(BF16))

    branch = summed_rows(lambda dx, dk: contract_columns(rows_of(gate_normed, dx, dk), out_full))
    layer_out = returned((hidden + branch).astype(BF16))

    normed_grad = lax.optimization_barrier(jnp.dot(cot, out_full, preferred_element_type=F32))
    out_grad = contract_rows(cot, gate_normed).astype(BF16)
    gate_gain_grad = jnp.sum(normed_grad * gated * gate_scale, axis=0)
    scaled_grad = normed_grad * gain
    cross_sum = summed_over_group(jnp.sum(scaled_grad * gated, axis=1))
    gated_grad = gate_scale * scaled_grad - gated * gate_scale**3 * (cross_sum / (4 * width))[:, None]
    mixed_grad = gated_grad * gate_act
    gate_in_grad = (gated_grad * mixed * gate_sig * (1.0 + gate_in * (1.0 - gate_sig))).astype(BF16)
    gate_grad = contract_rows(normed, gate_in_grad).astype(BF16)
    both_grad = jnp.concatenate([gate_grad, out_grad], axis=1)
    both_grad = lax.psum_scatter(both_grad, ("row", "tensor"), scatter_dimension=0, tiled=True)
    both_grad = crossed(both_grad).astype(F32)
    proj_grad, shared_part, fsum, ssum, hsum = mixer_backward(
        lens, order, proj, sequenced(mixed_grad), mixed_seq, kept, fw, fb, sf, sb, table, skip, spread
    )
    proj_grad, shared_part = unsequenced(proj_grad), unsequenced(shared_part)
    back = summed_rows(lambda dx, dk: jnp.concatenate([
        contract_columns(rows_of(gate_in_grad, dx, dk), gate_full)
        + contract_columns(rows_of(proj_grad, dx, dk), in_full[:, : width + LANES]),
        rows_of(shared_part, dx, dk),
    ], axis=1))
    own_shared = back[:, model_width:].astype(BF16)
    normed_back = back[:, :model_width] + contract_columns(own_shared, in_full[:, width + LANES :])
    norm_gain_grad = jnp.sum(normed_back * hidden * scale, axis=0)
    gained = normed_back * norm_gain
    along = jnp.mean(gained * hidden, axis=1, keepdims=True)
    input_work = own_cot.astype(F32) + scale * gained - hidden * (scale**3 * along)
    input_grad = returned(input_work.astype(BF16))

    in_grad = contract_rows(normed, jnp.concatenate([proj_grad, gathered(own_shared)], axis=1)).astype(BF16)
    in_grad = lax.psum_scatter(in_grad, ("row", "tensor"), scatter_dimension=0, tiled=True)
    in_grad = crossed(in_grad).astype(F32)
    inner_grad = jnp.stack([both_grad[:, :width], in_grad[:, :width]], axis=1)

    line = lambda v: jnp.pad(v, (0, -v.shape[0] % width)).reshape(-1, width)
    skip_grad = fsum[5].reshape(heads, -1).sum(axis=1)
    small = jnp.concatenate(
        [
            fsum[:5],
            gate_gain_grad[None],
            jnp.pad(jnp.concatenate([hsum[0, :heads], hsum[1, :heads], skip_grad]), (0, width - 3 * heads))[None],
            jnp.zeros((1, width), F32),
            line(norm_gain_grad),
            line(ssum[:5].reshape(-1)),
        ],
        axis=0,
    )
    small = summed(small, ("row", "tensor"))
    mine = crossed(small[:8])
    common = summed(small[8:], ("core", "side"))
    lines = line(norm_gain_grad).shape[0]
    norm_gain_grad = common[:lines].reshape(-1)[:model_width]
    shared_sums = common[lines:].reshape(-1)[: 5 * sf.shape[1]].reshape(5, -1)
    return (
        layer_out, input_grad, norm_gain_grad, inner_grad, in_grad[:, width + LANES :],
        in_grad[:, width : width + heads], mine[:4], mine[4], shared_sums[:4], shared_sums[4],
        mine[6, :heads], mine[6, heads : 2 * heads], mine[6, 2 * heads : 3 * heads], mine[5], both_grad[:, width:],
    )


def solution(mesh):
    count, planes = mesh.devices.shape
    assert planes == 4 and count % 4 == 0
    names = ("row", "side", "core", "tensor")
    inner = jax.sharding.Mesh(mesh.devices.reshape(count // 4, 2, 2, planes), names)
    dp = ("row", "side", "core")
    in_specs = (
        P(dp, None), P(dp, None), P(dp), P(dp, None), P(), P(dp, None, "tensor"), P(dp, None), P(dp, "tensor"),
        P(None, "tensor"), P("tensor"), P(), P(), P("tensor"), P("tensor"), P("tensor"), P("tensor"), P(dp, "tensor"),
    )
    out_specs = (
        P(dp, None), P(dp, None), P(), P(dp, None, "tensor"), P(dp, None), P(dp, "tensor"),
        P(None, "tensor"), P("tensor"), P(), P(), P("tensor"), P("tensor"), P("tensor"), P("tensor"), P(dp, "tensor"),
    )
    return jax.shard_map(on_device, mesh=inner, in_specs=in_specs, out_specs=out_specs, check_vma=False)
```

time: 1070 us -> 846 us (0.79)
  the two profiles are of different devices: /device:TPU:1 before, /device:TPU:21 now
where the time goes in v2:
time: 846 us; the launch traced here: 835 us
  waiting for transfers between devices  342 us (40%)
  matrix products  168 us (20%)
  starting transfers between devices  121 us (14%)
  Pallas kernels  77.8 us (9%)
  other arithmetic  68.5 us (8%)
  local copies, waits for them, and re-layouts  42.9 us (5%)
  between operations  15.5 us (2%)
    ppermute x29, waiting for transfers between devices, swap(): return lax.ppermute(v, axis, [(i, i ^ mask) for i in range(count)])  95.5 us
    ppermute x9, waiting for transfers between devices, line_flood(): lax.ppermute(right[-1], 'tensor', [(i + 1, i) for i in range(0, count - j)])  89.2 us
    ppermute x9, waiting for transfers between devices, line_flood(): lax.ppermute(left[-1], 'tensor', [(i, i + 1) for i in range(j - 1, count...  79.9 us
    ppermute x6, waiting for transfers between devices, crossed(): return lax.ppermute(v, ('side', 'core', 'tensor'), pairs)  58.5 us
    pallas_call x1, Pallas kernels, mixer_backward(): pl.pallas_call(backward_kernel, grid_spec=pltpu.PrefetchScalarGridSpec(nu...  51.8 us
    ppermute x29, starting transfers between devices, swap(): return lax.ppermute(v, axis, [(i, i ^ mask) for i in range(count)])  47 us
    dot_general x13, matrix products, contract_columns(): lax.dot_general(a, b, (((1,), (1,)), ((), ())), preferred_element_type=F32)  44.1 us
    dot_general x4, matrix products, settled(): jnp.dot(where.astype(BF16), jnp.concatenate([held[j] for j in which]), pr...  37.6 us
  transfers between devices with their start and end apart: 56, of which 24 were waited for; matrix products, arithmetic and copies ran while one was open for 26% of the time, Pallas kernels for 3%

profile of v2, /device:TPU:21, one launch (start us, length us, event | category | flops | bytes accessed | tf_op | source)
XLA Modules:
  0.0 835.5 jit_solution(10979607991060158700)
XLA Ops:
  44.0 13.7 %collective-permute-done = bf16[256,1536]{1,0:T(8,128)(2,1)S(1)} collective-permute-done((bf16[256,1536]{1,0:T(8,128)(2,1)}, bf16[256,1536]{1,0:T(8,128)(2,1)S(1)}, u32[]{:S(2)}, u32[]{:S(2)}) %collective-permute-start) | collective-permute-done | bytes 786464 | tf_op jit(solution)/shard_map/ppermute | solution.py:362
  78.2 13.5 %collective-permute-done.7 = bf16[2,192,1152]{2,1,0:T(8,128)(2,1)} collective-permute-done((bf16[2,192,1152]{2,1,0:T(8,128)(2,1)}, bf16[2,192,1152]{2,1,0:T(8,128)(2,1)}, u32[]{:S(2)}, u32[]{:S(2)}) %collective-permute-start.7) | collective-permute-done | bytes 884768 | tf_op jit(solution)/shard_map/ppermute | solution.py:395
  101.9 11.2 %collective-permute-done.8 = bf16[2,192,1152]{2,1,0:T(8,128)(2,1)} collective-permute-done((bf16[2,192,1152]{2,1,0:T(8,128)(2,1)}, bf16[2,192,1152]{2,1,0:T(8,128)(2,1)}, u32[]{:S(2)}, u32[]{:S(2)}) %collective-permute-start.8) | collective-permute-done | bytes 884768 | tf_op jit(solution)/shard_map/ppermute | solution.py:395
  119.6 10.2 %collective-permute-done.3 = bf16[512,1536]{1,0:T(8,128)(2,1)} collective-permute-done((bf16[512,1536]{1,0:T(8,128)(2,1)}, bf16[512,1536]{1,0:T(8,128)(2,1)}, u32[]{:S(2)}, u32[]{:S(2)}) %collective-permute-start.3) | collective-permute-done | bytes 1572896 | tf_op jit(solution)/shard_map/ppermute | solution.py:362
  145.6 17.0 %fusion.134.proj_ref.proj_before_ref = f32[2048,1152]{1,0:T(8,128)} fusion(bf16[1536,1152]{1,0:T(8,128)(2,1)S(1)} %bitcast.88, bf16[512,1536]{1,0:T(8,128)(2,1)S(1)} %collective-permute-done.4, bf16[512,1536]{1,0:T(8,128)(2,1)} %collective-permute-done.3, bf16[512,1536]{1,0:T(8,128)(2,1)S(1)} %collective-permute-done.2, bf16[512,1536]{1,0:T(8,128)(2,1)} %fusion.21), kind=kOutput, calls=%fused_computation.270 | convolution fusion | flops 7272923136 | bytes 19267584 | tf_op jit(solution)/shard_map/dot_general | solution.py:501
  162.6 25.9 %mixer_forward.1 = (f32[2048,768]{1,0:T(8,128)}, bf16[16,128,768]{2,1,0:T(8,128)(2,1)}) custom-call(s32[4]{0:T(128)} %fusion.123.lens_ref, s32[16]{0:T(128)} %fusion.120.order_ref, f32[2048,1152]{1,0:T(8,128)} %fusion.134.proj_ref.proj_before_ref, f32[4,768]{1,0:T(4,128)} %slice.301.fw_ref, f32[1,768]{1,0:T(1,128)} %get-tuple-element.150.fb_ref, ...), custom_call_target="tpu_custom_call" | custom-call | flops 20000000000 | bytes 30000000 | tf_op jit(solution)/shard_map/mixer_forward/pallas_call | solution.py:292
  188.5 18.4 %all-gather.2.cloned.1.call-done = bf16[1536,1536]{1,0:T(8,128)(2,1)} async-done(((bf16[192,1536]{1,0:T(8,128)(2,1)}), bf16[1536,1536]{1,0:T(8,128)(2,1)}) %all-gather.2.cloned.1.call-update) | async-done | bytes 4718608 | tf_op jit(solution)/shard_map/all_gather | solution.py:462
  207.0 10.1 %fusion.76 = f32[2048,768]{1,0:T(8,128)S(1)} fusion(bf16[1536,1536]{1,0:T(8,128)(2,1)} %all-gather.2.cloned.1.call-done, bf16[512,1536]{1,0:T(8,128)(2,1)} %copy-done.44, bf16[512,1536]{1,0:T(8,128)(2,1)} %collective-permute-done.3, bf16[512,1536]{1,0:T(8,128)(2,1)S(1)} %copy-done.42, bf16[512,1536]{1,0:T(8,128)(2,1)} %fusion.21), kind=kOutput, calls=%fused_computation.125 | convolution fusion | flops 4857004032 | bytes 14942208 | tf_op jit(solution)/shard_map/dot_general | solution.py:504
  225.8 20.5 %fusion.66 = f32[2048,768]{1,0:T(8,128)} fusion(bf16[2048,1536]{1,0:T(8,128)(2,1)} %constant_dynamic-update-slice_fusion, bf16[1536,1536]{1,0:T(8,128)(2,1)} %all-gather.2.cloned.1.call-done), kind=kOutput, calls=%fused_computation.115 | convolution fusion | flops 4831838208 | bytes 14942208 | tf_op jit(solution)/shard_map/dot_general | solution.py:540
  256.7 13.9 %multiply_convert_fusion = (bf16[2048,768]{1,0:T(8,128)(2,1)S(1)}, f32[2048,768]{1,0:T(8,128)}, bf16[2048,768]{1,0:T(8,128)(2,1)}) fusion(f32[2048,768]{1,0:T(8,128)} %copy-done.1, f32[2048,768]{1,0:T(8,128)} %get-tuple-element.46.out_ref, f32[2048]{0:T(1024)S(1)} %fusion.108, f32[2048,768]{1,0:T(8,128)} %get-tuple-element.125, f32[2048,768]{1,0:T(8,128)} %fusion.66, ...), kind=kLoop, calls=%fused_computation.15 | loop fusion | flops 31457280 | bytes 37776384 | tf_op jit(solution)/shard_map/convert_element_type | solution.py:547
  270.7 51.8 %mixer_backward.1 = (bf16[2048,896]{1,0:T(8,128)(2,1)}, f32[2048,256]{1,0:T(8,128)}, f32[8,768]{1,0:T(8,128)}, f32[8,256]{1,0:T(8,128)}, f32[8,128]{1,0:T(8,128)}) custom-call(s32[4]{0:T(128)} %fusion.123.lens_ref, s32[16]{0:T(128)} %fusion.120.order_ref, f32[2048,1152]{1,0:T(8,128)} %fusion.134.proj_ref.proj_before_ref, ...), custom_call_target="tpu_custom_call" | custom-call | flops 40000000000 | bytes 60000000 | tf_op jit(solution)/shard_map/mixer_backward/pallas_call | solution.py:327
  391.5 26.4 %collective-permute-done.18 = bf16[512,1536]{1,0:T(8,128)(2,1)} collective-permute-done((bf16[512,1536]{1,0:T(8,128)(2,1)}, bf16[512,1536]{1,0:T(8,128)(2,1)}, u32[]{:S(2)}, u32[]{:S(2)}) %collective-permute-start.18) | collective-permute-done | bytes 1572896 | tf_op jit(solution)/shard_map/ppermute | solution.py:362
  425.1 32.1 %collective-permute-done.34 = bf16[512,1792]{1,0:T(8,128)(2,1)} collective-permute-done((bf16[512,1792]{1,0:T(8,128)(2,1)}, bf16[512,1792]{1,0:T(8,128)(2,1)}, u32[]{:S(2)}, u32[]{:S(2)}) %collective-permute-start.34) | collective-permute-done | bytes 1835040 | tf_op jit(solution)/shard_map/ppermute | solution.py:362
  473.9 21.2 %collective-permute-start.44 = (f32[12,768]{1,0:T(8,128)S(1)}, f32[12,768]{1,0:T(8,128)S(1)}, u32[]{:S(2)}, u32[]{:S(2)}) collective-permute-start(f32[12,768]{1,0:T(8,128)S(1)} %add.273), channel_id=1, source_target_pairs={{0,2},{1,3},{2,0},{3,1},{4,6},{5,7},{6,4},{7,5},{8,10},{9,11},{10,... | collective-permute-start | bytes 110600 | tf_op jit(solution)/shard_map/ppermute | solution.py:362
  520.6 27.4 %collective-permute-done.52 = f32[8,768]{1,0:T(8,128)S(1)} collective-permute-done((f32[8,768]{1,0:T(8,128)S(1)}, f32[8,768]{1,0:T(8,128)S(1)}, u32[]{:S(2)}, u32[]{:S(2)}) %collective-permute-start.52) | collective-permute-done | bytes 24608 | tf_op jit(solution)/shard_map/ppermute | solution.py:367
  565.4 14.4 %convolution_convert_fusion = bf16[1536,1152]{1,0:T(8,128)(2,1)} fusion(bf16[512,256]{1,0:T(8,128)(2,1)} %collective-permute-done.50, bf16[512,256]{1,0:T(8,128)(2,1)} %collective-permute-done.49, bf16[512,256]{1,0:T(8,128)(2,1)} %collective-permute-done.48, bf16[512,256]{1,0:T(8,128)(2,1)S(1)} %slice.425, bf16[2048,896]{1,0:T(8,128)(2,1)} %get-tuple-element.48, ...), kind=kOutput, calls=%fused_computation.2 | convolution fusion | flops 7298285568 | bytes 14548992 | tf_op jit(solution)/shard_map/dot_general | solution.py:410
  579.8 15.2 %collective-permute-done.38 = bf16[512,1536]{1,0:T(8,128)(2,1)} collective-permute-done((bf16[512,1536]{1,0:T(8,128)(2,1)}, bf16[512,1536]{1,0:T(8,128)(2,1)}, u32[]{:S(2)}, u32[]{:S(2)}) %collective-permute-start.38) | collective-permute-done | bytes 1572896 | tf_op jit(solution)/shard_map/ppermute | solution.py:396
  611.6 41.1 %collective-permute-done.23 = bf16[512,1536]{1,0:T(8,128)(2,1)} collective-permute-done((bf16[512,1536]{1,0:T(8,128)(2,1)S(1)}, bf16[512,1536]{1,0:T(8,128)(2,1)}, u32[]{:S(2)}, u32[]{:S(2)}) %collective-permute-start.23) | collective-permute-done | bytes 1572896 | tf_op jit(solution)/shard_map/ppermute | solution.py:396
  671.4 29.4 %collective-permute-done.39 = bf16[512,1536]{1,0:T(8,128)(2,1)S(1)} collective-permute-done((bf16[512,1536]{1,0:T(8,128)(2,1)}, bf16[512,1536]{1,0:T(8,128)(2,1)S(1)}, u32[]{:S(2)}, u32[]{:S(2)}) %collective-permute-start.39) | collective-permute-done | bytes 1572896 | tf_op jit(solution)/shard_map/ppermute | solution.py:396
  709.1 9.7 %convolution_convert_fusion.2 = bf16[2048,1536]{1,0:T(8,128)(2,1)} fusion(bf16[512,1536]{1,0:T(8,128)(2,1)S(1)} %broadcast_select_fusion.4, bf16[256,1536]{1,0:T(8,128)(2,1)} %collective-permute-done.35, bf16[256,1536]{1,0:T(8,128)(2,1)S(1)} %get-tuple-element.131, pred[2048,512]{1,0:T(32,128)(4,1)S(1)} %copy-done.19, pred[2048,512]{1,0:T(32,128)(4,1)S(1)} %copy-done.20), kind=kOutput, calls=%fused_computation.4 | convolution fusion | flops 6457131008 | bytes 11534336 | tf_op jit(solution)/shard_map/dot_general | solution.py:534
  720.4 18.1 %collective-permute-done.25 = bf16[512,1536]{1,0:T(8,128)(2,1)S(1)} collective-permute-done((bf16[512,1536]{1,0:T(8,128)(2,1)}, bf16[512,1536]{1,0:T(8,128)(2,1)S(1)}, u32[]{:S(2)}, u32[]{:S(2)}) %collective-permute-start.25) | collective-permute-done | bytes 1572896 | tf_op jit(solution)/shard_map/ppermute | solution.py:395
  748.9 23.2 %collective-permute-done.41 = bf16[512,1536]{1,0:T(8,128)(2,1)S(1)} collective-permute-done((bf16[512,1536]{1,0:T(8,128)(2,1)S(1)}, bf16[512,1536]{1,0:T(8,128)(2,1)S(1)}, u32[]{:S(2)}, u32[]{:S(2)}) %collective-permute-start.41) | collective-permute-done | bytes 1572896 | tf_op jit(solution)/shard_map/ppermute | solution.py:395
  781.6 11.2 %fusion.2 = bf16[2048,1536]{1,0:T(8,128)(2,1)} fusion(bf16[2048,1536]{1,0:T(8,128)(2,1)} %convolution_convert_fusion.2, bf16[512,1536]{1,0:T(8,128)(2,1)} %broadcast_select_fusion, bf16[512,1536]{1,0:T(8,128)(2,1)S(1)} %broadcast_select_fusion.2, pred[2048,512]{1,0:T(32,128)(4,1)} %get-tuple-element.166, pred[2048,512]{1,0:T(32,128)(4,1)} %get-tuple-element.167), kind=kOutput, calls=%fused_computation.23 | convolution fusion | flops 6457131008 | bytes 17825792 | tf_op jit(solution)/shard_map/dot_general | solution.py:534
  792.8 22.8 %collective-permute-done.47 = bf16[192,1536]{1,0:T(8,128)(2,1)S(1)} collective-permute-done((bf16[192,1536]{1,0:T(8,128)(2,1)}, bf16[192,1536]{1,0:T(8,128)(2,1)S(1)}, u32[]{:S(2)}, u32[]{:S(2)}) %collective-permute-start.47) | collective-permute-done | bytes 589856 | tf_op jit(solution)/shard_map/ppermute | solution.py:367
  (358 shorter events, 321.4 us)
Async XLA Ops:
  7.2 199.7 %all-gather.2.cloned.1.call-start = ((), (), s32[]{:S(2)}) async-start(), calls=%async_computation.2 | async-start | bytes 5308416 | tf_op jit(solution)/shard_map/all_gather | solution.py:462
  30.7 42.9 %collective-permute-start.1 = (f32[8,768]{1,0:T(8,128)S(1)}, f32[8,768]{1,0:T(8,128)S(1)}, u32[]{:S(2)}, u32[]{:S(2)}) collective-permute-start(f32[8,768]{1,0:T(8,128)S(1)} %concatenate.93), channel_id=1, source_target_pairs={{0,0},{1,4},{2,8},{3,12},{4,1},{5,5},{6,9},{7,13},{8,2},{9,6},{10,... | collective-permute-start | bytes 73736 | tf_op jit(solution)/shard_map/ppermute | solution.py:367
  42.1 89.8 %collective-permute-start.27 = (bf16[512,1536]{1,0:T(8,128)(2,1)}, bf16[512,1536]{1,0:T(8,128)(2,1)}, u32[]{:S(2)}, u32[]{:S(2)}) collective-permute-start(bf16[512,1536]{1,0:T(8,128)(2,1)} %pad_maximum_fusion.6), channel_id=1, source_target_pairs={{0,4},{4,0},{1,5},{5,1},{2,6},{6,2},{3,7},{7,3},{8,12},{12,8},{9,1... | collective-permute-start | bytes 4718600 | tf_op jit(solution)/shard_map/ppermute | solution.py:362
  57.7 74.2 %collective-permute-start.28 = (bf16[512,1536]{1,0:T(8,128)(2,1)}, bf16[512,1536]{1,0:T(8,128)(2,1)}, u32[]{:S(2)}, u32[]{:S(2)}) collective-permute-start(bf16[512,1536]{1,0:T(8,128)(2,1)} %pad_maximum_fusion.6), channel_id=1, source_target_pairs={{0,8},{8,0},{1,9},{9,1},{2,10},{10,2},{3,11},{11,3},{4,12},{12,4},... | collective-permute-start | bytes 4718600 | tf_op jit(solution)/shard_map/ppermute | solution.py:362
  73.6 56.2 %collective-permute-start.3 = (bf16[512,1536]{1,0:T(8,128)(2,1)}, bf16[512,1536]{1,0:T(8,128)(2,1)}, u32[]{:S(2)}, u32[]{:S(2)}) collective-permute-start(bf16[512,1536]{1,0:T(8,128)(2,1)} %fusion.21), channel_id=1, source_target_pairs={{0,8},{8,0},{1,9},{9,1},{2,10},{10,2},{3,11},{11,3},{4,12},{12,4},... | collective-permute-start | bytes 4718600 | tf_op jit(solution)/shard_map/ppermute | solution.py:362
  118.6 656.2 %reduce-scatter.7.cloned.1.call-start = ((), (), s32[]{:S(2)}) async-start(), calls=%async_computation.3 | async-start | bytes 5308416 | tf_op jit(solution)/shard_map/reduce_scatter | solution.py:550
  132.0 91.1 %collective-permute-start.29 = (bf16[512,1536]{1,0:T(8,128)(2,1)}, bf16[512,1536]{1,0:T(8,128)(2,1)S(1)}, u32[]{:S(2)}, u32[]{:S(2)}) collective-permute-start(bf16[512,1536]{1,0:T(8,128)(2,1)} %collective-permute-done.28), channel_id=1, source_target_pairs={{0,4},{4,0},{1,5},{5,1},{2,6},{6,2},{3,7},{7,3},{8,12},{12,8},{9,1... | collective-permute-start | bytes 4718600 | tf_op jit(solution)/shard_map/ppermute | solution.py:362
  354.4 422.4 %reduce-scatter.9.cloned.1.call-start = ((), (), s32[]{:S(2)}) async-start(), calls=%async_computation.4 | async-start | bytes 3981312 | tf_op jit(solution)/shard_map/reduce_scatter | solution.py:570
  362.1 63.1 %collective-permute-start.32 = (bf16[512,1792]{1,0:T(8,128)(2,1)}, bf16[512,1792]{1,0:T(8,128)(2,1)}, u32[]{:S(2)}, u32[]{:S(2)}) collective-permute-start(bf16[512,1792]{1,0:T(8,128)(2,1)} %pad_maximum_fusion.2), channel_id=1, source_target_pairs={{0,4},{4,0},{1,5},{5,1},{2,6},{6,2},{3,7},{7,3},{8,12},{12,8},{9,1... | collective-permute-start | bytes 5505032 | tf_op jit(solution)/shard_map/ppermute | solution.py:362
  386.2 71.0 %collective-permute-start.34 = (bf16[512,1792]{1,0:T(8,128)(2,1)}, bf16[512,1792]{1,0:T(8,128)(2,1)}, u32[]{:S(2)}, u32[]{:S(2)}) collective-permute-start(bf16[512,1792]{1,0:T(8,128)(2,1)} %fusion.17), channel_id=1, source_target_pairs={{0,8},{8,0},{1,9},{9,1},{2,10},{10,2},{3,11},{11,3},{4,12},{12,4},... | collective-permute-start | bytes 5505032 | tf_op jit(solution)/shard_map/ppermute | solution.py:362
  424.0 76.6 %collective-permute-start.19 = (bf16[256,1536]{1,0:T(8,128)(2,1)}, bf16[256,1536]{1,0:T(8,128)(2,1)}, u32[]{:S(2)}, u32[]{:S(2)}) collective-permute-start(bf16[256,1536]{1,0:T(8,128)(2,1)} %get-tuple-element.137), channel_id=1, source_target_pairs={{0,16},{16,0},{1,17},{17,1},{2,18},{18,2},{3,19},{19,3},{4,20},{20... | collective-permute-start | bytes 2359304 | tf_op jit(solution)/shard_map/ppermute | solution.py:362
  496.1 56.0 %collective-permute-start.35 = (bf16[256,1536]{1,0:T(8,128)(2,1)}, bf16[256,1536]{1,0:T(8,128)(2,1)}, u32[]{:S(2)}, u32[]{:S(2)}) collective-permute-start(bf16[256,1536]{1,0:T(8,128)(2,1)} %get-tuple-element.132), channel_id=1, source_target_pairs={{0,16},{16,0},{1,17},{17,1},{2,18},{18,2},{3,19},{19,3},{4,20},{20... | collective-permute-start | bytes 2359304 | tf_op jit(solution)/shard_map/ppermute | solution.py:362
  503.0 58.0 %collective-permute-start.22 = (bf16[512,1536]{1,0:T(8,128)(2,1)}, bf16[512,1536]{1,0:T(8,128)(2,1)S(1)}, u32[]{:S(2)}, u32[]{:S(2)}) collective-permute-start(bf16[512,1536]{1,0:T(8,128)(2,1)} %pad_maximum_fusion.5), channel_id=1, source_target_pairs={{1,0},{2,1},{3,2},{5,4},{6,5},{7,6},{9,8},{10,9},{11,10},{13,12},{... | collective-permute-start | bytes 4718600 | tf_op jit(solution)/shard_map/ppermute | solution.py:396
  508.0 55.4 %collective-permute-start.20 = (bf16[512,1536]{1,0:T(8,128)(2,1)}, bf16[512,1536]{1,0:T(8,128)(2,1)}, u32[]{:S(2)}, u32[]{:S(2)}) collective-permute-start(bf16[512,1536]{1,0:T(8,128)(2,1)} %pad_maximum_fusion.5), channel_id=1, source_target_pairs={{0,1},{1,2},{2,3},{4,5},{5,6},{6,7},{8,9},{9,10},{10,11},{12,13},{... | collective-permute-start | bytes 4718600 | tf_op jit(solution)/shard_map/ppermute | solution.py:395
  556.4 50.2 %collective-permute-start.36 = (bf16[512,1536]{1,0:T(8,128)(2,1)}, bf16[512,1536]{1,0:T(8,128)(2,1)}, u32[]{:S(2)}, u32[]{:S(2)}) collective-permute-start(bf16[512,1536]{1,0:T(8,128)(2,1)} %pad_maximum_fusion.7), channel_id=1, source_target_pairs={{0,1},{1,2},{2,3},{4,5},{5,6},{6,7},{8,9},{9,10},{10,11},{12,13},{... | collective-permute-start | bytes 4718600 | tf_op jit(solution)/shard_map/ppermute | solution.py:395
  561.0 91.8 %collective-permute-start.23 = (bf16[512,1536]{1,0:T(8,128)(2,1)S(1)}, bf16[512,1536]{1,0:T(8,128)(2,1)}, u32[]{:S(2)}, u32[]{:S(2)}) collective-permute-start(bf16[512,1536]{1,0:T(8,128)(2,1)S(1)} %collective-permute-done.22), channel_id=1, source_target_pairs={{1,0},{2,1},{5,4},{6,5},{9,8},{10,9},{13,12},{14,13},{17,16},{18,1... | collective-permute-start | bytes 4718600 | tf_op jit(solution)/shard_map/ppermute | solution.py:396
  563.4 93.3 %collective-permute-start.21 = (bf16[512,1536]{1,0:T(8,128)(2,1)}, bf16[512,1536]{1,0:T(8,128)(2,1)}, u32[]{:S(2)}, u32[]{:S(2)}) collective-permute-start(bf16[512,1536]{1,0:T(8,128)(2,1)} %collective-permute-done.20), channel_id=1, source_target_pairs={{1,2},{2,3},{5,6},{6,7},{9,10},{10,11},{13,14},{14,15},{17,18},{18... | collective-permute-start | bytes 4718600 | tf_op jit(solution)/shard_map/ppermute | solution.py:395
  595.1 105.7 %collective-permute-start.39 = (bf16[512,1536]{1,0:T(8,128)(2,1)}, bf16[512,1536]{1,0:T(8,128)(2,1)S(1)}, u32[]{:S(2)}, u32[]{:S(2)}) collective-permute-start(bf16[512,1536]{1,0:T(8,128)(2,1)} %collective-permute-done.38), channel_id=1, source_target_pairs={{1,0},{2,1},{5,4},{6,5},{9,8},{10,9},{13,12},{14,13},{17,16},{18,1... | collective-permute-start | bytes 4718600 | tf_op jit(solution)/shard_map/ppermute | solution.py:396
  606.6 98.2 %collective-permute-start.37 = (bf16[512,1536]{1,0:T(8,128)(2,1)}, bf16[512,1536]{1,0:T(8,128)(2,1)S(1)}, u32[]{:S(2)}, u32[]{:S(2)}) collective-permute-start(bf16[512,1536]{1,0:T(8,128)(2,1)} %collective-permute-done.36), channel_id=1, source_target_pairs={{1,2},{2,3},{5,6},{6,7},{9,10},{10,11},{13,14},{14,15},{17,18},{18... | collective-permute-start | bytes 4718600 | tf_op jit(solution)/shard_map/ppermute | solution.py:395
  652.8 66.0 %collective-permute-start.24 = (bf16[512,1536]{1,0:T(8,128)(2,1)}, bf16[512,1536]{1,0:T(8,128)(2,1)S(1)}, u32[]{:S(2)}, u32[]{:S(2)}) collective-permute-start(bf16[512,1536]{1,0:T(8,128)(2,1)} %collective-permute-done.23), channel_id=1, source_target_pairs={{1,0},{5,4},{9,8},{13,12},{17,16},{21,20},{25,24},{29,28}} | collective-permute-start | bytes 4718600 | tf_op jit(solution)/shard_map/ppermute | solution.py:396
  656.7 81.8 %collective-permute-start.25 = (bf16[512,1536]{1,0:T(8,128)(2,1)}, bf16[512,1536]{1,0:T(8,128)(2,1)S(1)}, u32[]{:S(2)}, u32[]{:S(2)}) collective-permute-start(bf16[512,1536]{1,0:T(8,128)(2,1)} %collective-permute-done.21), channel_id=1, source_target_pairs={{2,3},{6,7},{10,11},{14,15},{18,19},{22,23},{26,27},{30,31}} | collective-permute-start | bytes 4718600 | tf_op jit(solution)/shard_map/ppermute | solution.py:395
  700.8 46.5 %collective-permute-start.40 = (bf16[512,1536]{1,0:T(8,128)(2,1)S(1)}, bf16[512,1536]{1,0:T(8,128)(2,1)S(1)}, u32[]{:S(2)}, u32[]{:S(2)}) collective-permute-start(bf16[512,1536]{1,0:T(8,128)(2,1)S(1)} %collective-permute-done.39), channel_id=1, source_target_pairs={{1,0},{5,4},{9,8},{13,12},{17,16},{21,20},{25,24},{29,28}} | collective-permute-start | bytes 4718600 | tf_op jit(solution)/shard_map/ppermute | solution.py:396
  704.8 67.3 %collective-permute-start.41 = (bf16[512,1536]{1,0:T(8,128)(2,1)S(1)}, bf16[512,1536]{1,0:T(8,128)(2,1)S(1)}, u32[]{:S(2)}, u32[]{:S(2)}) collective-permute-start(bf16[512,1536]{1,0:T(8,128)(2,1)S(1)} %collective-permute-done.37), channel_id=1, source_target_pairs={{2,3},{6,7},{10,11},{14,15},{18,19},{22,23},{26,27},{30,31}} | collective-permute-start | bytes 4718600 | tf_op jit(solution)/shard_map/ppermute | solution.py:395
  776.8 48.2 %collective-permute-start.51 = (bf16[192,1152]{1,0:T(8,128)(2,1)}, bf16[192,1152]{1,0:T(8,128)(2,1)S(1)}, u32[]{:S(2)}, u32[]{:S(2)}) collective-permute-start(bf16[192,1152]{1,0:T(8,128)(2,1)} %reduce-scatter.9.cloned.1.call-done), channel_id=1, source_target_pairs={{0,0},{1,4},{2,8},{3,12},{4,1},{5,5},{6,9},{7,13},{8,2},{9,6},{10,... | collective-permute-start | bytes 1327112 | tf_op jit(solution)/shard_map/ppermute | solution.py:367
  (86 other events, 1612.3 us)
Sparse Core Ops, SparseCore 0:
  118.8 88.1 all-gather.1
  354.6 123.7 reduce-scatter.6
  579.9 98.9 reduce-scatter.8

commit v3 on v2

--- a/solution.py
+++ b/solution.py
@@ -371,15 +371,6 @@
     return lax.dynamic_index_in_dim(stack, index, axis, keepdims=False)
 
 
-def in_order(pieces, index):
-    if len(pieces) == 2:
-        first, second = pieces
-        even = index == 0
-        return jnp.stack([jnp.where(even, first, second), jnp.where(even, second, first)])
-    whole = jnp.stack(pieces)
-    return jnp.stack([pick(whole, index ^ i) for i in range(len(pieces))])
-
-
 def row_doubling(v):
     pieces = [v]
     while len(pieces) < lax.axis_size("row"):
@@ -388,13 +379,26 @@
     return pieces
 
 
-def line_flood(v):
-    count = lax.axis_size("tensor")
-    left, right = [v], [v]
-    for j in range(1, count):
-        left.append(lax.ppermute(left[-1], "tensor", [(i, i + 1) for i in range(j - 1, count - 1)]))
-        right.append(lax.ppermute(right[-1], "tensor", [(i + 1, i) for i in range(0, count - j)]))
-    return left[1:], right[1:]
+SLOT_PLANES = ((0, 1, 2, 3), (1, 0, 2, 3), (2, 1, 3, 0), (3, 2, 1, 0))
+PLANE_SLOTS = ((0, 1, 2, 3), (1, 0, 2, 3), (3, 1, 0, 2), (3, 2, 1, 0))
+
+
+def line_step(pair, j):
+    left, right = pair
+    return (
+        lax.ppermute(left, "tensor", [(i, i + 1) for i in range(j - 1, 3)]),
+        lax.ppermute(right, "tensor", [(i + 1, i) for i in range(0, 4 - j)]),
+    )
+
+
+def slots_of(v, one, two, three):
+    plane = lax.axis_index("tensor")
+    return [
+        v,
+        jnp.where(plane == 0, one[1], one[0]),
+        jnp.where(plane == 0, two[1], jnp.where(plane == 3, two[0], one[1])),
+        jnp.where(plane == 0, three[1], jnp.where(plane == 1, two[1], jnp.where(plane == 2, two[0], three[0]))),
+    ]
 
 
 def summed(v, axes):
@@ -453,11 +457,14 @@
 
     step_low = jnp.pad(step_weight.astype(BF16), ((0, 0), (0, LANES - heads)))
     piece = jnp.concatenate([inner_weight[:, 1].astype(BF16), step_low, shared_weight.astype(BF16)], axis=1)
-    blocks = in_order(row_doubling(crossed(piece)), row)
-    left, right = line_flood(blocks)
-    stack = jnp.stack(left[::-1] + [blocks] + right)
-    in_full = lax.dynamic_slice_in_dim(stack, planes - 1 - plane, planes, 0)
-    in_full = in_full.transpose(1, 0, 2, 3).reshape(model_width, -1)
+    own_piece = crossed(piece)
+    one = line_step((own_piece, own_piece), 1)
+    two = line_step(one, 2)
+    whole = jnp.stack([p for slot in slots_of(own_piece, one, two, line_step(two, 3)) for p in row_doubling(slot)])
+    slots = jnp.array(PLANE_SLOTS, jnp.int32)[plane]
+    in_full = jnp.concatenate(
+        [pick(whole, slots[q] * rows_n + (r ^ row)) for r in range(rows_n) for q in range(planes)], axis=0
+    )
     piece = jnp.concatenate([inner_weight[:, 0].astype(BF16), out_weight.astype(BF16)], axis=1)
     both_full = lax.all_gather(crossed(piece), ("row", "tensor"), axis=0, tiled=True)
     gate_full, out_full = both_full[:, :width], both_full[:, width:]
@@ -495,79 +502,99 @@
         unsequenced = lambda v: v.reshape(4 * rows_n, group_rows, -1)[fro].reshape(v.shape)
 
     def summed_over_group(v):
-        v = v + swap(v, "core").reshape(2, 2, owned)[:, ::-1].reshape(-1)
-        return v + swap(v, "side").reshape(2, 2 * owned)[::-1].reshape(-1)
+        v = v + swap(v, "core").reshape(2, 2, 2, owned)[:, :, ::-1].reshape(2, -1)
+        return v + swap(v, "side").reshape(2, 2, 2 * owned)[:, ::-1].reshape(2, -1)
+
+    def rows_of(v, dx, dk):
+        return v[(dx * 2 + dk) * owned : (dx * 2 + dk + 1) * owned]
+
+    def group_parts(part):
+        return part(1, 1).astype(BF16), part(1, 0), part(0, 1).astype(BF16), part(0, 0)
+
+    def group_sum(parts):
+        far, side_part, near, own_part = parts
+        beside = swap((side_part + swap(far, "core").astype(F32)).astype(BF16), "side")
+        return own_part + swap(near, "core").astype(F32) + beside.astype(F32)
+
+    block_of = destination // row_count
+    row_of, plane_of = (block_of // planes) ^ row, block_of % planes
+    slot = row_of * group_rows + destination - block_of * row_count - source * group_rows
+    slot_planes = jnp.array(SLOT_PLANES, jnp.int32)[plane]
+
+    def returned(held):
+        def settled(which):
+            where = jnp.concatenate([jnp.where(plane_of == slot_planes[j], slot, -1)[:, None] == jnp.arange(owned)[None, :]
+                                     for j in which], axis=1)
+            return jnp.dot(where.astype(BF16), jnp.concatenate([held[j] for j in which]), preferred_element_type=F32)
+        return settled((0, 1)).astype(BF16) + settled((2, 3)).astype(BF16)
 
     proj = sequenced(jnp.dot(normed, in_full, preferred_element_type=F32))
     mixed_seq, kept = mixer_forward(lens, order, proj, fw, fb, sf, sb, table, skip, spread)
     mixed = unsequenced(mixed_seq)
     gate_in = lax.optimization_barrier(jnp.dot(normed, gate_full, preferred_element_type=F32))
+    normed_grad = lax.optimization_barrier(jnp.dot(cot, out_full, preferred_element_type=F32))
     gate_sig = jax.nn.sigmoid(gate_in)
     gate_act = gate_in * gate_sig
     gated = mixed * gate_act
-    square_sum = summed_over_group(jnp.sum(gated * gated, axis=1))
-    gate_scale = lax.rsqrt(square_sum / (4 * width) + EPSILON)[:, None]
+    scaled_grad = normed_grad * gain
+    sums = summed_over_group(jnp.stack([jnp.sum(gated * gated, axis=1), jnp.sum(scaled_grad * gated, axis=1)]))
+    gate_scale = lax.rsqrt(sums[0] / (4 * width) + EPSILON)[:, None]
     gate_normed = (gated * gate_scale * gain).astype(BF16)
-
-    def rows_of(v, dx, dk):
-        return v[(dx * 2 + dk) * owned : (dx * 2 + dk + 1) * owned]
-
-    def summed_rows(part):
-        far = swap(part(1, 1).astype(BF16), "core")
-        beside = swap((part(1, 0) + far.astype(F32)).astype(BF16), "side")
-        near = swap(part(0, 1).astype(BF16), "core")
-        return part(0, 0) + near.astype(F32) + beside.astype(F32)
-
-    block_of = destination // row_count
-    row_of, plane_of = (block_of // planes) ^ row, block_of % planes
-    slot = row_of * group_rows + destination - block_of * row_count - source * group_rows
-    steps_down = (plane - plane_of) % planes
-
-    def returned(rows):
-        back = exchanged(rows)
-        left, right = line_flood(back)
-        held = [back] + [jnp.where(plane >= j, left[j - 1], right[planes - 1 - j]) for j in range(1, planes)]
-
-        def settled(which):
-            where = jnp.concatenate([jnp.where(steps_down == j, slot, -1)[:, None] == jnp.arange(owned)[None, :]
-                                     for j in which], axis=1)
-            return jnp.dot(where.astype(BF16), jnp.concatenate([held[j] for j in which]), preferred_element_type=F32)
-        return (settled((0, 2)).astype(BF16) + settled((1, 3)).astype(BF16))
-
-    branch = summed_rows(lambda dx, dk: contract_columns(rows_of(gate_normed, dx, dk), out_full))
-    layer_out = returned((hidden + branch).astype(BF16))
-
-    normed_grad = lax.optimization_barrier(jnp.dot(cot, out_full, preferred_element_type=F32))
+    far, side_part, near, own_part = group_parts(
+        lambda dx, dk: contract_columns(rows_of(gate_normed, dx, dk), out_full)
+    )
+    sent = (side_part + swap(far, "core").astype(F32)).astype(BF16)
+    own_rows = hidden + own_part + swap(near, "core").astype(F32)
+
     out_grad = contract_rows(cot, gate_normed).astype(BF16)
     gate_gain_grad = jnp.sum(normed_grad * gated * gate_scale, axis=0)
-    scaled_grad = normed_grad * gain
-    cross_sum = summed_over_group(jnp.sum(scaled_grad * gated, axis=1))
-    gated_grad = gate_scale * scaled_grad - gated * gate_scale**3 * (cross_sum / (4 * width))[:, None]
+    gated_grad = gate_scale * scaled_grad - gated * gate_scale**3 * (sums[1] / (4 * width))[:, None]
     mixed_grad = gated_grad * gate_act
     gate_in_grad = (gated_grad * mixed * gate_sig * (1.0 + gate_in * (1.0 - gate_sig))).astype(BF16)
     gate_grad = contract_rows(normed, gate_in_grad).astype(BF16)
     both_grad = jnp.concatenate([gate_grad, out_grad], axis=1)
+    mixed_grad, both_grad, sent, own_rows = lax.optimization_barrier((mixed_grad, both_grad, sent, own_rows))
+    arrived = swap(sent, "side")
     both_grad = lax.psum_scatter(both_grad, ("row", "tensor"), scatter_dimension=0, tiled=True)
-    both_grad = crossed(both_grad).astype(F32)
     proj_grad, shared_part, fsum, ssum, hsum = mixer_backward(
         lens, order, proj, sequenced(mixed_grad), mixed_seq, kept, fw, fb, sf, sb, table, skip, spread
     )
     proj_grad, shared_part = unsequenced(proj_grad), unsequenced(shared_part)
-    back = summed_rows(lambda dx, dk: jnp.concatenate([
-        contract_columns(rows_of(gate_in_grad, dx, dk), gate_full)
-        + contract_columns(rows_of(proj_grad, dx, dk), in_full[:, : width + LANES]),
-        rows_of(shared_part, dx, dk),
-    ], axis=1))
-    own_shared = back[:, model_width:].astype(BF16)
-    normed_back = back[:, :model_width] + contract_columns(own_shared, in_full[:, width + LANES :])
+    proj_grad, shared_part, arrived = lax.optimization_barrier((proj_grad, shared_part, arrived))
+    out_rows = exchanged((own_rows + arrived.astype(F32)).astype(BF16))
+
+    def back_part(grads, dx, dk):
+        gate_part, proj_part = grads
+        return contract_columns(rows_of(gate_part, dx, dk), gate_full) + contract_columns(
+            rows_of(proj_part, dx, dk), in_full[:, : width + LANES]
+        )
+
+    shared_far, shared_side, shared_near, shared_own = group_parts(lambda dx, dk: rows_of(shared_part, dx, dk))
+    own_shared = group_sum((shared_far, shared_side, shared_near, shared_own)).astype(BF16)
+    far = swap(back_part((gate_in_grad, proj_grad), 1, 1).astype(BF16), "core")
+    near = swap(back_part((gate_in_grad, proj_grad), 0, 1).astype(BF16), "core")
+    far, gate_later, proj_later, out_rows = lax.optimization_barrier((far, gate_in_grad, proj_grad, out_rows))
+    out_one = line_step((out_rows, out_rows), 1)
+    sent = (back_part((gate_later, proj_later), 1, 0) + far.astype(F32)).astype(BF16)
+    own_back = back_part((gate_later, proj_later), 0, 0) + near.astype(F32)
+    beside = swap(sent, "side")
+    in_grad = contract_rows(normed, jnp.concatenate([proj_later, gathered(own_shared)], axis=1)).astype(BF16)
+    in_grad, out_one, both_grad, own_back = lax.optimization_barrier((in_grad, out_one, both_grad, own_back))
+    out_two = line_step(out_one, 2)
+    both_grad = crossed(both_grad).astype(F32)
+    in_grad = lax.psum_scatter(in_grad, ("row", "tensor"), scatter_dimension=0, tiled=True)
+    normed_back = own_back + beside.astype(F32) + contract_columns(own_shared, in_full[:, width + LANES :])
     norm_gain_grad = jnp.sum(normed_back * hidden * scale, axis=0)
     gained = normed_back * norm_gain
     along = jnp.mean(gained * hidden, axis=1, keepdims=True)
     input_work = own_cot.astype(F32) + scale * gained - hidden * (scale**3 * along)
-    input_grad = returned(input_work.astype(BF16))
-
-    in_grad = contract_rows(normed, jnp.concatenate([proj_grad, gathered(own_shared)], axis=1)).astype(BF16)
-    in_grad = lax.psum_scatter(in_grad, ("row", "tensor"), scatter_dimension=0, tiled=True)
+    back_rows = exchanged(input_work.astype(BF16))
+    back_rows, out_two = lax.optimization_barrier((back_rows, out_two))
+    layer_out = returned(slots_of(out_rows, out_one, out_two, line_step(out_two, 3)))
+    back_one = line_step((back_rows, back_rows), 1)
+    back_two = line_step(back_one, 2)
+    back_two, in_grad = lax.optimization_barrier((back_two, in_grad))
+    input_grad = returned(slots_of(back_rows, back_one, back_two, line_step(back_two, 3)))
     in_grad = crossed(in_grad).astype(F32)
     inner_grad = jnp.stack([both_grad[:, :width], in_grad[:, :width]], axis=1)
 

time: 846 us -> 796 us (0.941)
  the two profiles are of different devices: /device:TPU:21 before, /device:TPU:1 now
where the time goes in v3:
time: 796 us; the launch traced here: 783 us
  waiting for transfers between devices  335 us (42%)
  matrix products  153 us (19%)
  starting transfers between devices  97.1 us (12%)
  Pallas kernels  77.3 us (10%)
  other arithmetic  57.6 us (7%)
  local copies, waits for them, and re-layouts  45.4 us (6%)
  between operations  18.1 us (2%)
    ppermute x9, waiting for transfers between devices, line_step(): lax.ppermute(right, 'tensor', [(i + 1, i) for i in range(0, 4 - j)])  120 us
    ppermute x33, waiting for transfers between devices, swap(): return lax.ppermute(v, axis, [(i, i ^ mask) for i in range(count)])  103 us
    ppermute x6, waiting for transfers between devices, crossed(): return lax.ppermute(v, ('side', 'core', 'tensor'), pairs)  85 us
    pallas_call x1, Pallas kernels, mixer_backward(): pl.pallas_call(backward_kernel, grid_spec=pltpu.PrefetchScalarGridSpec(nu...  51.5 us
    ppermute x33, starting transfers between devices, swap(): return lax.ppermute(v, axis, [(i, i ^ mask) for i in range(count)])  42.4 us
    dot_general x4, matrix products, settled(): jnp.dot(where.astype(BF16), jnp.concatenate([held[j] for j in which]), pr...  37 us
    dot_general x13, matrix products, contract_columns(): lax.dot_general(a, b, (((1,), (1,)), ((), ())), preferred_element_type=F32)  36.9 us
    dot_general x3, matrix products, contract_rows(): lax.dot_general(a, b, (((0,), (0,)), ((), ())), preferred_element_type=F32)  30.5 us
  transfers between devices with their start and end apart: 60, of which 21 were waited for; matrix products, arithmetic and copies ran while one was open for 22% of the time, Pallas kernels for 10%

profile of v3, /device:TPU:1, one launch (start us, length us, event | category | flops | bytes accessed | tf_op | source)
XLA Modules:
  0.0 783.1 jit_solution(14109165025190325581)
XLA Ops:
  48.8 9.2 %collective-permute-done.6 = bf16[192,1152]{1,0:T(8,128)(2,1)S(1)} collective-permute-done((bf16[192,1152]{1,0:T(8,128)(2,1)}, bf16[192,1152]{1,0:T(8,128)(2,1)S(1)}, u32[]{:S(2)}, u32[]{:S(2)}) %collective-permute-start.6) | collective-permute-done | bytes 442400 | tf_op jit(solution)/shard_map/ppermute | solution.py:362
  58.0 7.5 collective-permute-start.8
  79.5 7.1 collective-permute-done.9
  88.4 23.1 %collective-permute-done.10 = bf16[192,1152]{1,0:T(8,128)(2,1)S(1)} collective-permute-done((bf16[192,1152]{1,0:T(8,128)(2,1)}, bf16[192,1152]{1,0:T(8,128)(2,1)S(1)}, u32[]{:S(2)}, u32[]{:S(2)}) %collective-permute-start.10) | collective-permute-done | bytes 442400 | tf_op jit(solution)/shard_map/ppermute | solution.py:390
  114.4 7.4 collective-permute-start.18
  125.3 42.3 %collective-permute-done.13 = bf16[192,1152]{1,0:T(8,128)(2,1)S(1)} collective-permute-done((bf16[192,1152]{1,0:T(8,128)(2,1)S(1)}, bf16[192,1152]{1,0:T(8,128)(2,1)S(1)}, u32[]{:S(2)}, u32[]{:S(2)}) %collective-permute-start.13) | collective-permute-done | bytes 442400 | tf_op jit(solution)/shard_map/ppermute | solution.py:390
  186.4 17.2 %collective-permute-done.3 = bf16[512,1536]{1,0:T(8,128)(2,1)S(1)} collective-permute-done((bf16[512,1536]{1,0:T(8,128)(2,1)S(1)}, bf16[512,1536]{1,0:T(8,128)(2,1)S(1)}, u32[]{:S(2)}, u32[]{:S(2)}) %collective-permute-start.3) | collective-permute-done | bytes 1572896 | tf_op jit(solution)/shard_map/ppermute | solution.py:362
  212.1 15.1 %fusion.127.proj_ref.proj_before_ref = f32[2048,1152]{1,0:T(8,128)} fusion(bf16[1536,1152]{1,0:T(8,128)(2,1)S(1)} %bitcast_dynamic-update-slice_fusion, bf16[512,1536]{1,0:T(8,128)(2,1)S(1)} %collective-permute-done.4, bf16[512,1536]{1,0:T(8,128)(2,1)S(1)} %collective-permute-done.3, bf16[512,1536]{1,0:T(8,128)(2,1)S(1)} %collective-permute-done.2, ...), kind=kOutput, calls=%fused_computation.268 | convolution fusion | flops 7272923136 | bytes 19267584 | tf_op jit(solution)/shard_map/dot_general | solution.py:531
  227.2 25.8 %mixer_forward.1 = (f32[2048,768]{1,0:T(8,128)}, bf16[16,128,768]{2,1,0:T(8,128)(2,1)}) custom-call(s32[4]{0:T(128)} %fusion.115.lens_ref, s32[16]{0:T(128)} %fusion.112.order_ref, f32[2048,1152]{1,0:T(8,128)} %fusion.127.proj_ref.proj_before_ref, f32[4,768]{1,0:T(4,128)} %slice.348.fw_ref, f32[1,768]{1,0:T(1,128)} %get-tuple-element.186.fb_ref, ...), custom_call_target="tpu_custom_call" | custom-call | flops 20000000000 | bytes 30000000 | tf_op jit(solution)/shard_map/mixer_forward/pallas_call | solution.py:292
  253.0 8.0 %fusion.66 = f32[2048,768]{1,0:T(8,128)S(1)} fusion(bf16[2048,1536]{1,0:T(8,128)(2,1)} %copy-done.24, bf16[1536,1536]{1,0:T(8,128)(2,1)} %all-gather.2.cloned.1.call-done), kind=kOutput, calls=%fused_computation.111 | convolution fusion | flops 4831838208 | bytes 14942208 | tf_op jit(solution)/shard_map/dot_general | solution.py:535
  261.0 12.8 %fusion.72 = f32[2048,768]{1,0:T(8,128)S(1)} fusion(bf16[1536,1536]{1,0:T(8,128)(2,1)} %all-gather.2.cloned.1.call-done, bf16[512,1536]{1,0:T(8,128)(2,1)} %copy-done.51, bf16[512,1536]{1,0:T(8,128)(2,1)} %copy-done.47, bf16[512,1536]{1,0:T(8,128)(2,1)} %copy-done.49, bf16[512,1536]{1,0:T(8,128)(2,1)S(1)} %copy-done.12), kind=kOutput, calls=%fused_computation.117 | convolution fusion | flops 4857004032 | bytes 14942208 | tf_op jit(solution)/shard_map/dot_general | solution.py:534
  284.6 13.3 %multiply_convert_fusion.1 = (bf16[2048,768]{1,0:T(8,128)(2,1)S(1)}, f32[2048,768]{1,0:T(8,128)}, f32[768]{0:T(1024)S(1)}, bf16[2048,768]{1,0:T(8,128)(2,1)S(1)}) fusion(f32[2048,768]{1,0:T(8,128)} %copy-done.1, f32[2048,768]{1,0:T(8,128)} %get-tuple-element.68.out_ref, f32[2048]{0:T(1024)S(1)} %bitcast.99, f32[2048,768]{1,0:T(8,128)} %get-tuple-element.150, ...), kind=kLoop, calls=%fused_computation.16 | loop fusion | flops 36175104 | bytes 37779456 | tf_op jit(solution)/shard_map/convert_element_type | solution.py:553
  297.9 9.3 %convolution_convert_fusion.5 = bf16[1536,768]{0,1:T(8,128)(2,1)S(1)} fusion(bf16[2048,1536]{1,0:T(8,128)(2,1)} %copy-done.24, bf16[2048,768]{1,0:T(8,128)(2,1)S(1)} %get-tuple-element.160), kind=kOutput, calls=%fused_computation.42 | convolution fusion | flops 4833017856 | bytes 11796480 | tf_op jit(solution)/shard_map/dot_general | solution.py:414
  340.2 51.5 %mixer_backward.1 = (bf16[2048,896]{1,0:T(8,128)(2,1)}, f32[2048,256]{1,0:T(8,128)}, f32[8,768]{1,0:T(8,128)}, f32[8,256]{1,0:T(8,128)}, f32[8,128]{1,0:T(8,128)}) custom-call(s32[4]{0:T(128)} %fusion.115.lens_ref, s32[16]{0:T(128)} %fusion.112.order_ref, f32[2048,1152]{1,0:T(8,128)} %fusion.127.proj_ref.proj_before_ref, ...), custom_call_target="tpu_custom_call" | custom-call | flops 40000000000 | bytes 60000000 | tf_op jit(solution)/shard_map/mixer_backward/pallas_call | solution.py:327
  438.1 14.4 %convolution_convert_fusion.4 = bf16[1536,1152]{1,0:T(8,128)(2,1)} fusion(bf16[512,256]{1,0:T(8,128)(2,1)S(1)} %collective-permute-done.33, bf16[512,256]{1,0:T(8,128)(2,1)S(1)} %collective-permute-done.32, bf16[512,256]{1,0:T(8,128)(2,1)S(1)} %collective-permute-done.31, bf16[512,256]{1,0:T(8,128)(2,1)S(1)} %add_convert_fusion.1, ...), kind=kOutput, calls=%fused_computation.6 | convolution fusion | flops 7298285568 | bytes 14548992 | tf_op jit(solution)/shard_map/dot_general | solution.py:414
  452.5 9.4 %reduce-scatter.7.cloned.1.call-done = bf16[192,1536]{1,0:T(8,128)(2,1)} async-done(((bf16[1536,1536]{1,0:T(8,128)(2,1)}), bf16[192,1536]{1,0:T(8,128)(2,1)}) %reduce-scatter.7.cloned.1.call-update) | async-done | bytes 589840
  464.2 12.5 %collective-permute-done.34 = bf16[512,1536]{1,0:T(8,128)(2,1)} collective-permute-done((bf16[512,1536]{1,0:T(8,128)(2,1)}, bf16[512,1536]{1,0:T(8,128)(2,1)}, u32[]{:S(2)}, u32[]{:S(2)}) %collective-permute-start.34) | collective-permute-done | bytes 1572896 | tf_op jit(solution)/shard_map/ppermute | solution.py:389
  498.8 51.7 %collective-permute-done.50 = f32[12,768]{1,0:T(8,128)S(1)} collective-permute-done((f32[12,768]{1,0:T(8,128)S(1)}, f32[12,768]{1,0:T(8,128)S(1)}, u32[]{:S(2)}, u32[]{:S(2)}) %collective-permute-start.50) | collective-permute-done | bytes 36896 | tf_op jit(solution)/shard_map/ppermute | solution.py:362
  582.7 83.4 %collective-permute-done.54 = bf16[192,1536]{1,0:T(8,128)(2,1)S(1)} collective-permute-done((bf16[192,1536]{1,0:T(8,128)(2,1)S(1)}, bf16[192,1536]{1,0:T(8,128)(2,1)S(1)}, u32[]{:S(2)}, u32[]{:S(2)}) %collective-permute-start.54) | collective-permute-done | bytes 589856 | tf_op jit(solution)/shard_map/ppermute | solution.py:367
  675.9 9.9 %convolution_convert_fusion.3 = bf16[2048,1536]{1,0:T(8,128)(2,1)} fusion(bf16[512,1536]{1,0:T(8,128)(2,1)S(1)} %get-tuple-element.166, bf16[512,1536]{1,0:T(8,128)(2,1)} %pad_maximum_fusion.4, pred[2048,512]{1,0:T(32,128)(4,1)S(1)} %copy-done.17, pred[2048,512]{1,0:T(32,128)(4,1)S(1)} %copy-done.19), kind=kOutput, calls=%fused_computation.5 | convolution fusion | flops 6453985280 | bytes 11534336 | tf_op jit(solution)/shard_map/dot_general | solution.py:528
  687.1 29.2 %collective-permute-done.46 = bf16[512,1536]{1,0:T(8,128)(2,1)} collective-permute-done((bf16[512,1536]{1,0:T(8,128)(2,1)}, bf16[512,1536]{1,0:T(8,128)(2,1)}, u32[]{:S(2)}, u32[]{:S(2)}) %collective-permute-start.46) | collective-permute-done | bytes 1572896 | tf_op jit(solution)/shard_map/ppermute | solution.py:390
  721.8 11.7 %fusion.1 = bf16[2048,1536]{1,0:T(8,128)(2,1)} fusion(bf16[2048,1536]{1,0:T(8,128)(2,1)} %convolution_convert_fusion.3, bf16[512,1536]{1,0:T(8,128)(2,1)} %get-tuple-element.164, bf16[512,1536]{1,0:T(8,128)(2,1)} %get-tuple-element.163, pred[2048,512]{1,0:T(32,128)(4,1)} %iota_compare_fusion, pred[2048,512]{1,0:T(32,128)(4,1)} %iota_compare_fusion.1), kind=kOutput, calls=%fused_computation.22 | convolution fusion | flops 6457131008 | bytes 17825792 | tf_op jit(solution)/shard_map/dot_general | solution.py:528
  737.0 20.1 %collective-permute-done.47 = bf16[512,1536]{1,0:T(8,128)(2,1)} collective-permute-done((bf16[512,1536]{1,0:T(8,128)(2,1)}, bf16[512,1536]{1,0:T(8,128)(2,1)}, u32[]{:S(2)}, u32[]{:S(2)}) %collective-permute-start.47) | collective-permute-done | bytes 1572896 | tf_op jit(solution)/shard_map/ppermute | solution.py:390
  767.7 8.6 %fusion.2 = bf16[2048,1536]{1,0:T(8,128)(2,1)} fusion(bf16[2048,1536]{1,0:T(8,128)(2,1)S(1)} %convolution_convert_fusion, bf16[512,1536]{1,0:T(8,128)(2,1)S(1)} %get-tuple-element.165, bf16[512,1536]{1,0:T(8,128)(2,1)S(1)} %pad_maximum_fusion.5, pred[2048,512]{1,0:T(32,128)(4,1)S(1)} %copy-done.18, pred[2048,512]{1,0:T(32,128)(4,1)S(1)} %copy-done.20), kind=kOutput, calls=%fused_computation.23 | convolution fusion | flops 6457131008 | bytes 17825792 | tf_op jit(solution)/shard_map/dot_general | solution.py:528
  (388 shorter events, 264.6 us)
Async XLA Ops:
  7.2 245.8 %all-gather.2.cloned.1.call-start = ((), (), s32[]{:S(2)}) async-start(), calls=%async_computation.2 | async-start | bytes 5308416 | tf_op jit(solution)/shard_map/all_gather | solution.py:469
  14.9 99.3 %collective-permute-start.17 = (bf16[256,1536]{1,0:T(8,128)(2,1)}, bf16[256,1536]{1,0:T(8,128)(2,1)S(1)}, u32[]{:S(2)}, u32[]{:S(2)}) collective-permute-start(bf16[256,1536]{1,0:T(8,128)(2,1)} %get-tuple-element.173), channel_id=1, source_target_pairs={{0,16},{16,0},{1,17},{17,1},{2,18},{18,2},{3,19},{19,3},{4,20},{20... | collective-permute-start | bytes 2359304 | tf_op jit(solution)/shard_map/ppermute | solution.py:362
  18.1 59.4 %collective-permute-start.16 = (bf16[192,1536]{1,0:T(8,128)(2,1)}, bf16[192,1536]{1,0:T(8,128)(2,1)}, u32[]{:S(2)}, u32[]{:S(2)}) collective-permute-start(bf16[192,1536]{1,0:T(8,128)(2,1)} %pad_maximum_fusion.7), channel_id=1, source_target_pairs={{0,0},{1,4},{2,8},{3,12},{4,1},{5,5},{6,9},{7,13},{8,2},{9,6},{10,... | collective-permute-start | bytes 1769480 | tf_op jit(solution)/shard_map/ppermute | solution.py:367
  32.3 89.5 %collective-permute-start.1 = (bf16[256,1536]{1,0:T(8,128)(2,1)}, bf16[256,1536]{1,0:T(8,128)(2,1)S(1)}, u32[]{:S(2)}, u32[]{:S(2)}) collective-permute-start(bf16[256,1536]{1,0:T(8,128)(2,1)} %get-tuple-element.175), channel_id=1, source_target_pairs={{0,16},{16,0},{1,17},{17,1},{2,18},{18,2},{3,19},{19,3},{4,20},{20... | collective-permute-start | bytes 2359304 | tf_op jit(solution)/shard_map/ppermute | solution.py:362
  77.5 384.5 %reduce-scatter.7.cloned.1.call-start = ((), (), s32[]{:S(2)}) async-start(), calls=%async_computation.3 | async-start | bytes 5308416
  114.4 95.9 %collective-permute-start.18 = (bf16[512,1536]{1,0:T(8,128)(2,1)S(1)}, bf16[512,1536]{1,0:T(8,128)(2,1)S(1)}, u32[]{:S(2)}, u32[]{:S(2)}) collective-permute-start(bf16[512,1536]{1,0:T(8,128)(2,1)S(1)} %pad_maximum_fusion.3), channel_id=1, source_target_pairs={{0,4},{4,0},{1,5},{5,1},{2,6},{6,2},{3,7},{7,3},{8,12},{12,8},{9,1... | collective-permute-start | bytes 4718600 | tf_op jit(solution)/shard_map/ppermute | solution.py:362
  121.8 61.5 %collective-permute-start.19 = (bf16[512,1536]{1,0:T(8,128)(2,1)S(1)}, bf16[512,1536]{1,0:T(8,128)(2,1)S(1)}, u32[]{:S(2)}, u32[]{:S(2)}) collective-permute-start(bf16[512,1536]{1,0:T(8,128)(2,1)S(1)} %pad_maximum_fusion.3), channel_id=1, source_target_pairs={{0,8},{8,0},{1,9},{9,1},{2,10},{10,2},{3,11},{11,3},{4,12},{12,4},... | collective-permute-start | bytes 4718600 | tf_op jit(solution)/shard_map/ppermute | solution.py:362
  122.2 45.4 %collective-permute-start.13 = (bf16[192,1152]{1,0:T(8,128)(2,1)S(1)}, bf16[192,1152]{1,0:T(8,128)(2,1)S(1)}, u32[]{:S(2)}, u32[]{:S(2)}) collective-permute-start(bf16[192,1152]{1,0:T(8,128)(2,1)S(1)} %collective-permute-done.10), channel_id=1, source_target_pairs={{1,0},{5,4},{9,8},{13,12},{17,16},{21,20},{25,24},{29,28}} | collective-permute-start | bytes 1327112 | tf_op jit(solution)/shard_map/ppermute | solution.py:390
  123.7 44.0 %collective-permute-start.14 = (bf16[192,1152]{1,0:T(8,128)(2,1)S(1)}, bf16[192,1152]{1,0:T(8,128)(2,1)S(1)}, u32[]{:S(2)}, u32[]{:S(2)}) collective-permute-start(bf16[192,1152]{1,0:T(8,128)(2,1)S(1)} %collective-permute-done.11), channel_id=1, source_target_pairs={{2,3},{6,7},{10,11},{14,15},{18,19},{22,23},{26,27},{30,31}} | collective-permute-start | bytes 1327112 | tf_op jit(solution)/shard_map/ppermute | solution.py:389
  332.4 61.8 %collective-permute-start.25 = (bf16[512,1536]{1,0:T(8,128)(2,1)}, bf16[512,1536]{1,0:T(8,128)(2,1)}, u32[]{:S(2)}, u32[]{:S(2)}) collective-permute-start(bf16[512,1536]{1,0:T(8,128)(2,1)} %fusion.46), channel_id=1, source_target_pairs={{0,8},{8,0},{1,9},{9,1},{2,10},{10,2},{3,11},{11,3},{4,12},{12,4},... | collective-permute-start | bytes 4718600 | tf_op jit(solution)/shard_map/ppermute | solution.py:362
  340.2 345.6 %reduce-scatter.9.cloned.1.call-start = ((), (), s32[]{:S(2)}) async-start(), calls=%async_computation.4 | async-start | bytes 3981312
  423.4 53.2 %collective-permute-start.34 = (bf16[512,1536]{1,0:T(8,128)(2,1)}, bf16[512,1536]{1,0:T(8,128)(2,1)}, u32[]{:S(2)}, u32[]{:S(2)}) collective-permute-start(bf16[512,1536]{1,0:T(8,128)(2,1)} %pad_maximum_fusion.4), channel_id=1, source_target_pairs={{0,1},{1,2},{2,3},{4,5},{5,6},{6,7},{8,9},{9,10},{10,11},{12,13},{... | collective-permute-start | bytes 4718600 | tf_op jit(solution)/shard_map/ppermute | solution.py:389
  426.0 53.4 %collective-permute-start.35 = (bf16[512,1536]{1,0:T(8,128)(2,1)}, bf16[512,1536]{1,0:T(8,128)(2,1)}, u32[]{:S(2)}, u32[]{:S(2)}) collective-permute-start(bf16[512,1536]{1,0:T(8,128)(2,1)} %pad_maximum_fusion.4), channel_id=1, source_target_pairs={{1,0},{2,1},{3,2},{5,4},{6,5},{7,6},{9,8},{10,9},{11,10},{13,12},{... | collective-permute-start | bytes 4718600 | tf_op jit(solution)/shard_map/ppermute | solution.py:390
  434.0 48.6 %collective-permute-start.37 = (bf16[512,1536]{1,0:T(8,128)(2,1)}, bf16[512,1536]{1,0:T(8,128)(2,1)}, u32[]{:S(2)}, u32[]{:S(2)}) collective-permute-start(bf16[512,1536]{1,0:T(8,128)(2,1)} %fusion.47), channel_id=1, source_target_pairs={{0,8},{8,0},{1,9},{9,1},{2,10},{10,2},{3,11},{11,3},{4,12},{12,4},... | collective-permute-start | bytes 4718600 | tf_op jit(solution)/shard_map/ppermute | solution.py:362
  479.4 82.4 %collective-permute-start.39 = (bf16[512,1536]{1,0:T(8,128)(2,1)}, bf16[512,1536]{1,0:T(8,128)(2,1)}, u32[]{:S(2)}, u32[]{:S(2)}) collective-permute-start(bf16[512,1536]{1,0:T(8,128)(2,1)} %collective-permute-done.34), channel_id=1, source_target_pairs={{1,2},{2,3},{5,6},{6,7},{9,10},{10,11},{13,14},{14,15},{17,18},{18... | collective-permute-start | bytes 4718600 | tf_op jit(solution)/shard_map/ppermute | solution.py:389
  481.2 80.6 %collective-permute-start.40 = (bf16[512,1536]{1,0:T(8,128)(2,1)}, bf16[512,1536]{1,0:T(8,128)(2,1)}, u32[]{:S(2)}, u32[]{:S(2)}) collective-permute-start(bf16[512,1536]{1,0:T(8,128)(2,1)} %collective-permute-done.35), channel_id=1, source_target_pairs={{1,0},{2,1},{5,4},{6,5},{9,8},{10,9},{13,12},{14,13},{17,16},{18,1... | collective-permute-start | bytes 4718600 | tf_op jit(solution)/shard_map/ppermute | solution.py:390
  494.0 56.4 %collective-permute-start.50 = (f32[12,768]{1,0:T(8,128)S(1)}, f32[12,768]{1,0:T(8,128)S(1)}, u32[]{:S(2)}, u32[]{:S(2)}) collective-permute-start(f32[12,768]{1,0:T(8,128)S(1)} %add.315), channel_id=1, source_target_pairs={{0,1},{1,0},{2,3},{3,2},{4,5},{5,4},{6,7},{7,6},{8,9},{9,8},{10,11... | collective-permute-start | bytes 110600 | tf_op jit(solution)/shard_map/ppermute | solution.py:362
  498.4 63.2 %collective-permute-start.38 = (bf16[256,1536]{1,0:T(8,128)(2,1)S(1)}, bf16[256,1536]{1,0:T(8,128)(2,1)S(1)}, u32[]{:S(2)}, u32[]{:S(2)}) collective-permute-start(bf16[256,1536]{1,0:T(8,128)(2,1)S(1)} %get-tuple-element.168), channel_id=1, source_target_pairs={{0,16},{16,0},{1,17},{17,1},{2,18},{18,2},{3,19},{19,3},{4,20},{20... | collective-permute-start | bytes 2359304 | tf_op jit(solution)/shard_map/ppermute | solution.py:362
  561.8 105.3 %collective-permute-start.44 = (bf16[512,1536]{1,0:T(8,128)(2,1)S(1)}, bf16[512,1536]{1,0:T(8,128)(2,1)}, u32[]{:S(2)}, u32[]{:S(2)}) collective-permute-start(bf16[512,1536]{1,0:T(8,128)(2,1)S(1)} %pad_maximum_fusion.5), channel_id=1, source_target_pairs={{0,1},{1,2},{2,3},{4,5},{5,6},{6,7},{8,9},{9,10},{10,11},{12,13},{... | collective-permute-start | bytes 4718600 | tf_op jit(solution)/shard_map/ppermute | solution.py:389
  564.3 104.8 %collective-permute-start.43 = (bf16[512,1536]{1,0:T(8,128)(2,1)S(1)}, bf16[512,1536]{1,0:T(8,128)(2,1)}, u32[]{:S(2)}, u32[]{:S(2)}) collective-permute-start(bf16[512,1536]{1,0:T(8,128)(2,1)S(1)} %pad_maximum_fusion.5), channel_id=1, source_target_pairs={{1,0},{2,1},{3,2},{5,4},{6,5},{7,6},{9,8},{10,9},{11,10},{13,12},{... | collective-permute-start | bytes 4718600 | tf_op jit(solution)/shard_map/ppermute | solution.py:390
  565.6 104.8 %collective-permute-start.41 = (bf16[512,1536]{1,0:T(8,128)(2,1)}, bf16[512,1536]{1,0:T(8,128)(2,1)}, u32[]{:S(2)}, u32[]{:S(2)}) collective-permute-start(bf16[512,1536]{1,0:T(8,128)(2,1)} %collective-permute-done.40), channel_id=1, source_target_pairs={{1,0},{5,4},{9,8},{13,12},{17,16},{21,20},{25,24},{29,28}} | collective-permute-start | bytes 4718600 | tf_op jit(solution)/shard_map/ppermute | solution.py:390
  566.9 103.5 %collective-permute-start.42 = (bf16[512,1536]{1,0:T(8,128)(2,1)}, bf16[512,1536]{1,0:T(8,128)(2,1)}, u32[]{:S(2)}, u32[]{:S(2)}) collective-permute-start(bf16[512,1536]{1,0:T(8,128)(2,1)} %collective-permute-done.39), channel_id=1, source_target_pairs={{2,3},{6,7},{10,11},{14,15},{18,19},{22,23},{26,27},{30,31}} | collective-permute-start | bytes 4718600 | tf_op jit(solution)/shard_map/ppermute | solution.py:389
  570.6 95.5 %collective-permute-start.54 = (bf16[192,1536]{1,0:T(8,128)(2,1)S(1)}, bf16[192,1536]{1,0:T(8,128)(2,1)S(1)}, u32[]{:S(2)}, u32[]{:S(2)}) collective-permute-start(bf16[192,1536]{1,0:T(8,128)(2,1)S(1)} %copy.50), channel_id=1, source_target_pairs={{0,0},{1,4},{2,8},{3,12},{4,1},{5,5},{6,9},{7,13},{8,2},{9,6},{10,... | collective-permute-start | bytes 1769480 | tf_op jit(solution)/shard_map/ppermute | solution.py:367
  669.1 47.1 %collective-permute-start.46 = (bf16[512,1536]{1,0:T(8,128)(2,1)}, bf16[512,1536]{1,0:T(8,128)(2,1)}, u32[]{:S(2)}, u32[]{:S(2)}) collective-permute-start(bf16[512,1536]{1,0:T(8,128)(2,1)} %collective-permute-done.43), channel_id=1, source_target_pairs={{1,0},{2,1},{5,4},{6,5},{9,8},{10,9},{13,12},{14,13},{17,16},{18,1... | collective-permute-start | bytes 4718600 | tf_op jit(solution)/shard_map/ppermute | solution.py:390
  (98 other events, 1776.1 us)
Sparse Core Ops, SparseCore 0:
  77.6 109.0 all-gather.1
  340.3 121.6 reduce-scatter.6
  482.7 108.8 reduce-scatter.8

commit v4 on v3

--- a/solution.py
+++ b/solution.py
@@ -367,10 +367,6 @@
     return lax.ppermute(v, ("side", "core", "tensor"), pairs)
 
 
-def pick(stack, index, axis=0):
-    return lax.dynamic_index_in_dim(stack, index, axis, keepdims=False)
-
-
 def row_doubling(v):
     pieces = [v]
     while len(pieces) < lax.axis_size("row"):
@@ -380,7 +376,10 @@
 
 
 SLOT_PLANES = ((0, 1, 2, 3), (1, 0, 2, 3), (2, 1, 3, 0), (3, 2, 1, 0))
-PLANE_SLOTS = ((0, 1, 2, 3), (1, 0, 2, 3), (3, 1, 0, 2), (3, 2, 1, 0))
+
+
+def tie(*values):
+    return lax.optimization_barrier(values)
 
 
 def line_step(pair, j):
@@ -391,14 +390,24 @@
     )
 
 
+def slot_one(one):
+    return jnp.where(lax.axis_index("tensor") == 0, one[1], one[0])
+
+
+def slot_two(one, two):
+    plane = lax.axis_index("tensor")
+    return jnp.where(plane == 0, two[1], jnp.where(plane == 3, two[0], one[1]))
+
+
+def slot_three(two, three):
+    plane = lax.axis_index("tensor")
+    return jnp.where(
+        plane == 0, three[1], jnp.where(plane == 1, two[1], jnp.where(plane == 2, two[0], three[0]))
+    )
+
+
 def slots_of(v, one, two, three):
-    plane = lax.axis_index("tensor")
-    return [
-        v,
-        jnp.where(plane == 0, one[1], one[0]),
-        jnp.where(plane == 0, two[1], jnp.where(plane == 3, two[0], one[1])),
-        jnp.where(plane == 0, three[1], jnp.where(plane == 1, two[1], jnp.where(plane == 2, two[0], three[0]))),
-    ]
+    return [v, slot_one(one), slot_two(one, two), slot_three(two, three)]
 
 
 def summed(v, axes):
@@ -448,26 +457,46 @@
         beside = swap(own, "side")
         return jnp.concatenate([own, swap(own, "core"), beside, swap(beside, "core")])
 
-    own_tokens = exchanged(jnp.dot(chosen, tokens, preferred_element_type=F32).astype(BF16))
+    slot_planes = jnp.array(SLOT_PLANES, jnp.int32)[plane]
+
+    def assembled(doubled):
+        rows, columns = doubled[0][0].shape
+        whole = jnp.zeros((planes * rows_n * rows, columns), BF16)
+        for i, pieces in enumerate(doubled):
+            for d, p in enumerate(pieces):
+                whole = lax.dynamic_update_slice(whole, p, (((row ^ d) * planes + slot_planes[i]) * rows, 0))
+        return whole
+
+    picked = jnp.dot(chosen, tokens, preferred_element_type=F32).astype(BF16)
+    step_low = jnp.pad(step_weight.astype(BF16), ((0, 0), (0, LANES - heads)))
+    piece = jnp.concatenate([inner_weight[:, 1].astype(BF16), step_low, shared_weight.astype(BF16)], axis=1)
+    gate_piece = jnp.concatenate([inner_weight[:, 0].astype(BF16), out_weight.astype(BF16)], axis=1)
+    own_tokens, piece, gate_piece = tie(exchanged(picked), crossed(piece), gate_piece)
+    one = line_step((piece, piece), 1)
+    in_slots = [row_doubling(piece)]
+    gate_piece = crossed(gate_piece)
     hidden = own_tokens.astype(F32)
     scale = lax.rsqrt(jnp.mean(hidden * hidden, axis=-1, keepdims=True) + EPSILON)
-    normed = gathered((hidden * scale * norm_gain).astype(BF16))
-    own_cot = exchanged(jnp.dot(chosen, cotangent, preferred_element_type=F32).astype(BF16))
-    cot = gathered(own_cot)
-
-    step_low = jnp.pad(step_weight.astype(BF16), ((0, 0), (0, LANES - heads)))
-    piece = jnp.concatenate([inner_weight[:, 1].astype(BF16), step_low, shared_weight.astype(BF16)], axis=1)
-    own_piece = crossed(piece)
-    one = line_step((own_piece, own_piece), 1)
+    own_normed = (hidden * scale * norm_gain).astype(BF16)
+    beside, near = swap(own_normed, "side"), swap(own_normed, "core")
+    picked_cot = jnp.dot(chosen, cotangent, preferred_element_type=F32).astype(BF16)
+    one, in_slots, near = tie(one, in_slots, near)
     two = line_step(one, 2)
-    whole = jnp.stack([p for slot in slots_of(own_piece, one, two, line_step(two, 3)) for p in row_doubling(slot)])
-    slots = jnp.array(PLANE_SLOTS, jnp.int32)[plane]
-    in_full = jnp.concatenate(
-        [pick(whole, slots[q] * rows_n + (r ^ row)) for r in range(rows_n) for q in range(planes)], axis=0
-    )
-    piece = jnp.concatenate([inner_weight[:, 0].astype(BF16), out_weight.astype(BF16)], axis=1)
-    both_full = lax.all_gather(crossed(piece), ("row", "tensor"), axis=0, tiled=True)
-    gate_full, out_full = both_full[:, :width], both_full[:, width:]
+    in_slots = in_slots + [row_doubling(slot_one(one))]
+    two, in_slots, gate_piece, picked_cot = tie(two, in_slots, gate_piece, picked_cot)
+    three = line_step(two, 3)
+    in_slots = in_slots + [row_doubling(slot_two(one, two))]
+    three, in_slots, beside = tie(three, in_slots, beside)
+    in_slots = in_slots + [row_doubling(slot_three(two, three))]
+    far = swap(beside, "core")
+    one = line_step((gate_piece, gate_piece), 1)
+    own_cot = exchanged(picked_cot)
+    in_slots, far, one, own_cot = tie(in_slots, far, one, own_cot)
+    two = line_step(one, 2)
+    gate_slots = [row_doubling(gate_piece), row_doubling(slot_one(one))]
+    cot_beside, cot_near = swap(own_cot, "side"), swap(own_cot, "core")
+    normed = jnp.concatenate([own_normed, near, beside, far])
+    in_full = assembled(in_slots)
 
     params = jnp.concatenate(
         [
@@ -519,7 +548,6 @@
     block_of = destination // row_count
     row_of, plane_of = (block_of // planes) ^ row, block_of % planes
     slot = row_of * group_rows + destination - block_of * row_count - source * group_rows
-    slot_planes = jnp.array(SLOT_PLANES, jnp.int32)[plane]
 
     def returned(held):
         def settled(which):
@@ -528,8 +556,16 @@
             return jnp.dot(where.astype(BF16), jnp.concatenate([held[j] for j in which]), preferred_element_type=F32)
         return settled((0, 1)).astype(BF16) + settled((2, 3)).astype(BF16)
 
-    proj = sequenced(jnp.dot(normed, in_full, preferred_element_type=F32))
+    proj = jnp.dot(normed, in_full, preferred_element_type=F32)
+    proj, two, gate_slots, cot_near = tie(proj, two, gate_slots, cot_near)
+    three = line_step(two, 3)
+    gate_slots = gate_slots + [row_doubling(slot_two(one, two))]
+    proj = sequenced(proj)
     mixed_seq, kept = mixer_forward(lens, order, proj, fw, fb, sf, sb, table, skip, spread)
+    mixed_seq, three, gate_slots, cot_beside = tie(mixed_seq, three, gate_slots, cot_beside)
+    both_full = assembled(gate_slots + [row_doubling(slot_three(two, three))])
+    gate_full, out_full = both_full[:, :width], both_full[:, width:]
+    cot = jnp.concatenate([own_cot, cot_near, cot_beside, swap(cot_beside, "core")])
     mixed = unsequenced(mixed_seq)
     gate_in = lax.optimization_barrier(jnp.dot(normed, gate_full, preferred_element_type=F32))
     normed_grad = lax.optimization_barrier(jnp.dot(cot, out_full, preferred_element_type=F32))
@@ -588,16 +624,6 @@
     gained = normed_back * norm_gain
     along = jnp.mean(gained * hidden, axis=1, keepdims=True)
     input_work = own_cot.astype(F32) + scale * gained - hidden * (scale**3 * along)
-    back_rows = exchanged(input_work.astype(BF16))
-    back_rows, out_two = lax.optimization_barrier((back_rows, out_two))
-    layer_out = returned(slots_of(out_rows, out_one, out_two, line_step(out_two, 3)))
-    back_one = line_step((back_rows, back_rows), 1)
-    back_two = line_step(back_one, 2)
-    back_two, in_grad = lax.optimization_barrier((back_two, in_grad))
-    input_grad = returned(slots_of(back_rows, back_one, back_two, line_step(back_two, 3)))
-    in_grad = crossed(in_grad).astype(F32)
-    inner_grad = jnp.stack([both_grad[:, :width], in_grad[:, :width]], axis=1)
-
     line = lambda v: jnp.pad(v, (0, -v.shape[0] % width)).reshape(-1, width)
     skip_grad = fsum[5].reshape(heads, -1).sum(axis=1)
     small = jnp.concatenate(
@@ -611,9 +637,25 @@
         ],
         axis=0,
     )
-    small = summed(small, ("row", "tensor"))
-    mine = crossed(small[:8])
-    common = summed(small[8:], ("core", "side"))
+    small = summed(small, ("row",))
+    small = jnp.concatenate([small[:8], summed(small[8:], ("core", "side"))], axis=0)
+    back_rows = exchanged(input_work.astype(BF16))
+    back_rows, out_two, small = tie(back_rows, out_two, small)
+    small_added = swap(small, "tensor", 1)
+    out_three = line_step(out_two, 3)
+    back_one = line_step((back_rows, back_rows), 1)
+    back_one, out_three, small_added = tie(back_one, out_three, small_added)
+    small = small + small_added
+    small_added = swap(small, "tensor", 2)
+    back_two = line_step(back_one, 2)
+    layer_out = returned(slots_of(out_rows, out_one, out_two, out_three))
+    back_two, in_grad, small_added = tie(back_two, in_grad, small_added)
+    small = small + small_added
+    mine, common = crossed(small[:8]), small[8:]
+    input_grad = returned(slots_of(back_rows, back_one, back_two, line_step(back_two, 3)))
+    in_grad = crossed(in_grad).astype(F32)
+    inner_grad = jnp.stack([both_grad[:, :width], in_grad[:, :width]], axis=1)
+
     lines = line(norm_gain_grad).shape[0]
     norm_gain_grad = common[:lines].reshape(-1)[:model_width]
     shared_sums = common[lines:].reshape(-1)[: 5 * sf.shape[1]].reshape(5, -1)

time: 796 us -> 771 us (0.969)
  waiting for transfers between devices: 335 us -> 304 us
  starting transfers between devices: 97.1 us -> 114 us
    ppermute x9 -> x12, waiting for transfers between devices: 120 us -> 70.4 us  [line_step(): lax.ppermute(right, 'tensor', [(i + 1, i) for i in range(0, 4 - j)])]
    ppermute x6, waiting for transfers between devices: 85 us -> 132 us  [crossed(): return lax.ppermute(v, ('side', 'core', 'tensor'), pairs)]
    ppermute x33 -> x37, waiting for transfers between devices: 103 us -> 79.6 us  [swap(): return lax.ppermute(v, axis, [(i, i ^ mask) for i in range(count)])]
    ppermute x9 -> x12, starting transfers between devices: 21.9 us -> 33.1 us  [line_step(): lax.ppermute(left, 'tensor', [(i, i + 1) for i in range(j - 1, 3)])]
    unnamed x144 -> x137, local copies, waits for them, and re-layouts: 24.7 us -> 17.2 us
    ppermute x9 -> x12, starting transfers between devices: 12.1 us -> 16.4 us  [line_step(): lax.ppermute(right, 'tensor', [(i + 1, i) for i in range(0, 4 - j)])]
    ppermute x33 -> x37, starting transfers between devices: 42.4 us -> 38.2 us  [swap(): return lax.ppermute(v, axis, [(i, i ^ mask) for i in range(count)])]
    ppermute x9 -> x12, waiting for transfers between devices: 17.9 us -> 15.9 us  [line_step(): lax.ppermute(left, 'tensor', [(i, i + 1) for i in range(j - 1, 3)])]
  transfers between devices with their start and end apart: 60 -> 69, of which waited for: 21 -> 28; matrix products, arithmetic and copies ran while one was open for 22% -> 22% of each run, Pallas kernels for 10% -> 10%
where the time goes in v4:
time: 771 us; the launch traced here: 763 us
  waiting for transfers between devices  304 us (39%)
  matrix products  149 us (19%)
  starting transfers between devices  114 us (15%)
  Pallas kernels  77.7 us (10%)
  other arithmetic  56.9 us (7%)
  local copies, waits for them, and re-layouts  40.1 us (5%)
  between operations  21.5 us (3%)
    ppermute x6, waiting for transfers between devices, crossed(): return lax.ppermute(v, ('side', 'core', 'tensor'), pairs)  132 us
    ppermute x37, waiting for transfers between devices, swap(): return lax.ppermute(v, axis, [(i, i ^ mask) for i in range(count)])  79.6 us
    ppermute x12, waiting for transfers between devices, line_step(): lax.ppermute(right, 'tensor', [(i + 1, i) for i in range(0, 4 - j)])  70.4 us
    pallas_call x1, Pallas kernels, mixer_backward(): pl.pallas_call(backward_kernel, grid_spec=pltpu.PrefetchScalarGridSpec(nu...  51.9 us
    ppermute x37, starting transfers between devices, swap(): return lax.ppermute(v, axis, [(i, i ^ mask) for i in range(count)])  38.2 us
    dot_general x4, matrix products, settled(): jnp.dot(where.astype(BF16), jnp.concatenate([held[j] for j in which]), pr...  37.1 us
    ppermute x12, starting transfers between devices, line_step(): lax.ppermute(left, 'tensor', [(i, i + 1) for i in range(j - 1, 3)])  33.1 us
    dot_general x3, matrix products, contract_rows(): lax.dot_general(a, b, (((0,), (0,)), ((), ())), preferred_element_type=F32)  29.9 us
  transfers between devices with their start and end apart: 69, of which 28 were waited for; matrix products, arithmetic and copies ran while one was open for 22% of the time, Pallas kernels for 10%

profile of v4, /device:TPU:1, one launch (start us, length us, event | category | flops | bytes accessed | tf_op | source)
XLA Modules:
  0.0 762.8 jit_solution(1716546722847318468)
XLA Ops:
  22.2 11.0 %collective-permute-done.1 = bf16[256,1536]{1,0:T(8,128)(2,1)} collective-permute-done((bf16[256,1536]{1,0:T(8,128)(2,1)S(1)}, bf16[256,1536]{1,0:T(8,128)(2,1)}, u32[]{:S(2)}, u32[]{:S(2)}) %collective-permute-start.1) | collective-permute-done | bytes 786464 | tf_op jit(solution)/shard_map/ppermute | solution.py:362
  44.2 7.4 fusion.43
  68.2 16.4 %collective-permute-done.10 = bf16[192,1536]{1,0:T(8,128)(2,1)} collective-permute-done((bf16[192,1536]{1,0:T(8,128)(2,1)S(1)}, bf16[192,1536]{1,0:T(8,128)(2,1)}, u32[]{:S(2)}, u32[]{:S(2)}) %collective-permute-start.10) | collective-permute-done | bytes 589856 | tf_op jit(solution)/shard_map/ppermute | solution.py:367
  104.5 9.1 %collective-permute-done.12 = bf16[192,1152]{1,0:T(8,128)(2,1)} collective-permute-done((bf16[192,1152]{1,0:T(8,128)(2,1)S(1)}, bf16[192,1152]{1,0:T(8,128)(2,1)}, u32[]{:S(2)}, u32[]{:S(2)}) %collective-permute-start.12) | collective-permute-done | bytes 442400 | tf_op jit(solution)/shard_map/ppermute | solution.py:389
  127.5 9.0 %collective-permute-done.19 = bf16[256,1536]{1,0:T(8,128)(2,1)} collective-permute-done((bf16[256,1536]{1,0:T(8,128)(2,1)}, bf16[256,1536]{1,0:T(8,128)(2,1)}, u32[]{:S(2)}, u32[]{:S(2)}) %collective-permute-start.19) | collective-permute-done | bytes 786464 | tf_op jit(solution)/shard_map/ppermute | solution.py:362
  153.3 16.4 %fusion.127.proj_ref.proj_before_ref = f32[2048,1152]{1,0:T(8,128)} fusion(bf16[1536,1152]{1,0:T(8,128)(2,1)S(1)} %constant_dynamic-update-slice_fusion.12, bf16[512,1536]{1,0:T(8,128)(2,1)} %collective-permute-done.16, bf16[512,1536]{1,0:T(8,128)(2,1)} %collective-permute-done.14, bf16[512,1536]{1,0:T(8,128)(2,1)} %collective-permute-done.6, ...), kind=kOutput, calls=%fused_computation.270 | convolution fusion | flops 7272923136 | bytes 19267584 | tf_op jit(solution)/shard_map/dot_general | solution.py:559
  176.7 25.8 %mixer_forward.1 = (f32[2048,768]{1,0:T(8,128)}, bf16[16,128,768]{2,1,0:T(8,128)(2,1)}) custom-call(s32[4]{0:T(128)} %fusion.115.lens_ref, s32[16]{0:T(128)} %fusion.112.order_ref, f32[2048,1152]{1,0:T(8,128)} %fusion.127.proj_ref.proj_before_ref, f32[4,768]{1,0:T(4,128)} %slice.348.fw_ref, f32[1,768]{1,0:T(1,128)} %get-tuple-element.305.fb_ref, ...), custom_call_target="tpu_custom_call" | custom-call | flops 20000000000 | bytes 30000000 | tf_op jit(solution)/shard_map/mixer_forward/pallas_call | solution.py:292
  225.6 11.4 %fusion.72 = f32[2048,768]{1,0:T(8,128)S(1)} fusion(bf16[1536,1536]{1,0:T(8,128)(2,1)S(1)} %constant_dynamic-update-slice_fusion.4, bf16[512,1536]{1,0:T(8,128)(2,1)} %collective-permute-done.16, bf16[512,1536]{1,0:T(8,128)(2,1)} %collective-permute-done.14, bf16[512,1536]{1,0:T(8,128)(2,1)} %collective-permute-done.6, bf16[512,1536]{1,0:T(8,128)(2,1)} %fusion.21), kind=kOutput, calls=%fused_computation.117 | convolution fusion | flops 4857004032 | bytes 14942208 | tf_op jit(solution)/shard_map/dot_general | solution.py:570
  238.3 10.5 %fusion.66 = f32[2048,768]{1,0:T(8,128)S(1)} fusion(bf16[2048,1536]{1,0:T(8,128)(2,1)} %constant_dynamic-update-slice_fusion, bf16[1536,1536]{1,0:T(8,128)(2,1)} %copy-done.4), kind=kOutput, calls=%fused_computation.111 | convolution fusion | flops 4831838208 | bytes 14942208 | tf_op jit(solution)/shard_map/dot_general | solution.py:571
  259.6 13.7 %multiply_convert_fusion.1 = (bf16[2048,768]{1,0:T(8,128)(2,1)S(1)}, f32[2048,768]{1,0:T(8,128)}, f32[768]{0:T(1024)S(1)}, bf16[2048,768]{1,0:T(8,128)(2,1)S(1)}) fusion(f32[2048,768]{1,0:T(8,128)} %copy-done, f32[2048,768]{1,0:T(8,128)} %get-tuple-element.175.out_ref, f32[2048]{0:T(1024)S(1)} %bitcast.61, f32[2048,768]{1,0:T(8,128)} %get-tuple-element.274, ...), kind=kLoop, calls=%fused_computation.16 | loop fusion | flops 36175104 | bytes 37779456 | tf_op jit(solution)/shard_map/convert_element_type | solution.py:589
  276.1 8.1 %convolution_convert_fusion.5 = bf16[1536,768]{0,1:T(8,128)(2,1)S(1)} fusion(bf16[2048,1536]{1,0:T(8,128)(2,1)} %constant_dynamic-update-slice_fusion, bf16[2048,768]{1,0:T(8,128)(2,1)S(1)} %get-tuple-element.280), kind=kOutput, calls=%fused_computation.42 | convolution fusion | flops 4833017856 | bytes 11796480 | tf_op jit(solution)/shard_map/dot_general | solution.py:423
  309.8 51.9 %mixer_backward.1 = (bf16[2048,896]{1,0:T(8,128)(2,1)}, f32[2048,256]{1,0:T(8,128)}, f32[8,768]{1,0:T(8,128)}, f32[8,256]{1,0:T(8,128)}, f32[8,128]{1,0:T(8,128)}) custom-call(s32[4]{0:T(128)} %fusion.115.lens_ref, s32[16]{0:T(128)} %fusion.112.order_ref, f32[2048,1152]{1,0:T(8,128)} %fusion.127.proj_ref.proj_before_ref, ...), custom_call_target="tpu_custom_call" | custom-call | flops 40000000000 | bytes 60000000 | tf_op jit(solution)/shard_map/mixer_backward/pallas_call | solution.py:327
  391.2 8.3 %collective-permute-start.44 = (bf16[512,1536]{1,0:T(8,128)(2,1)}, bf16[512,1536]{1,0:T(8,128)(2,1)}, u32[]{:S(2)}, u32[]{:S(2)}) collective-permute-start(bf16[512,1536]{1,0:T(8,128)(2,1)} %pad_maximum_fusion.4), channel_id=1, source_target_pairs={{0,1},{1,2},{2,3},{4,5},{5,6},{6,7},{8,9},{9,10},{10,11},{12,13},{... | collective-permute-start | bytes 4718600 | tf_op jit(solution)/shard_map/ppermute | solution.py:388
  410.4 14.4 %convolution_convert_fusion.4 = bf16[1536,1152]{1,0:T(8,128)(2,1)} fusion(bf16[512,256]{1,0:T(8,128)(2,1)S(1)} %collective-permute-done.43, bf16[512,256]{1,0:T(8,128)(2,1)S(1)} %collective-permute-done.42, bf16[512,256]{1,0:T(8,128)(2,1)S(1)} %collective-permute-done.41, bf16[512,256]{1,0:T(8,128)(2,1)S(1)} %add_convert_fusion.1, ...), kind=kOutput, calls=%fused_computation.6 | convolution fusion | flops 7298285568 | bytes 14548992 | tf_op jit(solution)/shard_map/dot_general | solution.py:423
  432.5 15.9 %collective-permute-done.44 = bf16[512,1536]{1,0:T(8,128)(2,1)} collective-permute-done((bf16[512,1536]{1,0:T(8,128)(2,1)}, bf16[512,1536]{1,0:T(8,128)(2,1)}, u32[]{:S(2)}, u32[]{:S(2)}) %collective-permute-start.44) | collective-permute-done | bytes 1572896 | tf_op jit(solution)/shard_map/ppermute | solution.py:388
  461.1 22.3 %collective-permute-done.51 = f32[12,768]{1,0:T(8,128)S(1)} collective-permute-done((f32[12,768]{1,0:T(8,128)S(1)}, f32[12,768]{1,0:T(8,128)S(1)}, u32[]{:S(2)}, u32[]{:S(2)}) %collective-permute-start.51) | collective-permute-done | bytes 36896 | tf_op jit(solution)/shard_map/ppermute | solution.py:362
  489.8 30.9 %collective-permute-done.50 = bf16[512,1536]{1,0:T(8,128)(2,1)} collective-permute-done((bf16[512,1536]{1,0:T(8,128)(2,1)}, bf16[512,1536]{1,0:T(8,128)(2,1)}, u32[]{:S(2)}, u32[]{:S(2)}) %collective-permute-start.50) | collective-permute-done | bytes 1572896 | tf_op jit(solution)/shard_map/ppermute | solution.py:389
  543.1 86.9 %collective-permute-done.64 = bf16[192,1536]{1,0:T(8,128)(2,1)S(1)} collective-permute-done((bf16[192,1536]{1,0:T(8,128)(2,1)S(1)}, bf16[192,1536]{1,0:T(8,128)(2,1)S(1)}, u32[]{:S(2)}, u32[]{:S(2)}) %collective-permute-start.64) | collective-permute-done | bytes 589856 | tf_op jit(solution)/shard_map/ppermute | solution.py:367
  641.3 8.5 %convolution_convert_fusion.2 = bf16[2048,1536]{1,0:T(8,128)(2,1)} fusion(bf16[512,1536]{1,0:T(8,128)(2,1)S(1)} %get-tuple-element.284, bf16[512,1536]{1,0:T(8,128)(2,1)S(1)} %get-tuple-element.283, pred[2048,512]{1,0:T(32,128)(4,1)S(1)} %get-tuple-element.323, pred[2048,512]{1,0:T(32,128)(4,1)S(1)} %get-tuple-element.324), kind=kOutput, calls=%fused_computation.4 | convolution fusion | flops 6453985280 | bytes 11534336 | tf_op jit(solution)/shard_map/dot_general | solution.py:556
  651.1 24.9 %collective-permute-done.60 = bf16[512,1536]{1,0:T(8,128)(2,1)} collective-permute-done((bf16[512,1536]{1,0:T(8,128)(2,1)}, bf16[512,1536]{1,0:T(8,128)(2,1)}, u32[]{:S(2)}, u32[]{:S(2)}) %collective-permute-start.60) | collective-permute-done | bytes 1572896 | tf_op jit(solution)/shard_map/ppermute | solution.py:389
  679.4 11.5 %fusion.1 = bf16[2048,1536]{1,0:T(8,128)(2,1)} fusion(bf16[2048,1536]{1,0:T(8,128)(2,1)} %convolution_convert_fusion.2, bf16[512,1536]{1,0:T(8,128)(2,1)} %get-tuple-element.286, bf16[512,1536]{1,0:T(8,128)(2,1)} %pad_maximum_fusion.4, pred[2048,512]{1,0:T(32,128)(4,1)S(1)} %get-tuple-element.325, pred[2048,512]{1,0:T(32,128)(4,1)} %get-tuple-element.326), kind=kOutput, calls=%fused_computation.22 | convolution fusion | flops 6457131008 | bytes 17825792 | tf_op jit(solution)/shard_map/dot_general | solution.py:556
  700.7 28.5 %collective-permute-done.66 = f32[8,768]{1,0:T(8,128)S(1)} collective-permute-done((f32[8,768]{1,0:T(8,128)S(1)}, f32[8,768]{1,0:T(8,128)S(1)}, u32[]{:S(2)}, u32[]{:S(2)}) %collective-permute-start.66) | collective-permute-done | bytes 24608 | tf_op jit(solution)/shard_map/ppermute | solution.py:367
  738.5 8.4 %convolution_convert_fusion.1 = bf16[2048,1536]{1,0:T(8,128)(2,1)S(1)} fusion(bf16[512,1536]{1,0:T(8,128)(2,1)S(1)} %get-tuple-element.285, bf16[512,1536]{1,0:T(8,128)(2,1)} %pad_maximum_fusion.5, pred[2048,512]{1,0:T(32,128)(4,1)S(1)} %copy-done.20, pred[2048,512]{1,0:T(32,128)(4,1)S(1)} %copy-done.21), kind=kOutput, calls=%fused_computation.3 | convolution fusion | flops 6453985280 | bytes 11534336 | tf_op jit(solution)/shard_map/dot_general | solution.py:556
  746.9 8.6 %fusion.2 = bf16[2048,1536]{1,0:T(8,128)(2,1)} fusion(bf16[2048,1536]{1,0:T(8,128)(2,1)S(1)} %convolution_convert_fusion.1, bf16[512,1536]{1,0:T(8,128)(2,1)S(1)} %get-tuple-element.282, bf16[512,1536]{1,0:T(8,128)(2,1)S(1)} %get-tuple-element.281, pred[2048,512]{1,0:T(32,128)(4,1)S(1)} %copy-done.23, pred[2048,512]{1,0:T(32,128)(4,1)S(1)} %copy-done.25), kind=kOutput, calls=%fused_computation.23 | convolution fusion | flops 6457131008 | bytes 17825792 | tf_op jit(solution)/shard_map/dot_general | solution.py:556
  (415 shorter events, 281.5 us)
Async XLA Ops:
  7.2 424.0 %reduce-scatter.7.cloned.1.call-start = ((), (), s32[]{:S(2)}) async-start(), calls=%async_computation.2 | async-start | bytes 5308416
  51.6 52.9 %collective-permute-start.14 = (bf16[512,1536]{1,0:T(8,128)(2,1)}, bf16[512,1536]{1,0:T(8,128)(2,1)}, u32[]{:S(2)}, u32[]{:S(2)}) collective-permute-start(bf16[512,1536]{1,0:T(8,128)(2,1)} %fusion.21), channel_id=1, source_target_pairs={{0,8},{8,0},{1,9},{9,1},{2,10},{10,2},{3,11},{11,3},{4,12},{12,4},... | collective-permute-start | bytes 4718600 | tf_op jit(solution)/shard_map/ppermute | solution.py:362
  113.7 32.1 %collective-permute-start.16 = (bf16[512,1536]{1,0:T(8,128)(2,1)}, bf16[512,1536]{1,0:T(8,128)(2,1)}, u32[]{:S(2)}, u32[]{:S(2)}) collective-permute-start(bf16[512,1536]{1,0:T(8,128)(2,1)} %collective-permute-done.14), channel_id=1, source_target_pairs={{0,4},{4,0},{1,5},{5,1},{2,6},{6,2},{3,7},{7,3},{8,12},{12,8},{9,1... | collective-permute-start | bytes 4718600 | tf_op jit(solution)/shard_map/ppermute | solution.py:362
  136.4 33.3 %collective-permute-start.22 = (bf16[192,1536]{1,0:T(8,128)(2,1)}, bf16[192,1536]{1,0:T(8,128)(2,1)S(1)}, u32[]{:S(2)}, u32[]{:S(2)}) collective-permute-start(bf16[192,1536]{1,0:T(8,128)(2,1)} %collective-permute-done.10), channel_id=1, source_target_pairs={{0,16},{16,0},{1,17},{17,1},{2,18},{18,2},{3,19},{19,3},{4,20},{20... | collective-permute-start | bytes 1769480 | tf_op jit(solution)/shard_map/ppermute | solution.py:362
  169.8 36.1 %collective-permute-start.28 = (bf16[512,1536]{1,0:T(8,128)(2,1)S(1)}, bf16[512,1536]{1,0:T(8,128)(2,1)}, u32[]{:S(2)}, u32[]{:S(2)}) collective-permute-start(bf16[512,1536]{1,0:T(8,128)(2,1)S(1)} %pad_maximum_fusion.3), channel_id=1, source_target_pairs={{0,8},{8,0},{1,9},{9,1},{2,10},{10,2},{3,11},{11,3},{4,12},{12,4},... | collective-permute-start | bytes 4718600 | tf_op jit(solution)/shard_map/ppermute | solution.py:362
  171.1 34.8 %collective-permute-start.25 = (bf16[192,1536]{1,0:T(8,128)(2,1)}, bf16[192,1536]{1,0:T(8,128)(2,1)}, u32[]{:S(2)}, u32[]{:S(2)}) collective-permute-start(bf16[192,1536]{1,0:T(8,128)(2,1)} %collective-permute-done.20), channel_id=1, source_target_pairs={{2,3},{6,7},{10,11},{14,15},{18,19},{22,23},{26,27},{30,31}} | collective-permute-start | bytes 1769480 | tf_op jit(solution)/shard_map/ppermute | solution.py:388
  174.6 31.2 %collective-permute-start.26 = (bf16[192,1536]{1,0:T(8,128)(2,1)}, bf16[192,1536]{1,0:T(8,128)(2,1)}, u32[]{:S(2)}, u32[]{:S(2)}) collective-permute-start(bf16[192,1536]{1,0:T(8,128)(2,1)} %collective-permute-done.21), channel_id=1, source_target_pairs={{1,0},{5,4},{9,8},{13,12},{17,16},{21,20},{25,24},{29,28}} | collective-permute-start | bytes 1769480 | tf_op jit(solution)/shard_map/ppermute | solution.py:389
  302.8 59.7 %collective-permute-start.35 = (bf16[512,1536]{1,0:T(8,128)(2,1)}, bf16[512,1536]{1,0:T(8,128)(2,1)S(1)}, u32[]{:S(2)}, u32[]{:S(2)}) collective-permute-start(bf16[512,1536]{1,0:T(8,128)(2,1)} %fusion.46), channel_id=1, source_target_pairs={{0,8},{8,0},{1,9},{9,1},{2,10},{10,2},{3,11},{11,3},{4,12},{12,4},... | collective-permute-start | bytes 4718600 | tf_op jit(solution)/shard_map/ppermute | solution.py:362
  309.8 340.0 %reduce-scatter.9.cloned.1.call-start = ((), (), s32[]{:S(2)}) async-start(), calls=%async_computation.3 | async-start | bytes 3981312
  391.2 57.2 %collective-permute-start.44 = (bf16[512,1536]{1,0:T(8,128)(2,1)}, bf16[512,1536]{1,0:T(8,128)(2,1)}, u32[]{:S(2)}, u32[]{:S(2)}) collective-permute-start(bf16[512,1536]{1,0:T(8,128)(2,1)} %pad_maximum_fusion.4), channel_id=1, source_target_pairs={{0,1},{1,2},{2,3},{4,5},{5,6},{6,7},{8,9},{9,10},{10,11},{12,13},{... | collective-permute-start | bytes 4718600 | tf_op jit(solution)/shard_map/ppermute | solution.py:388
  399.4 51.1 %collective-permute-start.45 = (bf16[512,1536]{1,0:T(8,128)(2,1)}, bf16[512,1536]{1,0:T(8,128)(2,1)}, u32[]{:S(2)}, u32[]{:S(2)}) collective-permute-start(bf16[512,1536]{1,0:T(8,128)(2,1)} %pad_maximum_fusion.4), channel_id=1, source_target_pairs={{1,0},{2,1},{3,2},{5,4},{6,5},{7,6},{9,8},{10,9},{11,10},{13,12},{... | collective-permute-start | bytes 4718600 | tf_op jit(solution)/shard_map/ppermute | solution.py:389
  407.2 46.5 %collective-permute-start.47 = (bf16[512,1536]{1,0:T(8,128)(2,1)}, bf16[512,1536]{1,0:T(8,128)(2,1)}, u32[]{:S(2)}, u32[]{:S(2)}) collective-permute-start(bf16[512,1536]{1,0:T(8,128)(2,1)} %fusion.47), channel_id=1, source_target_pairs={{0,8},{8,0},{1,9},{9,1},{2,10},{10,2},{3,11},{11,3},{4,12},{12,4},... | collective-permute-start | bytes 4718600 | tf_op jit(solution)/shard_map/ppermute | solution.py:362
  450.6 39.2 %collective-permute-start.49 = (bf16[512,1536]{1,0:T(8,128)(2,1)}, bf16[512,1536]{1,0:T(8,128)(2,1)}, u32[]{:S(2)}, u32[]{:S(2)}) collective-permute-start(bf16[512,1536]{1,0:T(8,128)(2,1)} %collective-permute-done.44), channel_id=1, source_target_pairs={{1,2},{2,3},{5,6},{6,7},{9,10},{10,11},{13,14},{14,15},{17,18},{18... | collective-permute-start | bytes 4718600 | tf_op jit(solution)/shard_map/ppermute | solution.py:388
  452.4 68.3 %collective-permute-start.50 = (bf16[512,1536]{1,0:T(8,128)(2,1)}, bf16[512,1536]{1,0:T(8,128)(2,1)}, u32[]{:S(2)}, u32[]{:S(2)}) collective-permute-start(bf16[512,1536]{1,0:T(8,128)(2,1)} %collective-permute-done.45), channel_id=1, source_target_pairs={{1,0},{2,1},{5,4},{6,5},{9,8},{10,9},{13,12},{14,13},{17,16},{18,1... | collective-permute-start | bytes 4718600 | tf_op jit(solution)/shard_map/ppermute | solution.py:389
  520.7 112.5 %collective-permute-start.54 = (bf16[512,1536]{1,0:T(8,128)(2,1)}, bf16[512,1536]{1,0:T(8,128)(2,1)}, u32[]{:S(2)}, u32[]{:S(2)}) collective-permute-start(bf16[512,1536]{1,0:T(8,128)(2,1)} %pad_maximum_fusion.5), channel_id=1, source_target_pairs={{0,1},{1,2},{2,3},{4,5},{5,6},{6,7},{8,9},{9,10},{10,11},{12,13},{... | collective-permute-start | bytes 4718600 | tf_op jit(solution)/shard_map/ppermute | solution.py:388
  524.9 108.2 %collective-permute-start.55 = (bf16[512,1536]{1,0:T(8,128)(2,1)}, bf16[512,1536]{1,0:T(8,128)(2,1)}, u32[]{:S(2)}, u32[]{:S(2)}) collective-permute-start(bf16[512,1536]{1,0:T(8,128)(2,1)} %pad_maximum_fusion.5), channel_id=1, source_target_pairs={{1,0},{2,1},{3,2},{5,4},{6,5},{7,6},{9,8},{10,9},{11,10},{13,12},{... | collective-permute-start | bytes 4718600 | tf_op jit(solution)/shard_map/ppermute | solution.py:389
  526.2 107.0 %collective-permute-start.56 = (bf16[512,1536]{1,0:T(8,128)(2,1)}, bf16[512,1536]{1,0:T(8,128)(2,1)}, u32[]{:S(2)}, u32[]{:S(2)}) collective-permute-start(bf16[512,1536]{1,0:T(8,128)(2,1)} %collective-permute-done.49), channel_id=1, source_target_pairs={{2,3},{6,7},{10,11},{14,15},{18,19},{22,23},{26,27},{30,31}} | collective-permute-start | bytes 4718600 | tf_op jit(solution)/shard_map/ppermute | solution.py:388
  528.0 105.2 %collective-permute-start.57 = (bf16[512,1536]{1,0:T(8,128)(2,1)}, bf16[512,1536]{1,0:T(8,128)(2,1)}, u32[]{:S(2)}, u32[]{:S(2)}) collective-permute-start(bf16[512,1536]{1,0:T(8,128)(2,1)} %collective-permute-done.50), channel_id=1, source_target_pairs={{1,0},{5,4},{9,8},{13,12},{17,16},{21,20},{25,24},{29,28}} | collective-permute-start | bytes 4718600 | tf_op jit(solution)/shard_map/ppermute | solution.py:389
  531.5 98.5 %collective-permute-start.64 = (bf16[192,1536]{1,0:T(8,128)(2,1)S(1)}, bf16[192,1536]{1,0:T(8,128)(2,1)S(1)}, u32[]{:S(2)}, u32[]{:S(2)}) collective-permute-start(bf16[192,1536]{1,0:T(8,128)(2,1)S(1)} %copy.49), channel_id=1, source_target_pairs={{0,0},{1,4},{2,8},{3,12},{4,1},{5,5},{6,9},{7,13},{8,2},{9,6},{10,... | collective-permute-start | bytes 1769480 | tf_op jit(solution)/shard_map/ppermute | solution.py:367
  635.1 40.9 %collective-permute-start.60 = (bf16[512,1536]{1,0:T(8,128)(2,1)}, bf16[512,1536]{1,0:T(8,128)(2,1)}, u32[]{:S(2)}, u32[]{:S(2)}) collective-permute-start(bf16[512,1536]{1,0:T(8,128)(2,1)} %collective-permute-done.55), channel_id=1, source_target_pairs={{1,0},{2,1},{5,4},{6,5},{9,8},{10,9},{13,12},{14,13},{17,16},{18,1... | collective-permute-start | bytes 4718600 | tf_op jit(solution)/shard_map/ppermute | solution.py:389
  676.0 58.6 %collective-permute-start.62 = (bf16[512,1536]{1,0:T(8,128)(2,1)}, bf16[512,1536]{1,0:T(8,128)(2,1)}, u32[]{:S(2)}, u32[]{:S(2)}) collective-permute-start(bf16[512,1536]{1,0:T(8,128)(2,1)} %collective-permute-done.60), channel_id=1, source_target_pairs={{1,0},{5,4},{9,8},{13,12},{17,16},{21,20},{25,24},{29,28}} | collective-permute-start | bytes 4718600 | tf_op jit(solution)/shard_map/ppermute | solution.py:389
  677.3 57.3 %collective-permute-start.63 = (bf16[512,1536]{1,0:T(8,128)(2,1)}, bf16[512,1536]{1,0:T(8,128)(2,1)}, u32[]{:S(2)}, u32[]{:S(2)}) collective-permute-start(bf16[512,1536]{1,0:T(8,128)(2,1)} %collective-permute-done.59), channel_id=1, source_target_pairs={{2,3},{6,7},{10,11},{14,15},{18,19},{22,23},{26,27},{30,31}} | collective-permute-start | bytes 4718600 | tf_op jit(solution)/shard_map/ppermute | solution.py:388
  691.2 39.8 %collective-permute-start.65 = (bf16[192,1152]{1,0:T(8,128)(2,1)S(1)}, bf16[192,1152]{1,0:T(8,128)(2,1)S(1)}, u32[]{:S(2)}, u32[]{:S(2)}) collective-permute-start(bf16[192,1152]{1,0:T(8,128)(2,1)S(1)} %copy.50), channel_id=1, source_target_pairs={{0,0},{1,4},{2,8},{3,12},{4,1},{5,5},{6,9},{7,13},{8,2},{9,6},{10,... | collective-permute-start | bytes 1327112 | tf_op jit(solution)/shard_map/ppermute | solution.py:367
  697.0 32.2 %collective-permute-start.66 = (f32[8,768]{1,0:T(8,128)S(1)}, f32[8,768]{1,0:T(8,128)S(1)}, u32[]{:S(2)}, u32[]{:S(2)}) collective-permute-start(f32[8,768]{1,0:T(8,128)S(1)} %slice.379), channel_id=1, source_target_pairs={{0,0},{1,4},{2,8},{3,12},{4,1},{5,5},{6,9},{7,13},{8,2},{9,6},{10,... | collective-permute-start | bytes 73736 | tf_op jit(solution)/shard_map/ppermute | solution.py:367
  (109 other events, 1753.3 us)
Sparse Core Ops, SparseCore 0:
  309.9 121.2 reduce-scatter.6
  453.8 110.0 reduce-scatter.8

commit v5 on v4

--- a/solution.py
+++ b/solution.py
@@ -406,10 +406,6 @@
     )
 
 
-def slots_of(v, one, two, three):
-    return [v, slot_one(one), slot_two(one, two), slot_three(two, three)]
-
-
 def summed(v, axes):
     for axis in axes:
         reach = 1
@@ -471,30 +467,30 @@
     step_low = jnp.pad(step_weight.astype(BF16), ((0, 0), (0, LANES - heads)))
     piece = jnp.concatenate([inner_weight[:, 1].astype(BF16), step_low, shared_weight.astype(BF16)], axis=1)
     gate_piece = jnp.concatenate([inner_weight[:, 0].astype(BF16), out_weight.astype(BF16)], axis=1)
-    own_tokens, piece, gate_piece = tie(exchanged(picked), crossed(piece), gate_piece)
+    picked_cot = jnp.dot(chosen, cotangent, preferred_element_type=F32).astype(BF16)
+    own_tokens, piece, picked_cot = tie(exchanged(picked), crossed(piece), picked_cot)
+    own_cot = exchanged(picked_cot)
     one = line_step((piece, piece), 1)
     in_slots = [row_doubling(piece)]
-    gate_piece = crossed(gate_piece)
     hidden = own_tokens.astype(F32)
     scale = lax.rsqrt(jnp.mean(hidden * hidden, axis=-1, keepdims=True) + EPSILON)
     own_normed = (hidden * scale * norm_gain).astype(BF16)
     beside, near = swap(own_normed, "side"), swap(own_normed, "core")
-    picked_cot = jnp.dot(chosen, cotangent, preferred_element_type=F32).astype(BF16)
-    one, in_slots, near = tie(one, in_slots, near)
+    one, near, gate_piece = tie(one, near, gate_piece)
     two = line_step(one, 2)
+    gate_piece = crossed(gate_piece)
     in_slots = in_slots + [row_doubling(slot_one(one))]
-    two, in_slots, gate_piece, picked_cot = tie(two, in_slots, gate_piece, picked_cot)
+    two, own_cot = tie(two, own_cot)
     three = line_step(two, 3)
     in_slots = in_slots + [row_doubling(slot_two(one, two))]
-    three, in_slots, beside = tie(three, in_slots, beside)
+    three, beside, gate_piece = tie(three, beside, gate_piece)
     in_slots = in_slots + [row_doubling(slot_three(two, three))]
     far = swap(beside, "core")
     one = line_step((gate_piece, gate_piece), 1)
-    own_cot = exchanged(picked_cot)
-    in_slots, far, one, own_cot = tie(in_slots, far, one, own_cot)
+    cot_beside, cot_near = swap(own_cot, "side"), swap(own_cot, "core")
+    in_slots, far, one = tie(in_slots, far, one)
     two = line_step(one, 2)
     gate_slots = [row_doubling(gate_piece), row_doubling(slot_one(one))]
-    cot_beside, cot_near = swap(own_cot, "side"), swap(own_cot, "core")
     normed = jnp.concatenate([own_normed, near, beside, far])
     in_full = assembled(in_slots)
 
@@ -549,12 +545,10 @@
     row_of, plane_of = (block_of // planes) ^ row, block_of % planes
     slot = row_of * group_rows + destination - block_of * row_count - source * group_rows
 
-    def returned(held):
-        def settled(which):
-            where = jnp.concatenate([jnp.where(plane_of == slot_planes[j], slot, -1)[:, None] == jnp.arange(owned)[None, :]
-                                     for j in which], axis=1)
-            return jnp.dot(where.astype(BF16), jnp.concatenate([held[j] for j in which]), preferred_element_type=F32)
-        return settled((0, 1)).astype(BF16) + settled((2, 3)).astype(BF16)
+    def settled(held, which):
+        where = jnp.concatenate([jnp.where(plane_of == slot_planes[j], slot, -1)[:, None] == jnp.arange(owned)[None, :]
+                                 for j in which], axis=1)
+        return jnp.dot(where.astype(BF16), jnp.concatenate(held), preferred_element_type=F32).astype(BF16)
 
     proj = jnp.dot(normed, in_full, preferred_element_type=F32)
     proj, two, gate_slots, cot_near = tie(proj, two, gate_slots, cot_near)
@@ -617,7 +611,7 @@
     in_grad = contract_rows(normed, jnp.concatenate([proj_later, gathered(own_shared)], axis=1)).astype(BF16)
     in_grad, out_one, both_grad, own_back = lax.optimization_barrier((in_grad, out_one, both_grad, own_back))
     out_two = line_step(out_one, 2)
-    both_grad = crossed(both_grad).astype(F32)
+    both_grad = crossed(both_grad)
     in_grad = lax.psum_scatter(in_grad, ("row", "tensor"), scatter_dimension=0, tiled=True)
     normed_back = own_back + beside.astype(F32) + contract_columns(own_shared, in_full[:, width + LANES :])
     norm_gain_grad = jnp.sum(normed_back * hidden * scale, axis=0)
@@ -640,21 +634,23 @@
     small = summed(small, ("row",))
     small = jnp.concatenate([small[:8], summed(small[8:], ("core", "side"))], axis=0)
     back_rows = exchanged(input_work.astype(BF16))
-    back_rows, out_two, small = tie(back_rows, out_two, small)
-    small_added = swap(small, "tensor", 1)
+    back_rows, out_two, small, both_grad = tie(back_rows, out_two, small, both_grad)
+    back_one = line_step((back_rows, back_rows), 1)
     out_three = line_step(out_two, 3)
-    back_one = line_step((back_rows, back_rows), 1)
-    back_one, out_three, small_added = tie(back_one, out_three, small_added)
-    small = small + small_added
-    small_added = swap(small, "tensor", 2)
     back_two = line_step(back_one, 2)
-    layer_out = returned(slots_of(out_rows, out_one, out_two, out_three))
-    back_two, in_grad, small_added = tie(back_two, in_grad, small_added)
-    small = small + small_added
+    back_two, in_grad = tie(back_two, in_grad)
+    back_three = line_step(back_two, 3)
+    out_three, _ = tie(out_three, back_two)
+    layer_out = settled([out_rows, slot_one(out_one)], (0, 1))
+    layer_out = layer_out + settled([slot_two(out_one, out_two), slot_three(out_two, out_three)], (2, 3))
+    input_grad = settled([back_rows, slot_one(back_one)], (0, 1))
+    layer_out, input_grad, back_three, small = tie(layer_out, input_grad, back_three, small)
+    input_grad = input_grad + settled([slot_two(back_one, back_two), slot_three(back_two, back_three)], (2, 3))
+    small = small + swap(small, "tensor", 1)
+    small = small + swap(small, "tensor", 2)
     mine, common = crossed(small[:8]), small[8:]
-    input_grad = returned(slots_of(back_rows, back_one, back_two, line_step(back_two, 3)))
     in_grad = crossed(in_grad).astype(F32)
-    inner_grad = jnp.stack([both_grad[:, :width], in_grad[:, :width]], axis=1)
+    inner_grad = jnp.stack([both_grad[:, :width].astype(F32), in_grad[:, :width]], axis=1)
 
     lines = line(norm_gain_grad).shape[0]
     norm_gain_grad = common[:lines].reshape(-1)[:model_width]
@@ -662,7 +658,7 @@
     return (
         layer_out, input_grad, norm_gain_grad, inner_grad, in_grad[:, width + LANES :],
         in_grad[:, width : width + heads], mine[:4], mine[4], shared_sums[:4], shared_sums[4],
-        mine[6, :heads], mine[6, heads : 2 * heads], mine[6, 2 * heads : 3 * heads], mine[5], both_grad[:, width:],
+        mine[6, :heads], mine[6, heads : 2 * heads], mine[6, 2 * heads : 3 * heads], mine[5], both_grad[:, width:].astype(F32),
     )
 
 

time: 771 us -> 772 us (level)
  waiting for transfers between devices: 304 us -> 276 us
  starting transfers between devices: 114 us -> 140 us
  other arithmetic: 56.9 us -> 64.8 us
    ppermute x6, waiting for transfers between devices: 132 us -> 38.6 us  [crossed(): return lax.ppermute(v, ('side', 'core', 'tensor'), pairs)]
    ppermute x12, waiting for transfers between devices: 15.9 us -> 58.1 us  [line_step(): lax.ppermute(left, 'tensor', [(i, i + 1) for i in range(j - 1, 3)])]
    ppermute x12, waiting for transfers between devices: 70.4 us -> 107 us  [line_step(): lax.ppermute(right, 'tensor', [(i + 1, i) for i in range(0, 4 - j)])]
    ppermute x6, starting transfers between devices: 26 us -> 41.9 us  [crossed(): return lax.ppermute(v, ('side', 'core', 'tensor'), pairs)]
    ppermute x12, starting transfers between devices: 16.4 us -> 27.4 us  [line_step(): lax.ppermute(right, 'tensor', [(i + 1, i) for i in range(0, 4 - j)])]
    ppermute x37, waiting for transfers between devices: 79.6 us -> 69.3 us  [swap(): return lax.ppermute(v, axis, [(i, i ^ mask) for i in range(count)])]
    add x2 -> x3, other arithmetic: 0.02 us -> 9.07 us  [the longest x1 9.05 us: on_device(): input_grad + settled([slot_two(back_one, back_two), slot_three(back_two,...]
    unnamed x137 -> x139, local copies, waits for them, and re-layouts: 17.2 us -> 18.6 us
  transfers between devices with their start and end apart: 69 -> 69, of which waited for: 28 -> 26; matrix products, arithmetic and copies ran while one was open for 22% -> 24% of each run, Pallas kernels for 10% -> 10%
where the time goes in v5:
time: 772 us; the launch traced here: 765 us
  waiting for transfers between devices  276 us (36%)
  matrix products  145 us (19%)
  starting transfers between devices  140 us (18%)
  Pallas kernels  77.5 us (10%)
  other arithmetic  64.8 us (8%)
  local copies, waits for them, and re-layouts  41.1 us (5%)
  between operations  21.2 us (3%)
    ppermute x12, waiting for transfers between devices, line_step(): lax.ppermute(right, 'tensor', [(i + 1, i) for i in range(0, 4 - j)])  107 us
    ppermute x37, waiting for transfers between devices, swap(): return lax.ppermute(v, axis, [(i, i ^ mask) for i in range(count)])  69.3 us
    ppermute x12, waiting for transfers between devices, line_step(): lax.ppermute(left, 'tensor', [(i, i + 1) for i in range(j - 1, 3)])  58.1 us
    pallas_call x1, Pallas kernels, mixer_backward(): pl.pallas_call(backward_kernel, grid_spec=pltpu.PrefetchScalarGridSpec(nu...  51.7 us
    ppermute x37, starting transfers between devices, swap(): return lax.ppermute(v, axis, [(i, i ^ mask) for i in range(count)])  43.6 us
    ppermute x6, starting transfers between devices, crossed(): return lax.ppermute(v, ('side', 'core', 'tensor'), pairs)  41.9 us
    ppermute x6, waiting for transfers between devices, crossed(): return lax.ppermute(v, ('side', 'core', 'tensor'), pairs)  38.6 us
    dot_general x4, matrix products, settled(): jnp.dot(where.astype(BF16), jnp.concatenate(held), preferred_element_type...  33.9 us
  transfers between devices with their start and end apart: 69, of which 26 were waited for; matrix products, arithmetic and copies ran while one was open for 24% of the time, Pallas kernels for 10%

profile of v5, /device:TPU:1, one launch (start us, length us, event | category | flops | bytes accessed | tf_op | source)
XLA Modules:
  0.0 765.3 jit_solution(3296008153483473916)
XLA Ops:
  37.7 8.4 %collective-permute-start.11 = (bf16[512,1536]{1,0:T(8,128)(2,1)}, bf16[512,1536]{1,0:T(8,128)(2,1)}, u32[]{:S(2)}, u32[]{:S(2)}) collective-permute-start(bf16[512,1536]{1,0:T(8,128)(2,1)} %fusion.20), channel_id=1, source_target_pairs={{0,8},{8,0},{1,9},{9,1},{2,10},{10,2},{3,11},{11,3},{4,12},{12,4},... | collective-permute-start | bytes 4718600 | tf_op jit(solution)/shard_map/ppermute | solution.py:362
  71.3 10.0 %collective-permute-done.7 = bf16[192,1152]{1,0:T(8,128)(2,1)} collective-permute-done((bf16[192,1152]{1,0:T(8,128)(2,1)S(1)}, bf16[192,1152]{1,0:T(8,128)(2,1)}, u32[]{:S(2)}, u32[]{:S(2)}) %collective-permute-start.7) | collective-permute-done | bytes 442400 | tf_op jit(solution)/shard_map/ppermute | solution.py:389
  84.2 16.3 %collective-permute-start = (f32[8,768]{1,0:T(8,128)S(1)}, f32[8,768]{1,0:T(8,128)S(1)}, u32[]{:S(2)}, u32[]{:S(2)}) collective-permute-start(f32[8,768]{1,0:T(8,128)S(1)} %concatenate.77), channel_id=1, source_target_pairs={{0,0},{1,4},{2,8},{3,12},{4,1},{5,5},{6,9},{7,13},{8,2},{9,6},{10,... | collective-permute-start | bytes 73736 | tf_op jit(solution)/shard_map/ppermute | solution.py:367
  132.8 8.2 %collective-permute-done.15 = bf16[192,1152]{1,0:T(8,128)(2,1)S(1)} collective-permute-done((bf16[192,1152]{1,0:T(8,128)(2,1)}, bf16[192,1152]{1,0:T(8,128)(2,1)S(1)}, u32[]{:S(2)}, u32[]{:S(2)}) %collective-permute-start.15) | collective-permute-done | bytes 442400 | tf_op jit(solution)/shard_map/ppermute | solution.py:362
  153.3 13.0 %collective-permute-start.21 = (bf16[192,1536]{1,0:T(8,128)(2,1)}, bf16[192,1536]{1,0:T(8,128)(2,1)}, u32[]{:S(2)}, u32[]{:S(2)}) collective-permute-start(bf16[192,1536]{1,0:T(8,128)(2,1)} %collective-permute-done.19), channel_id=1, source_target_pairs={{1,0},{2,1},{5,4},{6,5},{9,8},{10,9},{13,12},{14,13},{17,16},{18,1... | collective-permute-start | bytes 1769480 | tf_op jit(solution)/shard_map/ppermute | solution.py:389
  171.6 16.1 %fusion.126.proj_ref.proj_before_ref = f32[2048,1152]{1,0:T(8,128)} fusion(bf16[1536,1152]{1,0:T(8,128)(2,1)S(1)} %constant_dynamic-update-slice_fusion.12, bf16[512,1536]{1,0:T(8,128)(2,1)} %collective-permute-done.17, bf16[512,1536]{1,0:T(8,128)(2,1)} %collective-permute-done.11, bf16[512,1536]{1,0:T(8,128)(2,1)S(1)} %copy-done.54, ...), kind=kOutput, calls=%fused_computation.270 | convolution fusion | flops 7272923136 | bytes 19267584 | tf_op jit(solution)/shard_map/dot_general | solution.py:553
  195.0 25.8 %mixer_forward.1 = (f32[2048,768]{1,0:T(8,128)}, bf16[16,128,768]{2,1,0:T(8,128)(2,1)}) custom-call(s32[4]{0:T(128)} %fusion.114.lens_ref, s32[16]{0:T(128)} %fusion.111.order_ref, f32[2048,1152]{1,0:T(8,128)} %fusion.126.proj_ref.proj_before_ref, f32[4,768]{1,0:T(4,128)} %slice.348.fw_ref, f32[1,768]{1,0:T(1,128)} %get-tuple-element.289.fb_ref, ...), custom_call_target="tpu_custom_call" | custom-call | flops 20000000000 | bytes 30000000 | tf_op jit(solution)/shard_map/mixer_forward/pallas_call | solution.py:292
  240.8 10.6 %fusion.71 = f32[2048,768]{1,0:T(8,128)S(1)} fusion(bf16[1536,1536]{1,0:T(8,128)(2,1)S(1)} %constant_dynamic-update-slice_fusion.4, bf16[512,1536]{1,0:T(8,128)(2,1)} %collective-permute-done.17, bf16[512,1536]{1,0:T(8,128)(2,1)} %collective-permute-done.11, bf16[512,1536]{1,0:T(8,128)(2,1)S(1)} %copy-done.55, bf16[512,1536]{1,0:T(8,128)(2,1)} %fusion.20), kind=kOutput, calls=%fused_computation.116 | convolution fusion | flops 4857004032 | bytes 14942208 | tf_op jit(solution)/shard_map/dot_general | solution.py:564
  252.7 10.5 %fusion.65 = f32[2048,768]{1,0:T(8,128)S(1)} fusion(bf16[2048,1536]{1,0:T(8,128)(2,1)} %constant_dynamic-update-slice_fusion, bf16[1536,1536]{1,0:T(8,128)(2,1)} %copy-done.4), kind=kOutput, calls=%fused_computation.110 | convolution fusion | flops 4831838208 | bytes 14942208 | tf_op jit(solution)/shard_map/dot_general | solution.py:565
  275.4 14.0 %multiply_convert_fusion.1 = (bf16[2048,768]{1,0:T(8,128)(2,1)S(1)}, f32[2048,768]{1,0:T(8,128)}, f32[768]{0:T(1024)S(1)}, bf16[2048,768]{1,0:T(8,128)(2,1)S(1)}) fusion(f32[2048,768]{1,0:T(8,128)} %copy-done, f32[2048,768]{1,0:T(8,128)} %get-tuple-element.153.out_ref, f32[2048]{0:T(1024)S(1)} %bitcast.62, f32[2048,768]{1,0:T(8,128)} %get-tuple-element.254, ...), kind=kLoop, calls=%fused_computation.16 | loop fusion | flops 36175104 | bytes 37779456 | tf_op jit(solution)/shard_map/convert_element_type | solution.py:583
  293.4 8.2 %convolution_convert_fusion.5 = bf16[1536,768]{0,1:T(8,128)(2,1)S(1)} fusion(bf16[2048,1536]{1,0:T(8,128)(2,1)} %constant_dynamic-update-slice_fusion, bf16[2048,768]{1,0:T(8,128)(2,1)S(1)} %get-tuple-element.260), kind=kOutput, calls=%fused_computation.41 | convolution fusion | flops 4833017856 | bytes 11796480 | tf_op jit(solution)/shard_map/dot_general | solution.py:419
  327.1 51.7 %mixer_backward.1 = (bf16[2048,896]{1,0:T(8,128)(2,1)}, f32[2048,256]{1,0:T(8,128)}, f32[8,768]{1,0:T(8,128)}, f32[8,256]{1,0:T(8,128)}, f32[8,128]{1,0:T(8,128)}) custom-call(s32[4]{0:T(128)} %fusion.114.lens_ref, s32[16]{0:T(128)} %fusion.111.order_ref, f32[2048,1152]{1,0:T(8,128)} %fusion.126.proj_ref.proj_before_ref, ...), custom_call_target="tpu_custom_call" | custom-call | flops 40000000000 | bytes 60000000 | tf_op jit(solution)/shard_map/mixer_backward/pallas_call | solution.py:327
  424.0 14.6 %convolution_convert_fusion.4 = bf16[1536,1152]{1,0:T(8,128)(2,1)} fusion(bf16[512,256]{1,0:T(8,128)(2,1)S(1)} %collective-permute-done.43, bf16[512,256]{1,0:T(8,128)(2,1)S(1)} %collective-permute-done.42, bf16[512,256]{1,0:T(8,128)(2,1)S(1)} %collective-permute-done.41, bf16[512,256]{1,0:T(8,128)(2,1)S(1)} %add_convert_fusion.1, ...), kind=kOutput, calls=%fused_computation.6 | convolution fusion | flops 7298285568 | bytes 14548992 | tf_op jit(solution)/shard_map/dot_general | solution.py:419
  443.1 17.1 %collective-permute-done.44 = bf16[512,1536]{1,0:T(8,128)(2,1)} collective-permute-done((bf16[512,1536]{1,0:T(8,128)(2,1)}, bf16[512,1536]{1,0:T(8,128)(2,1)}, u32[]{:S(2)}, u32[]{:S(2)}) %collective-permute-start.44) | collective-permute-done | bytes 1572896 | tf_op jit(solution)/shard_map/ppermute | solution.py:388
  473.7 22.7 %collective-permute-done.51 = f32[12,768]{1,0:T(8,128)S(1)} collective-permute-done((f32[12,768]{1,0:T(8,128)S(1)}, f32[12,768]{1,0:T(8,128)S(1)}, u32[]{:S(2)}, u32[]{:S(2)}) %collective-permute-start.51) | collective-permute-done | bytes 36896 | tf_op jit(solution)/shard_map/ppermute | solution.py:362
  507.7 38.6 %collective-permute-done.54 = bf16[192,1536]{1,0:T(8,128)(2,1)S(1)} collective-permute-done((bf16[192,1536]{1,0:T(8,128)(2,1)}, bf16[192,1536]{1,0:T(8,128)(2,1)S(1)}, u32[]{:S(2)}, u32[]{:S(2)}) %collective-permute-start.54) | collective-permute-done | bytes 589856 | tf_op jit(solution)/shard_map/ppermute | solution.py:367
  562.6 34.3 %collective-permute-done.57 = bf16[512,1536]{1,0:T(8,128)(2,1)} collective-permute-done((bf16[512,1536]{1,0:T(8,128)(2,1)S(1)}, bf16[512,1536]{1,0:T(8,128)(2,1)}, u32[]{:S(2)}, u32[]{:S(2)}) %collective-permute-start.57) | collective-permute-done | bytes 1572896 | tf_op jit(solution)/shard_map/ppermute | solution.py:388
  598.8 10.7 %collective-permute-done.59 = bf16[512,1536]{1,0:T(8,128)(2,1)S(1)} collective-permute-done((bf16[512,1536]{1,0:T(8,128)(2,1)S(1)}, bf16[512,1536]{1,0:T(8,128)(2,1)S(1)}, u32[]{:S(2)}, u32[]{:S(2)}) %collective-permute-start.59) | collective-permute-done | bytes 1572896 | tf_op jit(solution)/shard_map/ppermute | solution.py:389
  610.9 8.5 %convolution_convert_fusion.1 = bf16[2048,1536]{1,0:T(8,128)(2,1)} fusion(bf16[512,1536]{1,0:T(8,128)(2,1)S(1)} %broadcast_select_fusion, bf16[512,1536]{1,0:T(8,128)(2,1)S(1)} %pad_maximum_fusion.5, pred[2048,512]{1,0:T(32,128)(4,1)S(1)} %get-tuple-element.309, pred[2048,512]{1,0:T(32,128)(4,1)S(1)} %get-tuple-element.310), kind=kOutput, calls=%fused_computation.3 | convolution fusion | flops 6453985280 | bytes 11534336 | tf_op jit(solution)/shard_map/dot_general | solution.py:551
  620.7 56.2 %collective-permute-done.60 = bf16[512,1536]{1,0:T(8,128)(2,1)} collective-permute-done((bf16[512,1536]{1,0:T(8,128)(2,1)S(1)}, bf16[512,1536]{1,0:T(8,128)(2,1)}, u32[]{:S(2)}, u32[]{:S(2)}) %collective-permute-start.60) | collective-permute-done | bytes 1572896 | tf_op jit(solution)/shard_map/ppermute | solution.py:389
  694.6 10.0 %fusion.1 = bf16[2048,1536]{1,0:T(8,128)(2,1)} fusion(bf16[2048,1536]{1,0:T(8,128)(2,1)S(1)} %convolution_convert_fusion.2, bf16[512,1536]{1,0:T(8,128)(2,1)S(1)} %get-tuple-element.265, bf16[512,1536]{1,0:T(8,128)(2,1)} %pad_maximum_fusion.4, pred[2048,512]{1,0:T(32,128)(4,1)S(1)} %copy-done.22, pred[2048,512]{1,0:T(32,128)(4,1)S(1)} %copy-done.24), kind=kOutput, calls=%fused_computation.22 | convolution fusion | flops 6457131008 | bytes 17825792 | tf_op jit(solution)/shard_map/dot_general | solution.py:551
  708.1 19.8 %collective-permute-done.62 = bf16[512,1536]{1,0:T(8,128)(2,1)} collective-permute-done((bf16[512,1536]{1,0:T(8,128)(2,1)}, bf16[512,1536]{1,0:T(8,128)(2,1)}, u32[]{:S(2)}, u32[]{:S(2)}) %collective-permute-start.62) | collective-permute-done | bytes 1572896 | tf_op jit(solution)/shard_map/ppermute | solution.py:389
  731.2 8.5 %convolution_convert_fusion = bf16[2048,1536]{1,0:T(8,128)(2,1)} fusion(bf16[512,1536]{1,0:T(8,128)(2,1)S(1)} %get-tuple-element.262, bf16[512,1536]{1,0:T(8,128)(2,1)S(1)} %get-tuple-element.261, pred[2048,512]{1,0:T(32,128)(4,1)S(1)} %copy-done.18, pred[2048,512]{1,0:T(32,128)(4,1)S(1)} %copy-done.20), kind=kOutput, calls=%fused_computation.2 | convolution fusion | flops 6453985280 | bytes 11534336 | tf_op jit(solution)/shard_map/dot_general | solution.py:551
  739.7 9.1 %add.331 = bf16[2048,1536]{1,0:T(8,128)(2,1)} add(bf16[2048,1536]{1,0:T(8,128)(2,1)} %convolution_convert_fusion.1, bf16[2048,1536]{1,0:T(8,128)(2,1)} %convolution_convert_fusion) | non-fusion elementwise | flops 3145728 | bytes 18874368 | tf_op jit(solution)/shard_map/add | solution.py:648
  (415 shorter events, 301.4 us)
Async XLA Ops:
  7.2 434.5 %reduce-scatter.7.cloned.1.call-start = ((), (), s32[]{:S(2)}) async-start(), calls=%async_computation.2 | async-start | bytes 5308416
  37.7 63.5 %collective-permute-start.11 = (bf16[512,1536]{1,0:T(8,128)(2,1)}, bf16[512,1536]{1,0:T(8,128)(2,1)}, u32[]{:S(2)}, u32[]{:S(2)}) collective-permute-start(bf16[512,1536]{1,0:T(8,128)(2,1)} %fusion.20), channel_id=1, source_target_pairs={{0,8},{8,0},{1,9},{9,1},{2,10},{10,2},{3,11},{11,3},{4,12},{12,4},... | collective-permute-start | bytes 4718600 | tf_op jit(solution)/shard_map/ppermute | solution.py:362
  64.5 36.7 %collective-permute-start.12 = (bf16[192,1536]{1,0:T(8,128)(2,1)}, bf16[192,1536]{1,0:T(8,128)(2,1)}, u32[]{:S(2)}, u32[]{:S(2)}) collective-permute-start(bf16[192,1536]{1,0:T(8,128)(2,1)} %pad_maximum_fusion.7), channel_id=1, source_target_pairs={{0,0},{1,4},{2,8},{3,12},{4,1},{5,5},{6,9},{7,13},{8,2},{9,6},{10,... | collective-permute-start | bytes 1769480 | tf_op jit(solution)/shard_map/ppermute | solution.py:367
  84.2 38.5 %collective-permute-start = (f32[8,768]{1,0:T(8,128)S(1)}, f32[8,768]{1,0:T(8,128)S(1)}, u32[]{:S(2)}, u32[]{:S(2)}) collective-permute-start(f32[8,768]{1,0:T(8,128)S(1)} %concatenate.77), channel_id=1, source_target_pairs={{0,0},{1,4},{2,8},{3,12},{4,1},{5,5},{6,9},{7,13},{8,2},{9,6},{10,... | collective-permute-start | bytes 73736 | tf_op jit(solution)/shard_map/ppermute | solution.py:367
  105.7 44.9 %collective-permute-start.17 = (bf16[512,1536]{1,0:T(8,128)(2,1)}, bf16[512,1536]{1,0:T(8,128)(2,1)}, u32[]{:S(2)}, u32[]{:S(2)}) collective-permute-start(bf16[512,1536]{1,0:T(8,128)(2,1)} %collective-permute-done.11), channel_id=1, source_target_pairs={{0,4},{4,0},{1,5},{5,1},{2,6},{6,2},{3,7},{7,3},{8,12},{12,8},{9,1... | collective-permute-start | bytes 4718600 | tf_op jit(solution)/shard_map/ppermute | solution.py:362
  141.0 46.8 %collective-permute-start.24 = (bf16[512,1536]{1,0:T(8,128)(2,1)S(1)}, bf16[512,1536]{1,0:T(8,128)(2,1)S(1)}, u32[]{:S(2)}, u32[]{:S(2)}) collective-permute-start(bf16[512,1536]{1,0:T(8,128)(2,1)S(1)} %pad_maximum_fusion.3), channel_id=1, source_target_pairs={{0,4},{4,0},{1,5},{5,1},{2,6},{6,2},{3,7},{7,3},{8,12},{12,8},{9,1... | collective-permute-start | bytes 4718600 | tf_op jit(solution)/shard_map/ppermute | solution.py:362
  150.5 37.2 %collective-permute-start.22 = (bf16[192,1536]{1,0:T(8,128)(2,1)}, bf16[192,1536]{1,0:T(8,128)(2,1)S(1)}, u32[]{:S(2)}, u32[]{:S(2)}) collective-permute-start(bf16[192,1536]{1,0:T(8,128)(2,1)} %collective-permute-done.12), channel_id=1, source_target_pairs={{0,16},{16,0},{1,17},{17,1},{2,18},{18,2},{3,19},{19,3},{4,20},{20... | collective-permute-start | bytes 1769480 | tf_op jit(solution)/shard_map/ppermute | solution.py:362
  150.6 38.5 %collective-permute-start.20 = (bf16[192,1536]{1,0:T(8,128)(2,1)}, bf16[192,1536]{1,0:T(8,128)(2,1)}, u32[]{:S(2)}, u32[]{:S(2)}) collective-permute-start(bf16[192,1536]{1,0:T(8,128)(2,1)} %collective-permute-done.18), channel_id=1, source_target_pairs={{1,2},{2,3},{5,6},{6,7},{9,10},{10,11},{13,14},{14,15},{17,18},{18... | collective-permute-start | bytes 1769480 | tf_op jit(solution)/shard_map/ppermute | solution.py:388
  153.3 35.8 %collective-permute-start.21 = (bf16[192,1536]{1,0:T(8,128)(2,1)}, bf16[192,1536]{1,0:T(8,128)(2,1)}, u32[]{:S(2)}, u32[]{:S(2)}) collective-permute-start(bf16[192,1536]{1,0:T(8,128)(2,1)} %collective-permute-done.19), channel_id=1, source_target_pairs={{1,0},{2,1},{5,4},{6,5},{9,8},{10,9},{13,12},{14,13},{17,16},{18,1... | collective-permute-start | bytes 1769480 | tf_op jit(solution)/shard_map/ppermute | solution.py:389
  320.1 58.7 %collective-permute-start.35 = (bf16[512,1536]{1,0:T(8,128)(2,1)}, bf16[512,1536]{1,0:T(8,128)(2,1)S(1)}, u32[]{:S(2)}, u32[]{:S(2)}) collective-permute-start(bf16[512,1536]{1,0:T(8,128)(2,1)} %fusion.45), channel_id=1, source_target_pairs={{0,8},{8,0},{1,9},{9,1},{2,10},{10,2},{3,11},{11,3},{4,12},{12,4},... | collective-permute-start | bytes 4718600 | tf_op jit(solution)/shard_map/ppermute | solution.py:362
  327.0 292.4 %reduce-scatter.9.cloned.1.call-start = ((), (), s32[]{:S(2)}) async-start(), calls=%async_computation.3 | async-start | bytes 3981312
  407.3 52.9 %collective-permute-start.44 = (bf16[512,1536]{1,0:T(8,128)(2,1)}, bf16[512,1536]{1,0:T(8,128)(2,1)}, u32[]{:S(2)}, u32[]{:S(2)}) collective-permute-start(bf16[512,1536]{1,0:T(8,128)(2,1)} %pad_maximum_fusion.4), channel_id=1, source_target_pairs={{0,1},{1,2},{2,3},{4,5},{5,6},{6,7},{8,9},{9,10},{10,11},{12,13},{... | collective-permute-start | bytes 4718600 | tf_op jit(solution)/shard_map/ppermute | solution.py:388
  412.5 49.9 %collective-permute-start.45 = (bf16[512,1536]{1,0:T(8,128)(2,1)}, bf16[512,1536]{1,0:T(8,128)(2,1)}, u32[]{:S(2)}, u32[]{:S(2)}) collective-permute-start(bf16[512,1536]{1,0:T(8,128)(2,1)} %pad_maximum_fusion.4), channel_id=1, source_target_pairs={{1,0},{2,1},{3,2},{5,4},{6,5},{7,6},{9,8},{10,9},{11,10},{13,12},{... | collective-permute-start | bytes 4718600 | tf_op jit(solution)/shard_map/ppermute | solution.py:389
  420.3 46.2 %collective-permute-start.47 = (bf16[512,1536]{1,0:T(8,128)(2,1)}, bf16[512,1536]{1,0:T(8,128)(2,1)}, u32[]{:S(2)}, u32[]{:S(2)}) collective-permute-start(bf16[512,1536]{1,0:T(8,128)(2,1)} %fusion.46), channel_id=1, source_target_pairs={{0,8},{8,0},{1,9},{9,1},{2,10},{10,2},{3,11},{11,3},{4,12},{12,4},... | collective-permute-start | bytes 4718600 | tf_op jit(solution)/shard_map/ppermute | solution.py:362
  463.1 83.1 %collective-permute-start.49 = (bf16[512,1536]{1,0:T(8,128)(2,1)}, bf16[512,1536]{1,0:T(8,128)(2,1)}, u32[]{:S(2)}, u32[]{:S(2)}) collective-permute-start(bf16[512,1536]{1,0:T(8,128)(2,1)} %collective-permute-done.44), channel_id=1, source_target_pairs={{1,2},{2,3},{5,6},{6,7},{9,10},{10,11},{13,14},{14,15},{17,18},{18... | collective-permute-start | bytes 4718600 | tf_op jit(solution)/shard_map/ppermute | solution.py:388
  465.1 81.1 %collective-permute-start.50 = (bf16[512,1536]{1,0:T(8,128)(2,1)}, bf16[512,1536]{1,0:T(8,128)(2,1)}, u32[]{:S(2)}, u32[]{:S(2)}) collective-permute-start(bf16[512,1536]{1,0:T(8,128)(2,1)} %collective-permute-done.45), channel_id=1, source_target_pairs={{1,0},{2,1},{5,4},{6,5},{9,8},{10,9},{13,12},{14,13},{17,16},{18,1... | collective-permute-start | bytes 4718600 | tf_op jit(solution)/shard_map/ppermute | solution.py:389
  471.4 36.1 %collective-permute-start.48 = (bf16[256,1536]{1,0:T(8,128)(2,1)S(1)}, bf16[256,1536]{1,0:T(8,128)(2,1)S(1)}, u32[]{:S(2)}, u32[]{:S(2)}) collective-permute-start(bf16[256,1536]{1,0:T(8,128)(2,1)S(1)} %get-tuple-element.267), channel_id=1, source_target_pairs={{0,16},{16,0},{1,17},{17,1},{2,18},{18,2},{3,19},{19,3},{4,20},{20... | collective-permute-start | bytes 2359304 | tf_op jit(solution)/shard_map/ppermute | solution.py:362
  498.7 47.6 %collective-permute-start.54 = (bf16[192,1536]{1,0:T(8,128)(2,1)}, bf16[192,1536]{1,0:T(8,128)(2,1)S(1)}, u32[]{:S(2)}, u32[]{:S(2)}) collective-permute-start(bf16[192,1536]{1,0:T(8,128)(2,1)} %copy.48), channel_id=1, source_target_pairs={{0,0},{1,4},{2,8},{3,12},{4,1},{5,5},{6,9},{7,13},{8,2},{9,6},{10,... | collective-permute-start | bytes 1769480 | tf_op jit(solution)/shard_map/ppermute | solution.py:367
  546.2 50.7 %collective-permute-start.57 = (bf16[512,1536]{1,0:T(8,128)(2,1)S(1)}, bf16[512,1536]{1,0:T(8,128)(2,1)}, u32[]{:S(2)}, u32[]{:S(2)}) collective-permute-start(bf16[512,1536]{1,0:T(8,128)(2,1)S(1)} %pad_maximum_fusion.5), channel_id=1, source_target_pairs={{0,1},{1,2},{2,3},{4,5},{5,6},{6,7},{8,9},{9,10},{10,11},{12,13},{... | collective-permute-start | bytes 4718600 | tf_op jit(solution)/shard_map/ppermute | solution.py:388
  550.6 58.9 %collective-permute-start.59 = (bf16[512,1536]{1,0:T(8,128)(2,1)S(1)}, bf16[512,1536]{1,0:T(8,128)(2,1)S(1)}, u32[]{:S(2)}, u32[]{:S(2)}) collective-permute-start(bf16[512,1536]{1,0:T(8,128)(2,1)S(1)} %pad_maximum_fusion.5), channel_id=1, source_target_pairs={{1,0},{2,1},{3,2},{5,4},{6,5},{7,6},{9,8},{10,9},{11,10},{13,12},{... | collective-permute-start | bytes 4718600 | tf_op jit(solution)/shard_map/ppermute | solution.py:389
  558.6 125.2 %collective-permute-start.55 = (bf16[512,1536]{1,0:T(8,128)(2,1)}, bf16[512,1536]{1,0:T(8,128)(2,1)}, u32[]{:S(2)}, u32[]{:S(2)}) collective-permute-start(bf16[512,1536]{1,0:T(8,128)(2,1)} %collective-permute-done.49), channel_id=1, source_target_pairs={{2,3},{6,7},{10,11},{14,15},{18,19},{22,23},{26,27},{30,31}} | collective-permute-start | bytes 4718600 | tf_op jit(solution)/shard_map/ppermute | solution.py:388
  560.5 123.4 %collective-permute-start.56 = (bf16[512,1536]{1,0:T(8,128)(2,1)}, bf16[512,1536]{1,0:T(8,128)(2,1)}, u32[]{:S(2)}, u32[]{:S(2)}) collective-permute-start(bf16[512,1536]{1,0:T(8,128)(2,1)} %collective-permute-done.50), channel_id=1, source_target_pairs={{1,0},{5,4},{9,8},{13,12},{17,16},{21,20},{25,24},{29,28}} | collective-permute-start | bytes 4718600 | tf_op jit(solution)/shard_map/ppermute | solution.py:389
  609.4 67.5 %collective-permute-start.60 = (bf16[512,1536]{1,0:T(8,128)(2,1)S(1)}, bf16[512,1536]{1,0:T(8,128)(2,1)}, u32[]{:S(2)}, u32[]{:S(2)}) collective-permute-start(bf16[512,1536]{1,0:T(8,128)(2,1)S(1)} %collective-permute-done.59), channel_id=1, source_target_pairs={{1,0},{2,1},{5,4},{6,5},{9,8},{10,9},{13,12},{14,13},{17,16},{18,1... | collective-permute-start | bytes 4718600 | tf_op jit(solution)/shard_map/ppermute | solution.py:389
  682.4 45.5 %collective-permute-start.62 = (bf16[512,1536]{1,0:T(8,128)(2,1)}, bf16[512,1536]{1,0:T(8,128)(2,1)}, u32[]{:S(2)}, u32[]{:S(2)}) collective-permute-start(bf16[512,1536]{1,0:T(8,128)(2,1)} %collective-permute-done.60), channel_id=1, source_target_pairs={{1,0},{5,4},{9,8},{13,12},{17,16},{21,20},{25,24},{29,28}} | collective-permute-start | bytes 4718600 | tf_op jit(solution)/shard_map/ppermute | solution.py:389
  (110 other events, 1930.6 us)
Sparse Core Ops, SparseCore 0:
  327.1 114.5 reduce-scatter.6
  462.5 117.6 reduce-scatter.8

commit v6 on v5

--- a/solution.py
+++ b/solution.py
@@ -415,6 +415,18 @@
     return v
 
 
+def row_scattered(v):
+    row, reach = lax.axis_index("row"), lax.axis_size("row") // 2
+    while reach:
+        half = v.shape[0] // 2
+        high = (row // reach) % 2
+        kept = lax.dynamic_slice_in_dim(v, high * half, half, 0)
+        given = lax.dynamic_slice_in_dim(v, (1 - high) * half, half, 0)
+        v = (kept.astype(F32) + swap(given, "row", reach).astype(F32)).astype(BF16)
+        reach = reach // 2
+    return v
+
+
 def contract_rows(a, b):
     return lax.dot_general(a, b, (((0,), (0,)), ((), ())), preferred_element_type=F32)
 
@@ -480,10 +492,10 @@
     two = line_step(one, 2)
     gate_piece = crossed(gate_piece)
     in_slots = in_slots + [row_doubling(slot_one(one))]
-    two, own_cot = tie(two, own_cot)
+    two, own_cot, in_slots = tie(two, own_cot, in_slots)
     three = line_step(two, 3)
     in_slots = in_slots + [row_doubling(slot_two(one, two))]
-    three, beside, gate_piece = tie(three, beside, gate_piece)
+    three, beside, gate_piece, in_slots = tie(three, beside, gate_piece, in_slots)
     in_slots = in_slots + [row_doubling(slot_three(two, three))]
     far = swap(beside, "core")
     one = line_step((gate_piece, gate_piece), 1)
@@ -612,7 +624,7 @@
     in_grad, out_one, both_grad, own_back = lax.optimization_barrier((in_grad, out_one, both_grad, own_back))
     out_two = line_step(out_one, 2)
     both_grad = crossed(both_grad)
-    in_grad = lax.psum_scatter(in_grad, ("row", "tensor"), scatter_dimension=0, tiled=True)
+    in_grad = lax.psum_scatter(row_scattered(in_grad), "tensor", scatter_dimension=0, tiled=True)
     normed_back = own_back + beside.astype(F32) + contract_columns(own_shared, in_full[:, width + LANES :])
     norm_gain_grad = jnp.sum(normed_back * hidden * scale, axis=0)
     gained = normed_back * norm_gain
@@ -631,9 +643,10 @@
         ],
         axis=0,
     )
+    back_rows, small = tie(input_work.astype(BF16), small)
+    back_rows = exchanged(back_rows)
     small = summed(small, ("row",))
     small = jnp.concatenate([small[:8], summed(small[8:], ("core", "side"))], axis=0)
-    back_rows = exchanged(input_work.astype(BF16))
     back_rows, out_two, small, both_grad = tie(back_rows, out_two, small, both_grad)
     back_one = line_step((back_rows, back_rows), 1)
     out_three = line_step(out_two, 3)

time: 772 us -> 770 us (level)
  waiting for transfers between devices: 276 us -> 256 us
  local copies, waits for them, and re-layouts: 41.1 us -> 50.4 us
    ppermute x6, waiting for transfers between devices: 38.6 us -> 0.02 us  [crossed(): return lax.ppermute(v, ('side', 'core', 'tensor'), pairs)]
    ppermute x12, waiting for transfers between devices: 107 us -> 128 us  [line_step(): lax.ppermute(right, 'tensor', [(i + 1, i) for i in range(0, 4 - j)])]
    ppermute x37 -> x38, waiting for transfers between devices: 69.3 us -> 84.4 us  [swap(): return lax.ppermute(v, axis, [(i, i ^ mask) for i in range(count)])]
    ppermute x12, waiting for transfers between devices: 58.1 us -> 44.1 us  [line_step(): lax.ppermute(left, 'tensor', [(i, i + 1) for i in range(j - 1, 3)])]
    ppermute x37 -> x38, starting transfers between devices: 43.6 us -> 45.1 us  [swap(): return lax.ppermute(v, axis, [(i, i ^ mask) for i in range(count)])]
    unnamed x139 -> x131, local copies, waits for them, and re-layouts: 18.6 us -> 17.1 us
  transfers between devices with their start and end apart: 69 -> 70, of which waited for: 26 -> 23; matrix products, arithmetic and copies ran while one was open for 24% -> 26% of each run, Pallas kernels for 10% -> 10%
where the time goes in v6:
time: 770 us; the launch traced here: 763 us
  waiting for transfers between devices  256 us (33%)
  matrix products  148 us (19%)
  starting transfers between devices  141 us (18%)
  Pallas kernels  77.5 us (10%)
  other arithmetic  69 us (9%)
  local copies, waits for them, and re-layouts  50.4 us (7%)
  between operations  21.1 us (3%)
    ppermute x12, waiting for transfers between devices, line_step(): lax.ppermute(right, 'tensor', [(i + 1, i) for i in range(0, 4 - j)])  128 us
    ppermute x38, waiting for transfers between devices, swap(): return lax.ppermute(v, axis, [(i, i ^ mask) for i in range(count)])  84.4 us
    pallas_call x1, Pallas kernels, mixer_backward(): pl.pallas_call(backward_kernel, grid_spec=pltpu.PrefetchScalarGridSpec(nu...  51.7 us
    ppermute x38, starting transfers between devices, swap(): return lax.ppermute(v, axis, [(i, i ^ mask) for i in range(count)])  45.1 us
    ppermute x12, waiting for transfers between devices, line_step(): lax.ppermute(left, 'tensor', [(i, i + 1) for i in range(j - 1, 3)])  44.1 us
    ppermute x6, starting transfers between devices, crossed(): return lax.ppermute(v, ('side', 'core', 'tensor'), pairs)  38.6 us
    dot_general x4, matrix products, settled(): jnp.dot(where.astype(BF16), jnp.concatenate(held), preferred_element_type...  35.3 us
    dot_general x13, matrix products, contract_columns(): lax.dot_general(a, b, (((1,), (1,)), ((), ())), preferred_element_type=F32)  31.5 us
  transfers between devices with their start and end apart: 70, of which 23 were waited for; matrix products, arithmetic and copies ran while one was open for 26% of the time, Pallas kernels for 10%

profile of v6, /device:TPU:1, one launch (start us, length us, event | category | flops | bytes accessed | tf_op | source)
XLA Modules:
  0.0 763.4 jit_solution(13940442166309395676)
XLA Ops:
  49.7 8.4 %collective-permute-start.13 = (bf16[512,1536]{1,0:T(8,128)(2,1)}, bf16[512,1536]{1,0:T(8,128)(2,1)}, u32[]{:S(2)}, u32[]{:S(2)}) collective-permute-start(bf16[512,1536]{1,0:T(8,128)(2,1)} %fusion.20), channel_id=1, source_target_pairs={{0,8},{8,0},{1,9},{9,1},{2,10},{10,2},{3,11},{11,3},{4,12},{12,4},... | collective-permute-start | bytes 4718600 | tf_op jit(solution)/shard_map/ppermute | solution.py:362
  71.8 11.2 %collective-permute-start.14 = (bf16[192,1536]{1,0:T(8,128)(2,1)}, bf16[192,1536]{1,0:T(8,128)(2,1)}, u32[]{:S(2)}, u32[]{:S(2)}) collective-permute-start(bf16[192,1536]{1,0:T(8,128)(2,1)} %pad_maximum_fusion.7), channel_id=1, source_target_pairs={{0,0},{1,4},{2,8},{3,12},{4,1},{5,5},{6,9},{7,13},{8,2},{9,6},{10,... | collective-permute-start | bytes 1769480 | tf_op jit(solution)/shard_map/ppermute | solution.py:367
  94.7 10.3 %collective-permute-start = (f32[8,768]{1,0:T(8,128)S(1)}, f32[8,768]{1,0:T(8,128)S(1)}, u32[]{:S(2)}, u32[]{:S(2)}) collective-permute-start(f32[8,768]{1,0:T(8,128)S(1)} %concatenate.77), channel_id=1, source_target_pairs={{0,0},{1,4},{2,8},{3,12},{4,1},{5,5},{6,9},{7,13},{8,2},{9,6},{10,... | collective-permute-start | bytes 73736 | tf_op jit(solution)/shard_map/ppermute | solution.py:367
  105.0 8.0 %collective-permute-done.12 = bf16[192,1152]{1,0:T(8,128)(2,1)} collective-permute-done((bf16[192,1152]{1,0:T(8,128)(2,1)}, bf16[192,1152]{1,0:T(8,128)(2,1)}, u32[]{:S(2)}, u32[]{:S(2)}) %collective-permute-start.12) | collective-permute-done | bytes 442400 | tf_op jit(solution)/shard_map/ppermute | solution.py:389
  128.9 9.3 %collective-permute-done.16 = bf16[192,1152]{1,0:T(8,128)(2,1)S(1)} collective-permute-done((bf16[192,1152]{1,0:T(8,128)(2,1)S(1)}, bf16[192,1152]{1,0:T(8,128)(2,1)S(1)}, u32[]{:S(2)}, u32[]{:S(2)}) %collective-permute-start.16) | collective-permute-done | bytes 442400 | tf_op jit(solution)/shard_map/ppermute | solution.py:362
  142.5 12.7 %collective-permute-start.21 = (bf16[192,1536]{1,0:T(8,128)(2,1)S(1)}, bf16[192,1536]{1,0:T(8,128)(2,1)}, u32[]{:S(2)}, u32[]{:S(2)}) collective-permute-start(bf16[192,1536]{1,0:T(8,128)(2,1)S(1)} %collective-permute-done.19), channel_id=1, source_target_pairs={{1,0},{2,1},{5,4},{6,5},{9,8},{10,9},{13,12},{14,13},{17,16},{18,1... | collective-permute-start | bytes 1769480 | tf_op jit(solution)/shard_map/ppermute | solution.py:389
  162.8 16.4 %fusion.126.proj_ref.proj_before_ref = f32[2048,1152]{1,0:T(8,128)} fusion(bf16[1536,1152]{1,0:T(8,128)(2,1)S(1)} %constant_dynamic-update-slice_fusion.12, bf16[512,1536]{1,0:T(8,128)(2,1)} %collective-permute-done.17, bf16[512,1536]{1,0:T(8,128)(2,1)} %collective-permute-done.13, bf16[512,1536]{1,0:T(8,128)(2,1)} %collective-permute-done.5, ...), kind=kOutput, calls=%fused_computation.272 | convolution fusion | flops 7272923136 | bytes 19267584 | tf_op jit(solution)/shard_map/dot_general | solution.py:565
  185.7 25.8 %mixer_forward.1 = (f32[2048,768]{1,0:T(8,128)}, bf16[16,128,768]{2,1,0:T(8,128)(2,1)}) custom-call(s32[4]{0:T(128)} %fusion.114.lens_ref, s32[16]{0:T(128)} %fusion.111.order_ref, f32[2048,1152]{1,0:T(8,128)} %fusion.126.proj_ref.proj_before_ref, f32[4,768]{1,0:T(4,128)} %slice.348.fw_ref, f32[1,768]{1,0:T(1,128)} %get-tuple-element.310.fb_ref, ...), custom_call_target="tpu_custom_call" | custom-call | flops 20000000000 | bytes 30000000 | tf_op jit(solution)/shard_map/mixer_forward/pallas_call | solution.py:292
  232.5 11.4 %fusion.71 = f32[2048,768]{1,0:T(8,128)S(1)} fusion(bf16[1536,1536]{1,0:T(8,128)(2,1)S(1)} %constant_dynamic-update-slice_fusion.4, bf16[512,1536]{1,0:T(8,128)(2,1)} %collective-permute-done.17, bf16[512,1536]{1,0:T(8,128)(2,1)} %collective-permute-done.13, bf16[512,1536]{1,0:T(8,128)(2,1)} %collective-permute-done.5, bf16[512,1536]{1,0:T(8,128)(2,1)} %fusion.20), kind=kOutput, calls=%fused_computation.117 | convolution fusion | flops 4857004032 | bytes 14942208 | tf_op jit(solution)/shard_map/dot_general | solution.py:576
  245.2 10.5 %fusion.65 = f32[2048,768]{1,0:T(8,128)S(1)} fusion(bf16[2048,1536]{1,0:T(8,128)(2,1)} %constant_dynamic-update-slice_fusion, bf16[1536,1536]{1,0:T(8,128)(2,1)} %copy-done.5), kind=kOutput, calls=%fused_computation.111 | convolution fusion | flops 4831838208 | bytes 14942208 | tf_op jit(solution)/shard_map/dot_general | solution.py:577
  267.7 13.6 %multiply_convert_fusion.1 = (bf16[2048,768]{1,0:T(8,128)(2,1)S(1)}, f32[2048,768]{1,0:T(8,128)}, f32[768]{0:T(1024)S(1)}, bf16[2048,768]{1,0:T(8,128)(2,1)S(1)}) fusion(f32[2048,768]{1,0:T(8,128)} %copy-done, f32[2048,768]{1,0:T(8,128)} %get-tuple-element.175.out_ref, f32[2048]{0:T(1024)S(1)} %bitcast.64, f32[2048,768]{1,0:T(8,128)} %get-tuple-element.278, ...), kind=kLoop, calls=%fused_computation.16 | loop fusion | flops 36175104 | bytes 37779456 | tf_op jit(solution)/shard_map/convert_element_type | solution.py:595
  288.6 8.3 %convolution_convert_fusion.5 = bf16[1536,768]{0,1:T(8,128)(2,1)S(1)} fusion(bf16[2048,1536]{1,0:T(8,128)(2,1)} %constant_dynamic-update-slice_fusion, bf16[2048,768]{1,0:T(8,128)(2,1)S(1)} %get-tuple-element.284), kind=kOutput, calls=%fused_computation.42 | convolution fusion | flops 4833017856 | bytes 11796480 | tf_op jit(solution)/shard_map/dot_general | solution.py:431
  321.2 51.7 %mixer_backward.1 = (bf16[2048,896]{1,0:T(8,128)(2,1)}, f32[2048,256]{1,0:T(8,128)}, f32[8,768]{1,0:T(8,128)}, f32[8,256]{1,0:T(8,128)}, f32[8,128]{1,0:T(8,128)}) custom-call(s32[4]{0:T(128)} %fusion.114.lens_ref, s32[16]{0:T(128)} %fusion.111.order_ref, f32[2048,1152]{1,0:T(8,128)} %fusion.126.proj_ref.proj_before_ref, ...), custom_call_target="tpu_custom_call" | custom-call | flops 40000000000 | bytes 60000000 | tf_op jit(solution)/shard_map/mixer_backward/pallas_call | solution.py:327
  422.4 14.8 %convolution_convert_fusion.4 = bf16[1536,1152]{1,0:T(8,128)(2,1)} fusion(bf16[512,256]{1,0:T(8,128)(2,1)} %collective-permute-done.43, bf16[512,256]{1,0:T(8,128)(2,1)} %copy-done.49, bf16[512,256]{1,0:T(8,128)(2,1)} %copy-done.50, bf16[512,256]{1,0:T(8,128)(2,1)S(1)} %add_convert_fusion.2, bf16[2048,896]{1,0:T(8,128)(2,1)} %get-tuple-element.195, ...), kind=kOutput, calls=%fused_computation.6 | convolution fusion | flops 7298285568 | bytes 14548992 | tf_op jit(solution)/shard_map/dot_general | solution.py:431
  439.5 15.9 %collective-permute-done.44 = bf16[512,1536]{1,0:T(8,128)(2,1)} collective-permute-done((bf16[512,1536]{1,0:T(8,128)(2,1)}, bf16[512,1536]{1,0:T(8,128)(2,1)}, u32[]{:S(2)}, u32[]{:S(2)}) %collective-permute-start.44) | collective-permute-done | bytes 1572896 | tf_op jit(solution)/shard_map/ppermute | solution.py:388
  468.9 32.6 %collective-permute-done.51 = f32[12,768]{1,0:T(8,128)S(1)} collective-permute-done((f32[12,768]{1,0:T(8,128)S(1)}, f32[12,768]{1,0:T(8,128)S(1)}, u32[]{:S(2)}, u32[]{:S(2)}) %collective-permute-start.51) | collective-permute-done | bytes 36896 | tf_op jit(solution)/shard_map/ppermute | solution.py:362
  514.0 9.1 %collective-permute-done.48 = bf16[256,1536]{1,0:T(8,128)(2,1)S(1)} collective-permute-done((bf16[256,1536]{1,0:T(8,128)(2,1)}, bf16[256,1536]{1,0:T(8,128)(2,1)S(1)}, u32[]{:S(2)}, u32[]{:S(2)}) %collective-permute-start.48) | collective-permute-done | bytes 786464 | tf_op jit(solution)/shard_map/ppermute | solution.py:362
  542.4 24.2 %collective-permute-done.57 = bf16[512,1536]{1,0:T(8,128)(2,1)} collective-permute-done((bf16[512,1536]{1,0:T(8,128)(2,1)}, bf16[512,1536]{1,0:T(8,128)(2,1)}, u32[]{:S(2)}, u32[]{:S(2)}) %collective-permute-start.57) | collective-permute-done | bytes 1572896 | tf_op jit(solution)/shard_map/ppermute | solution.py:388
  568.4 39.0 %collective-permute-done.59 = bf16[512,1536]{1,0:T(8,128)(2,1)S(1)} collective-permute-done((bf16[512,1536]{1,0:T(8,128)(2,1)}, bf16[512,1536]{1,0:T(8,128)(2,1)S(1)}, u32[]{:S(2)}, u32[]{:S(2)}) %collective-permute-start.59) | collective-permute-done | bytes 1572896 | tf_op jit(solution)/shard_map/ppermute | solution.py:389
  609.0 10.0 %convolution_convert_fusion.1 = bf16[2048,1536]{1,0:T(8,128)(2,1)} fusion(bf16[512,1536]{1,0:T(8,128)(2,1)S(1)} %broadcast_select_fusion, bf16[512,1536]{1,0:T(8,128)(2,1)} %pad_maximum_fusion.5, pred[2048,512]{1,0:T(32,128)(4,1)S(1)} %get-tuple-element.330, pred[2048,512]{1,0:T(32,128)(4,1)S(1)} %get-tuple-element.331), kind=kOutput, calls=%fused_computation.3 | convolution fusion | flops 6453985280 | bytes 11534336 | tf_op jit(solution)/shard_map/dot_general | solution.py:563
  620.2 55.8 %collective-permute-done.60 = bf16[512,1536]{1,0:T(8,128)(2,1)} collective-permute-done((bf16[512,1536]{1,0:T(8,128)(2,1)S(1)}, bf16[512,1536]{1,0:T(8,128)(2,1)}, u32[]{:S(2)}, u32[]{:S(2)}) %collective-permute-start.60) | collective-permute-done | bytes 1572896 | tf_op jit(solution)/shard_map/ppermute | solution.py:389
  693.0 10.0 %fusion.1 = bf16[2048,1536]{1,0:T(8,128)(2,1)} fusion(bf16[2048,1536]{1,0:T(8,128)(2,1)S(1)} %convolution_convert_fusion.2, bf16[512,1536]{1,0:T(8,128)(2,1)S(1)} %get-tuple-element.289, bf16[512,1536]{1,0:T(8,128)(2,1)} %pad_maximum_fusion.4, pred[2048,512]{1,0:T(32,128)(4,1)S(1)} %copy-done.22, pred[2048,512]{1,0:T(32,128)(4,1)S(1)} %copy-done.24), kind=kOutput, calls=%fused_computation.22 | convolution fusion | flops 6457131008 | bytes 17825792 | tf_op jit(solution)/shard_map/dot_general | solution.py:563
  706.6 19.9 %collective-permute-done.63 = bf16[512,1536]{1,0:T(8,128)(2,1)} collective-permute-done((bf16[512,1536]{1,0:T(8,128)(2,1)}, bf16[512,1536]{1,0:T(8,128)(2,1)}, u32[]{:S(2)}, u32[]{:S(2)}) %collective-permute-start.63) | collective-permute-done | bytes 1572896 | tf_op jit(solution)/shard_map/ppermute | solution.py:389
  730.0 8.5 %convolution_convert_fusion = bf16[2048,1536]{1,0:T(8,128)(2,1)} fusion(bf16[512,1536]{1,0:T(8,128)(2,1)S(1)} %get-tuple-element.286, bf16[512,1536]{1,0:T(8,128)(2,1)S(1)} %get-tuple-element.285, pred[2048,512]{1,0:T(32,128)(4,1)S(1)} %copy-done.18, pred[2048,512]{1,0:T(32,128)(4,1)S(1)} %copy-done.20), kind=kOutput, calls=%fused_computation.2 | convolution fusion | flops 6453985280 | bytes 11534336 | tf_op jit(solution)/shard_map/dot_general | solution.py:563
  (414 shorter events, 304.8 us)
Async XLA Ops:
  7.2 430.0 %reduce-scatter.7.cloned.1.call-start = ((), (), s32[]{:S(2)}) async-start(), calls=%async_computation.2 | async-start | bytes 5308416
  49.7 45.0 %collective-permute-start.13 = (bf16[512,1536]{1,0:T(8,128)(2,1)}, bf16[512,1536]{1,0:T(8,128)(2,1)}, u32[]{:S(2)}, u32[]{:S(2)}) collective-permute-start(bf16[512,1536]{1,0:T(8,128)(2,1)} %fusion.20), channel_id=1, source_target_pairs={{0,8},{8,0},{1,9},{9,1},{2,10},{10,2},{3,11},{11,3},{4,12},{12,4},... | collective-permute-start | bytes 4718600 | tf_op jit(solution)/shard_map/ppermute | solution.py:362
  128.5 51.4 %collective-permute-start.24 = (bf16[512,1536]{1,0:T(8,128)(2,1)S(1)}, bf16[512,1536]{1,0:T(8,128)(2,1)S(1)}, u32[]{:S(2)}, u32[]{:S(2)}) collective-permute-start(bf16[512,1536]{1,0:T(8,128)(2,1)S(1)} %pad_maximum_fusion.3), channel_id=1, source_target_pairs={{0,4},{4,0},{1,5},{5,1},{2,6},{6,2},{3,7},{7,3},{8,12},{12,8},{9,1... | collective-permute-start | bytes 4718600 | tf_op jit(solution)/shard_map/ppermute | solution.py:362
  138.2 41.0 %collective-permute-start.22 = (bf16[192,1536]{1,0:T(8,128)(2,1)}, bf16[192,1536]{1,0:T(8,128)(2,1)S(1)}, u32[]{:S(2)}, u32[]{:S(2)}) collective-permute-start(bf16[192,1536]{1,0:T(8,128)(2,1)} %collective-permute-done.14), channel_id=1, source_target_pairs={{0,16},{16,0},{1,17},{17,1},{2,18},{18,2},{3,19},{19,3},{4,20},{20... | collective-permute-start | bytes 1769480 | tf_op jit(solution)/shard_map/ppermute | solution.py:362
  140.9 39.0 %collective-permute-start.20 = (bf16[192,1536]{1,0:T(8,128)(2,1)S(1)}, bf16[192,1536]{1,0:T(8,128)(2,1)}, u32[]{:S(2)}, u32[]{:S(2)}) collective-permute-start(bf16[192,1536]{1,0:T(8,128)(2,1)S(1)} %collective-permute-done.18), channel_id=1, source_target_pairs={{1,2},{2,3},{5,6},{6,7},{9,10},{10,11},{13,14},{14,15},{17,18},{18... | collective-permute-start | bytes 1769480 | tf_op jit(solution)/shard_map/ppermute | solution.py:388
  142.5 37.4 %collective-permute-start.21 = (bf16[192,1536]{1,0:T(8,128)(2,1)S(1)}, bf16[192,1536]{1,0:T(8,128)(2,1)}, u32[]{:S(2)}, u32[]{:S(2)}) collective-permute-start(bf16[192,1536]{1,0:T(8,128)(2,1)S(1)} %collective-permute-done.19), channel_id=1, source_target_pairs={{1,0},{2,1},{5,4},{6,5},{9,8},{10,9},{13,12},{14,13},{17,16},{18,1... | collective-permute-start | bytes 1769480 | tf_op jit(solution)/shard_map/ppermute | solution.py:389
  179.2 34.8 %collective-permute-start.28 = (bf16[512,1536]{1,0:T(8,128)(2,1)S(1)}, bf16[512,1536]{1,0:T(8,128)(2,1)}, u32[]{:S(2)}, u32[]{:S(2)}) collective-permute-start(bf16[512,1536]{1,0:T(8,128)(2,1)S(1)} %pad_maximum_fusion.3), channel_id=1, source_target_pairs={{0,8},{8,0},{1,9},{9,1},{2,10},{10,2},{3,11},{11,3},{4,12},{12,4},... | collective-permute-start | bytes 4718600 | tf_op jit(solution)/shard_map/ppermute | solution.py:362
  179.9 34.2 %collective-permute-start.25 = (bf16[192,1536]{1,0:T(8,128)(2,1)}, bf16[192,1536]{1,0:T(8,128)(2,1)}, u32[]{:S(2)}, u32[]{:S(2)}) collective-permute-start(bf16[192,1536]{1,0:T(8,128)(2,1)} %collective-permute-done.20), channel_id=1, source_target_pairs={{2,3},{6,7},{10,11},{14,15},{18,19},{22,23},{26,27},{30,31}} | collective-permute-start | bytes 1769480 | tf_op jit(solution)/shard_map/ppermute | solution.py:388
  314.1 61.3 %collective-permute-start.35 = (bf16[512,1536]{1,0:T(8,128)(2,1)}, bf16[512,1536]{1,0:T(8,128)(2,1)S(1)}, u32[]{:S(2)}, u32[]{:S(2)}) collective-permute-start(bf16[512,1536]{1,0:T(8,128)(2,1)} %fusion.45), channel_id=1, source_target_pairs={{0,8},{8,0},{1,9},{9,1},{2,10},{10,2},{3,11},{11,3},{4,12},{12,4},... | collective-permute-start | bytes 4718600 | tf_op jit(solution)/shard_map/ppermute | solution.py:362
  321.2 297.8 %reduce-scatter.9.cloned.1.call-start = ((), (), s32[]{:S(2)}) async-start(), calls=%async_computation.3 | async-start | bytes 2211840
  403.7 51.7 %collective-permute-start.44 = (bf16[512,1536]{1,0:T(8,128)(2,1)}, bf16[512,1536]{1,0:T(8,128)(2,1)}, u32[]{:S(2)}, u32[]{:S(2)}) collective-permute-start(bf16[512,1536]{1,0:T(8,128)(2,1)} %pad_maximum_fusion.4), channel_id=1, source_target_pairs={{0,1},{1,2},{2,3},{4,5},{5,6},{6,7},{8,9},{9,10},{10,11},{12,13},{... | collective-permute-start | bytes 4718600 | tf_op jit(solution)/shard_map/ppermute | solution.py:388
  410.4 47.2 %collective-permute-start.45 = (bf16[512,1536]{1,0:T(8,128)(2,1)}, bf16[512,1536]{1,0:T(8,128)(2,1)}, u32[]{:S(2)}, u32[]{:S(2)}) collective-permute-start(bf16[512,1536]{1,0:T(8,128)(2,1)} %pad_maximum_fusion.4), channel_id=1, source_target_pairs={{1,0},{2,1},{3,2},{5,4},{6,5},{7,6},{9,8},{10,9},{11,10},{13,12},{... | collective-permute-start | bytes 4718600 | tf_op jit(solution)/shard_map/ppermute | solution.py:389
  418.3 43.4 %collective-permute-start.47 = (bf16[512,1536]{1,0:T(8,128)(2,1)}, bf16[512,1536]{1,0:T(8,128)(2,1)S(1)}, u32[]{:S(2)}, u32[]{:S(2)}) collective-permute-start(bf16[512,1536]{1,0:T(8,128)(2,1)} %fusion.46), channel_id=1, source_target_pairs={{0,8},{8,0},{1,9},{9,1},{2,10},{10,2},{3,11},{11,3},{4,12},{12,4},... | collective-permute-start | bytes 4718600 | tf_op jit(solution)/shard_map/ppermute | solution.py:362
  460.4 69.4 %collective-permute-start.61 = (bf16[768,1152]{1,0:T(8,128)(2,1)}, bf16[768,1152]{1,0:T(8,128)(2,1)}, u32[]{:S(2)}, u32[]{:S(2)}) collective-permute-start(bf16[768,1152]{1,0:T(8,128)(2,1)} %constant_dynamic-slice_fusion), channel_id=1, source_target_pairs={{0,16},{16,0},{1,17},{17,1},{2,18},{18,2},{3,19},{19,3},{4,20},{20... | collective-permute-start | bytes 5308424 | tf_op jit(solution)/shard_map/ppermute | solution.py:362
  465.3 36.3 %collective-permute-start.51 = (f32[12,768]{1,0:T(8,128)S(1)}, f32[12,768]{1,0:T(8,128)S(1)}, u32[]{:S(2)}, u32[]{:S(2)}) collective-permute-start(f32[12,768]{1,0:T(8,128)S(1)} %concatenate.92), channel_id=1, source_target_pairs={{0,16},{16,0},{1,17},{17,1},{2,18},{18,2},{3,19},{19,3},{4,20},{20... | collective-permute-start | bytes 110600 | tf_op jit(solution)/shard_map/ppermute | solution.py:362
  465.7 58.7 %collective-permute-start.49 = (bf16[512,1536]{1,0:T(8,128)(2,1)}, bf16[512,1536]{1,0:T(8,128)(2,1)}, u32[]{:S(2)}, u32[]{:S(2)}) collective-permute-start(bf16[512,1536]{1,0:T(8,128)(2,1)} %collective-permute-done.44), channel_id=1, source_target_pairs={{1,2},{2,3},{5,6},{6,7},{9,10},{10,11},{13,14},{14,15},{17,18},{18... | collective-permute-start | bytes 4718600 | tf_op jit(solution)/shard_map/ppermute | solution.py:388
  467.6 56.8 %collective-permute-start.50 = (bf16[512,1536]{1,0:T(8,128)(2,1)}, bf16[512,1536]{1,0:T(8,128)(2,1)}, u32[]{:S(2)}, u32[]{:S(2)}) collective-permute-start(bf16[512,1536]{1,0:T(8,128)(2,1)} %collective-permute-done.45), channel_id=1, source_target_pairs={{1,0},{2,1},{5,4},{6,5},{9,8},{10,9},{13,12},{14,13},{17,16},{18,1... | collective-permute-start | bytes 4718600 | tf_op jit(solution)/shard_map/ppermute | solution.py:389
  524.4 42.2 %collective-permute-start.57 = (bf16[512,1536]{1,0:T(8,128)(2,1)}, bf16[512,1536]{1,0:T(8,128)(2,1)}, u32[]{:S(2)}, u32[]{:S(2)}) collective-permute-start(bf16[512,1536]{1,0:T(8,128)(2,1)} %pad_maximum_fusion.5), channel_id=1, source_target_pairs={{0,1},{1,2},{2,3},{4,5},{5,6},{6,7},{8,9},{9,10},{10,11},{12,13},{... | collective-permute-start | bytes 4718600 | tf_op jit(solution)/shard_map/ppermute | solution.py:388
  528.6 78.9 %collective-permute-start.59 = (bf16[512,1536]{1,0:T(8,128)(2,1)}, bf16[512,1536]{1,0:T(8,128)(2,1)S(1)}, u32[]{:S(2)}, u32[]{:S(2)}) collective-permute-start(bf16[512,1536]{1,0:T(8,128)(2,1)} %pad_maximum_fusion.5), channel_id=1, source_target_pairs={{1,0},{2,1},{3,2},{5,4},{6,5},{7,6},{9,8},{10,9},{11,10},{13,12},{... | collective-permute-start | bytes 4718600 | tf_op jit(solution)/shard_map/ppermute | solution.py:389
  538.4 144.0 %collective-permute-start.55 = (bf16[512,1536]{1,0:T(8,128)(2,1)}, bf16[512,1536]{1,0:T(8,128)(2,1)}, u32[]{:S(2)}, u32[]{:S(2)}) collective-permute-start(bf16[512,1536]{1,0:T(8,128)(2,1)} %collective-permute-done.49), channel_id=1, source_target_pairs={{2,3},{6,7},{10,11},{14,15},{18,19},{22,23},{26,27},{30,31}} | collective-permute-start | bytes 4718600 | tf_op jit(solution)/shard_map/ppermute | solution.py:388
  540.3 142.1 %collective-permute-start.56 = (bf16[512,1536]{1,0:T(8,128)(2,1)}, bf16[512,1536]{1,0:T(8,128)(2,1)}, u32[]{:S(2)}, u32[]{:S(2)}) collective-permute-start(bf16[512,1536]{1,0:T(8,128)(2,1)} %collective-permute-done.50), channel_id=1, source_target_pairs={{1,0},{5,4},{9,8},{13,12},{17,16},{21,20},{25,24},{29,28}} | collective-permute-start | bytes 4718600 | tf_op jit(solution)/shard_map/ppermute | solution.py:389
  566.6 53.6 %collective-permute-start.58 = (bf16[512,1536]{1,0:T(8,128)(2,1)}, bf16[512,1536]{1,0:T(8,128)(2,1)}, u32[]{:S(2)}, u32[]{:S(2)}) collective-permute-start(bf16[512,1536]{1,0:T(8,128)(2,1)} %collective-permute-done.57), channel_id=1, source_target_pairs={{1,2},{2,3},{5,6},{6,7},{9,10},{10,11},{13,14},{14,15},{17,18},{18... | collective-permute-start | bytes 4718600 | tf_op jit(solution)/shard_map/ppermute | solution.py:388
  607.4 68.5 %collective-permute-start.60 = (bf16[512,1536]{1,0:T(8,128)(2,1)S(1)}, bf16[512,1536]{1,0:T(8,128)(2,1)}, u32[]{:S(2)}, u32[]{:S(2)}) collective-permute-start(bf16[512,1536]{1,0:T(8,128)(2,1)S(1)} %collective-permute-done.59), channel_id=1, source_target_pairs={{1,0},{2,1},{5,4},{6,5},{9,8},{10,9},{13,12},{14,13},{17,16},{18,1... | collective-permute-start | bytes 4718600 | tf_op jit(solution)/shard_map/ppermute | solution.py:389
  680.9 45.5 %collective-permute-start.63 = (bf16[512,1536]{1,0:T(8,128)(2,1)}, bf16[512,1536]{1,0:T(8,128)(2,1)}, u32[]{:S(2)}, u32[]{:S(2)}) collective-permute-start(bf16[512,1536]{1,0:T(8,128)(2,1)} %collective-permute-done.60), channel_id=1, source_target_pairs={{1,0},{5,4},{9,8},{13,12},{17,16},{21,20},{25,24},{29,28}} | collective-permute-start | bytes 4718600 | tf_op jit(solution)/shard_map/ppermute | solution.py:389
  (107 other events, 1956.4 us)
Sparse Core Ops, SparseCore 0:
  321.3 113.0 reduce-scatter.6
  533.7 75.8 reduce-scatter.8

commit v7 on v6

--- a/solution.py
+++ b/solution.py
@@ -1,3 +1,5 @@
+import functools
+
 import jax
 import jax.numpy as jnp
 from jax import lax
@@ -143,25 +145,24 @@
 
 
 def backward_kernel(
-    lens_ref, order_ref, proj_ref, proj_before_ref, grad_ref, out_ref, kept_ref,
+    first_chunk, lens_ref, order_ref, proj_ref, proj_before_ref, grad_ref, out_ref, kept_ref,
     fw_ref, fb_ref, sf_ref, sb_ref, head_ref, skip_ref, spread_ref,
-    proj_grad_ref, shared_grad_ref, fsum_ref, ssum_ref, hsum_ref,
-    memory_grad, after, shared_after,
+    memory_from, after_from, shared_after_from, proj_grad_from, shared_grad_from,
+    proj_grad_ref, shared_grad_ref, fsum_ref, ssum_ref, hsum_ref, memory_grad, after, shared_after,
 ):
     step = pl.program_id(0)
-    steps = pl.num_programs(0)
     span = proj_ref.shape[0]
     width = out_ref.shape[1]
     reach = fw_ref.shape[0]
     pairs = width // LANES
-    chunk = steps - 1 - step
+    chunk = first_chunk - step
     base = chunk * span
 
     @pl.when(step == 0)
     def _():
-        memory_grad[...] = jnp.zeros_like(memory_grad)
-        after[...] = jnp.zeros_like(after)
-        shared_after[...] = jnp.zeros_like(shared_after)
+        memory_grad[...] = memory_from[...]
+        after[...] = after_from[...]
+        shared_after[...] = shared_after_from[...]
         fsum_ref[...] = jnp.zeros_like(fsum_ref)
         ssum_ref[...] = jnp.zeros_like(ssum_ref)
         hsum_ref[...] = jnp.zeros_like(hsum_ref)
@@ -314,47 +315,57 @@
     )(lens, order, proj, fw, fb, sf, sb, table, skip, spread)
 
 
-def mixer_backward(lens, order, proj, grad, out, kept, fw, fb, sf, sb, table, skip, spread):
+def mixer_backward(half, carried, lens, order, proj, grad, out, kept, fw, fb, sf, sb, table, skip, spread):
     rows = proj.shape[0]
     width = fw.shape[1]
-    steps = rows // SPAN
+    steps = rows // SPAN // 2
+    first_chunk = (2 - half) * steps - 1
     lead = SPAN // HALO
-    block = lambda cols: pl.BlockSpec((SPAN, cols), lambda i, lens_ref, order_ref: (order_ref[steps - 1 - i], 0))
+    block = lambda cols: pl.BlockSpec((SPAN, cols), lambda i, lens_ref, order_ref: (order_ref[first_chunk - i], 0))
     ahead = lambda cols: pl.BlockSpec(
         (HALO, cols),
-        lambda i, lens_ref, order_ref: (order_ref[jnp.maximum(steps - 2 - i, 0)] * lead + lead - 1, 0),
-    )
+        lambda i, lens_ref, order_ref: (order_ref[jnp.maximum(first_chunk - 1 - i, 0)] * lead + lead - 1, 0),
+    )
+    anywhere = pl.BlockSpec(memory_space=pl.ANY)
+    out_shape = [
+        jax.ShapeDtypeStruct((rows, width + LANES), BF16),
+        jax.ShapeDtypeStruct((rows, sf.shape[1]), F32),
+        jax.ShapeDtypeStruct((8, width), F32),
+        jax.ShapeDtypeStruct((8, sf.shape[1]), F32),
+        jax.ShapeDtypeStruct((8, LANES), F32),
+        jax.ShapeDtypeStruct((LANES, width), F32),
+        jax.ShapeDtypeStruct((HALO, width), F32),
+        jax.ShapeDtypeStruct((HALO, sf.shape[1]), F32),
+    ]
+    if carried is None:
+        carried = [jnp.zeros(v.shape, F32) for v in out_shape[5:]] + [jnp.zeros((8, LANES), F32)] * 2
+        aliases = {}
+    else:
+        aliases = {17: 0, 18: 1}
     return pl.pallas_call(
-        backward_kernel,
+        functools.partial(backward_kernel, first_chunk),
         grid_spec=pltpu.PrefetchScalarGridSpec(
             num_scalar_prefetch=2,
             grid=(steps,),
             in_specs=[
                 block(proj.shape[1]), ahead(proj.shape[1]),
-                block(width), block(width), pl.BlockSpec((1, LANES, width), lambda i, *_: (steps - 1 - i, 0, 0)),
+                block(width), block(width),
+                pl.BlockSpec((1, LANES, width), lambda i, *_: (first_chunk - i, 0, 0)),
                 fixed(fw.shape), fixed(fb.shape), fixed(sf.shape),
                 fixed(sb.shape), fixed(table.shape), fixed(skip.shape), fixed(spread.shape),
+                fixed((LANES, width)), fixed((HALO, width)), fixed((HALO, sf.shape[1])), anywhere, anywhere,
             ],
             out_specs=[
                 block(width + LANES), block(sf.shape[1]),
                 fixed((8, width)), fixed((8, sf.shape[1])), fixed((8, LANES)),
-            ],
-            scratch_shapes=[
-                pltpu.VMEM((LANES, width), F32),
-                pltpu.VMEM((HALO, width), F32),
-                pltpu.VMEM((HALO, sf.shape[1]), F32),
+                fixed((LANES, width)), fixed((HALO, width)), fixed((HALO, sf.shape[1])),
             ],
         ),
-        out_shape=[
-            jax.ShapeDtypeStruct((rows, width + LANES), BF16),
-            jax.ShapeDtypeStruct((rows, sf.shape[1]), F32),
-            jax.ShapeDtypeStruct((8, width), F32),
-            jax.ShapeDtypeStruct((8, sf.shape[1]), F32),
-            jax.ShapeDtypeStruct((8, LANES), F32),
-        ],
-        cost_estimate=pl.CostEstimate(flops=40 * 10**9, bytes_accessed=60 * 10**6, transcendentals=0),
+        out_shape=out_shape,
+        input_output_aliases=aliases,
+        cost_estimate=pl.CostEstimate(flops=20 * 10**9, bytes_accessed=30 * 10**6, transcendentals=0),
         name="mixer_backward",
-    )(lens, order, proj, proj, grad, out, kept, fw, fb, sf, sb, table, skip, spread)
+    )(lens, order, proj, proj, grad, out, kept, fw, fb, sf, sb, table, skip, spread, *carried)
 
 
 def swap(v, axis, mask=1):
@@ -499,7 +510,6 @@
     in_slots = in_slots + [row_doubling(slot_three(two, three))]
     far = swap(beside, "core")
     one = line_step((gate_piece, gate_piece), 1)
-    cot_beside, cot_near = swap(own_cot, "side"), swap(own_cot, "core")
     in_slots, far, one = tie(in_slots, far, one)
     two = line_step(one, 2)
     gate_slots = [row_doubling(gate_piece), row_doubling(slot_one(one))]
@@ -563,7 +573,8 @@
         return jnp.dot(where.astype(BF16), jnp.concatenate(held), preferred_element_type=F32).astype(BF16)
 
     proj = jnp.dot(normed, in_full, preferred_element_type=F32)
-    proj, two, gate_slots, cot_near = tie(proj, two, gate_slots, cot_near)
+    proj, two, gate_slots, own_cot = tie(proj, two, gate_slots, own_cot)
+    cot_beside, cot_near = swap(own_cot, "side"), swap(own_cot, "core")
     three = line_step(two, 3)
     gate_slots = gate_slots + [row_doubling(slot_two(one, two))]
     proj = sequenced(proj)
@@ -598,12 +609,17 @@
     mixed_grad, both_grad, sent, own_rows = lax.optimization_barrier((mixed_grad, both_grad, sent, own_rows))
     arrived = swap(sent, "side")
     both_grad = lax.psum_scatter(both_grad, ("row", "tensor"), scatter_dimension=0, tiled=True)
-    proj_grad, shared_part, fsum, ssum, hsum = mixer_backward(
-        lens, order, proj, sequenced(mixed_grad), mixed_seq, kept, fw, fb, sf, sb, table, skip, spread
-    )
+    shared_inputs = (lens, order, proj, sequenced(mixed_grad), mixed_seq, kept, fw, fb, sf, sb, table, skip, spread)
+    proj_grad, shared_part, *sums_late, memory, after, shared_after = mixer_backward(0, None, *shared_inputs)
+    memory, arrived = tie(memory, arrived)
+    out_rows = exchanged((own_rows + arrived.astype(F32)).astype(BF16))
+    proj_grad, shared_part, *sums_early, _, _, _ = mixer_backward(
+        1, [memory, after, shared_after, proj_grad, shared_part], *shared_inputs
+    )
+    fsum, ssum, hsum = (a + b for a, b in zip(sums_late, sums_early))
     proj_grad, shared_part = unsequenced(proj_grad), unsequenced(shared_part)
-    proj_grad, shared_part, arrived = lax.optimization_barrier((proj_grad, shared_part, arrived))
-    out_rows = exchanged((own_rows + arrived.astype(F32)).astype(BF16))
+    proj_grad, shared_part, out_rows = tie(proj_grad, shared_part, out_rows)
+    out_one = line_step((out_rows, out_rows), 1)
 
     def back_part(grads, dx, dk):
         gate_part, proj_part = grads
@@ -615,16 +631,16 @@
     own_shared = group_sum((shared_far, shared_side, shared_near, shared_own)).astype(BF16)
     far = swap(back_part((gate_in_grad, proj_grad), 1, 1).astype(BF16), "core")
     near = swap(back_part((gate_in_grad, proj_grad), 0, 1).astype(BF16), "core")
-    far, gate_later, proj_later, out_rows = lax.optimization_barrier((far, gate_in_grad, proj_grad, out_rows))
-    out_one = line_step((out_rows, out_rows), 1)
+    far, gate_later, proj_later = tie(far, gate_in_grad, proj_grad)
     sent = (back_part((gate_later, proj_later), 1, 0) + far.astype(F32)).astype(BF16)
     own_back = back_part((gate_later, proj_later), 0, 0) + near.astype(F32)
     beside = swap(sent, "side")
+    proj_later, out_one = tie(proj_later, out_one)
     in_grad = contract_rows(normed, jnp.concatenate([proj_later, gathered(own_shared)], axis=1)).astype(BF16)
-    in_grad, out_one, both_grad, own_back = lax.optimization_barrier((in_grad, out_one, both_grad, own_back))
     out_two = line_step(out_one, 2)
+    in_grad, both_grad, own_back = tie(in_grad, both_grad, own_back)
+    beside, out_two = tie(beside, out_two)
     both_grad = crossed(both_grad)
-    in_grad = lax.psum_scatter(row_scattered(in_grad), "tensor", scatter_dimension=0, tiled=True)
     normed_back = own_back + beside.astype(F32) + contract_columns(own_shared, in_full[:, width + LANES :])
     norm_gain_grad = jnp.sum(normed_back * hidden * scale, axis=0)
     gained = normed_back * norm_gain
@@ -643,11 +659,11 @@
         ],
         axis=0,
     )
-    back_rows, small = tie(input_work.astype(BF16), small)
-    back_rows = exchanged(back_rows)
+    back_rows = exchanged(input_work.astype(BF16))
     small = summed(small, ("row",))
     small = jnp.concatenate([small[:8], summed(small[8:], ("core", "side"))], axis=0)
-    back_rows, out_two, small, both_grad = tie(back_rows, out_two, small, both_grad)
+    back_rows, out_two, small, both_grad, in_grad = tie(back_rows, out_two, small, both_grad, in_grad)
+    in_grad = lax.psum_scatter(row_scattered(in_grad), "tensor", scatter_dimension=0, tiled=True)
     back_one = line_step((back_rows, back_rows), 1)
     out_three = line_step(out_two, 3)
     back_two = line_step(back_one, 2)

time: 770 us -> 789 us (1.025)
  starting transfers between devices: 141 us -> 121 us
  waiting for transfers between devices: 256 us -> 274 us
  other arithmetic: 69 us -> 85.4 us
    unnamed x4, waiting for transfers between devices: 0.05 us -> 38.9 us
    ppermute x12, waiting for transfers between devices: 44.1 us -> 23.1 us  [line_step(): lax.ppermute(left, 'tensor', [(i, i + 1) for i in range(j - 1, 3)])]
    ppermute x12, waiting for transfers between devices: 128 us -> 108 us  [line_step(): lax.ppermute(right, 'tensor', [(i + 1, i) for i in range(0, 4 - j)])]
    ppermute x12, starting transfers between devices: 27.2 us -> 16.2 us  [line_step(): lax.ppermute(right, 'tensor', [(i + 1, i) for i in range(0, 4 - j)])]
    ppermute x38, waiting for transfers between devices: 84.4 us -> 94.5 us  [swap(): return lax.ppermute(v, axis, [(i, i ^ mask) for i in range(count)])]
    ppermute x6, waiting for transfers between devices: 0.02 us -> 9.68 us  [crossed(): return lax.ppermute(v, ('side', 'core', 'tensor'), pairs)]
    convert_element_type x1, other arithmetic: 13.6 us -> 21.8 us  [on_device(): (gated_grad * mixed * gate_sig * (1.0 + gate_in * (1.0 - gate_sig))).asty...]
    pallas_call x1 -> x2, Pallas kernels: 51.7 us -> 55.1 us  [mixer_backward(): pl.pallas_call(functools.partial(backward_kernel, first_chunk), grid_spec...]
  transfers between devices with their start and end apart: 70 -> 70, of which waited for: 23 -> 28; matrix products, arithmetic and copies ran while one was open for 26% -> 26% of each run, Pallas kernels for 10% -> 10%
where the time goes in v7:
time: 789 us; the launch traced here: 777 us
  waiting for transfers between devices  274 us (35%)
  matrix products  145 us (18%)
  starting transfers between devices  121 us (15%)
  other arithmetic  85.4 us (11%)
  Pallas kernels  80.9 us (10%)
  local copies, waits for them, and re-layouts  49.7 us (6%)
  between operations  21.5 us (3%)
    ppermute x12, waiting for transfers between devices, line_step(): lax.ppermute(right, 'tensor', [(i + 1, i) for i in range(0, 4 - j)])  108 us
    ppermute x38, waiting for transfers between devices, swap(): return lax.ppermute(v, axis, [(i, i ^ mask) for i in range(count)])  94.5 us
    pallas_call x2, Pallas kernels, mixer_backward(): pl.pallas_call(functools.partial(backward_kernel, first_chunk), grid_spec...  55.1 us
    ppermute x38, starting transfers between devices, swap(): return lax.ppermute(v, axis, [(i, i ^ mask) for i in range(count)])  43.1 us
    unnamed x4, waiting for transfers between devices  38.9 us
    ppermute x6, starting transfers between devices, crossed(): return lax.ppermute(v, ('side', 'core', 'tensor'), pairs)  34.3 us
    dot_general x4, matrix products, settled(): jnp.dot(where.astype(BF16), jnp.concatenate(held), preferred_element_type...  34.2 us
    dot_general x13, matrix products, contract_columns(): lax.dot_general(a, b, (((1,), (1,)), ((), ())), preferred_element_type=F32)  30.2 us
  transfers between devices with their start and end apart: 70, of which 28 were waited for; matrix products, arithmetic and copies ran while one was open for 26% of the time, Pallas kernels for 10%

profile of v7, /device:TPU:1, one launch (start us, length us, event | category | flops | bytes accessed | tf_op | source)
XLA Modules:
  0.0 777.1 jit_solution(1143699967067141481)
XLA Ops:
  73.0 10.0 %collective-permute-start.14 = (bf16[192,1536]{1,0:T(8,128)(2,1)}, bf16[192,1536]{1,0:T(8,128)(2,1)}, u32[]{:S(2)}, u32[]{:S(2)}) collective-permute-start(bf16[192,1536]{1,0:T(8,128)(2,1)} %pad_maximum_fusion.7), channel_id=1, source_target_pairs={{0,0},{1,4},{2,8},{3,12},{4,1},{5,5},{6,9},{7,13},{8,2},{9,6},{10,... | collective-permute-start | bytes 1769480 | tf_op jit(solution)/shard_map/ppermute | solution.py:378
  94.7 10.4 %collective-permute-start = (f32[8,768]{1,0:T(8,128)S(1)}, f32[8,768]{1,0:T(8,128)S(1)}, u32[]{:S(2)}, u32[]{:S(2)}) collective-permute-start(f32[8,768]{1,0:T(8,128)S(1)} %concatenate.77), channel_id=1, source_target_pairs={{0,0},{1,4},{2,8},{3,12},{4,1},{5,5},{6,9},{7,13},{8,2},{9,6},{10,... | collective-permute-start | bytes 73736 | tf_op jit(solution)/shard_map/ppermute | solution.py:378
  129.2 9.0 %collective-permute-done.16 = bf16[192,1152]{1,0:T(8,128)(2,1)S(1)} collective-permute-done((bf16[192,1152]{1,0:T(8,128)(2,1)S(1)}, bf16[192,1152]{1,0:T(8,128)(2,1)S(1)}, u32[]{:S(2)}, u32[]{:S(2)}) %collective-permute-start.16) | collective-permute-done | bytes 442400 | tf_op jit(solution)/shard_map/ppermute | solution.py:373
  151.7 16.4 %fusion.124.proj_ref.proj_before_ref = f32[2048,1152]{1,0:T(8,128)} fusion(bf16[1536,1152]{1,0:T(8,128)(2,1)S(1)} %constant_dynamic-update-slice_fusion.12, bf16[512,1536]{1,0:T(8,128)(2,1)} %collective-permute-done.17, bf16[512,1536]{1,0:T(8,128)(2,1)} %collective-permute-done.13, bf16[512,1536]{1,0:T(8,128)(2,1)} %collective-permute-done.5, ...), kind=kOutput, calls=%fused_computation.273 | convolution fusion | flops 7272923136 | bytes 19267584 | tf_op jit(solution)/shard_map/dot_general | solution.py:575
  176.0 25.8 %mixer_forward.1 = (f32[2048,768]{1,0:T(8,128)}, bf16[16,128,768]{2,1,0:T(8,128)(2,1)}) custom-call(s32[4]{0:T(128)} %fusion.112.lens_ref, s32[16]{0:T(128)} %fusion.109.order_ref, f32[2048,1152]{1,0:T(8,128)} %fusion.124.proj_ref.proj_before_ref, f32[4,768]{1,0:T(4,128)} %slice.348.fw_ref, f32[1,768]{1,0:T(1,128)} %get-tuple-element.335.fb_ref, ...), custom_call_target="tpu_custom_call" | custom-call | flops 20000000000 | bytes 30000000 | tf_op jit(solution)/shard_map/mixer_forward/pallas_call | solution.py:293
  225.0 11.4 %fusion.71 = f32[2048,768]{1,0:T(8,128)S(1)} fusion(bf16[1536,1536]{1,0:T(8,128)(2,1)S(1)} %constant_dynamic-update-slice_fusion.4, bf16[512,1536]{1,0:T(8,128)(2,1)} %collective-permute-done.17, bf16[512,1536]{1,0:T(8,128)(2,1)} %collective-permute-done.13, bf16[512,1536]{1,0:T(8,128)(2,1)} %collective-permute-done.5, bf16[512,1536]{1,0:T(8,128)(2,1)} %fusion.20), kind=kOutput, calls=%fused_computation.117 | convolution fusion | flops 4857004032 | bytes 14942208 | tf_op jit(solution)/shard_map/dot_general | solution.py:587
  237.7 10.5 %fusion.65 = f32[2048,768]{1,0:T(8,128)S(1)} fusion(bf16[2048,1536]{1,0:T(8,128)(2,1)} %constant_dynamic-update-slice_fusion, bf16[1536,1536]{1,0:T(8,128)(2,1)} %copy-done.4), kind=kOutput, calls=%fused_computation.111 | convolution fusion | flops 4831838208 | bytes 14942208 | tf_op jit(solution)/shard_map/dot_general | solution.py:588
  259.1 21.8 %multiply_convert_fusion.1 = (bf16[2048,768]{1,0:T(8,128)(2,1)S(1)}, f32[2048,768]{1,0:T(8,128)}, f32[768]{0:T(1024)S(1)}, bf16[2048,768]{1,0:T(8,128)(2,1)S(1)}) fusion(f32[2048,768]{1,0:T(8,128)} %copy-done, f32[2048,768]{1,0:T(8,128)} %get-tuple-element.188.out_ref, f32[2048]{0:T(1024)S(1)} %bitcast.62, f32[2048,768]{1,0:T(8,128)} %get-tuple-element.303, ...), kind=kLoop, calls=%fused_computation.16 | loop fusion | flops 36175104 | bytes 37779456 | tf_op jit(solution)/shard_map/convert_element_type | solution.py:606
  320.3 27.6 %mixer_backward.2 = (bf16[2048,896]{1,0:T(8,128)(2,1)}, f32[2048,256]{1,0:T(8,128)}, f32[8,768]{1,0:T(8,128)}, f32[8,256]{1,0:T(8,128)}, f32[8,128]{1,0:T(8,128)...) custom-call(s32[4]{0:T(128)} %fusion.112.lens_ref, s32[16]{0:T(128)} %fusion.109.order_ref, ...), custom_call_target="tpu_custom_call" | custom-call | flops 20000000000 | bytes 30000000 | tf_op jit(solution)/shard_map/mixer_backward/pallas_call | solution.py:345
  351.6 27.5 %mixer_backward.3 = (bf16[2048,896]{1,0:T(8,128)(2,1)}, f32[2048,256]{1,0:T(8,128)}, f32[8,768]{1,0:T(8,128)}, f32[8,256]{1,0:T(8,128)}, f32[8,128]{1,0:T(8,128)...) custom-call(s32[4]{0:T(128)} %fusion.112.lens_ref, ...), custom_call_target="tpu_custom_call", output_to_operand_aliasing={{0}: (17, {}), {1}: (18, {})} | custom-call | flops 20000000000 | bytes 30000000 | tf_op jit(solution)/shard_map/mixer_backward/pallas_call | solution.py:345
  420.2 19.0 %collective-permute-done.38 = bf16[512,1536]{1,0:T(8,128)(2,1)S(1)} collective-permute-done((bf16[512,1536]{1,0:T(8,128)(2,1)S(1)}, bf16[512,1536]{1,0:T(8,128)(2,1)S(1)}, u32[]{:S(2)}, u32[]{:S(2)}) %collective-permute-start.38) | collective-permute-done | bytes 1572896 | tf_op jit(solution)/shard_map/ppermute | solution.py:399
  453.3 14.3 %convolution_convert_fusion.3 = bf16[1536,1152]{1,0:T(8,128)(2,1)} fusion(bf16[512,256]{1,0:T(8,128)(2,1)} %collective-permute-done.45, bf16[512,256]{1,0:T(8,128)(2,1)} %copy-done.53, bf16[512,256]{1,0:T(8,128)(2,1)} %copy-done.54, bf16[512,256]{1,0:T(8,128)(2,1)S(1)} %add_convert_fusion.2, bf16[2048,896]{1,0:T(8,128)(2,1)} %get-tuple-element.216, ...), kind=kOutput, calls=%fused_computation.5 | convolution fusion | flops 7298285568 | bytes 14548992 | tf_op jit(solution)/shard_map/dot_general | solution.py:442
  473.6 12.2 %collective-permute-done.49 = bf16[512,1536]{1,0:T(8,128)(2,1)} collective-permute-done((bf16[512,1536]{1,0:T(8,128)(2,1)}, bf16[512,1536]{1,0:T(8,128)(2,1)}, u32[]{:S(2)}, u32[]{:S(2)}) %collective-permute-start.49) | collective-permute-done | bytes 1572896 | tf_op jit(solution)/shard_map/ppermute | solution.py:400
  495.1 15.4 %collective-permute-done.51 = f32[12,768]{1,0:T(8,128)S(1)} collective-permute-done((f32[12,768]{1,0:T(8,128)S(1)}, f32[12,768]{1,0:T(8,128)S(1)}, u32[]{:S(2)}, u32[]{:S(2)}) %collective-permute-start.51) | collective-permute-done | bytes 36896 | tf_op jit(solution)/shard_map/ppermute | solution.py:373
  522.3 9.7 %collective-permute-done.54 = bf16[192,1536]{1,0:T(8,128)(2,1)S(1)} collective-permute-done((bf16[192,1536]{1,0:T(8,128)(2,1)}, bf16[192,1536]{1,0:T(8,128)(2,1)S(1)}, u32[]{:S(2)}, u32[]{:S(2)}) %collective-permute-start.54) | collective-permute-done | bytes 589856 | tf_op jit(solution)/shard_map/ppermute | solution.py:378
  543.5 23.7 %collective-permute-done.61 = bf16[768,1152]{1,0:T(8,128)(2,1)S(1)} collective-permute-done((bf16[768,1152]{1,0:T(8,128)(2,1)}, bf16[768,1152]{1,0:T(8,128)(2,1)S(1)}, u32[]{:S(2)}, u32[]{:S(2)}) %collective-permute-start.61) | collective-permute-done | bytes 1769504 | tf_op jit(solution)/shard_map/ppermute | solution.py:373
  581.0 11.2 %collective-permute-done.59 = bf16[512,1536]{1,0:T(8,128)(2,1)S(1)} collective-permute-done((bf16[512,1536]{1,0:T(8,128)(2,1)}, bf16[512,1536]{1,0:T(8,128)(2,1)S(1)}, u32[]{:S(2)}, u32[]{:S(2)}) %collective-permute-start.59) | collective-permute-done | bytes 1572896 | tf_op jit(solution)/shard_map/ppermute | solution.py:400
  593.7 10.0 %convolution_convert_fusion.1 = bf16[2048,1536]{1,0:T(8,128)(2,1)} fusion(bf16[512,1536]{1,0:T(8,128)(2,1)S(1)} %broadcast_select_fusion, bf16[512,1536]{1,0:T(8,128)(2,1)} %pad_maximum_fusion.5, pred[2048,512]{1,0:T(32,128)(4,1)S(1)} %get-tuple-element.354, pred[2048,512]{1,0:T(32,128)(4,1)S(1)} %get-tuple-element.355), kind=kOutput, calls=%fused_computation.3 | convolution fusion | flops 6453985280 | bytes 11534336 | tf_op jit(solution)/shard_map/dot_general | solution.py:573
  603.7 38.8 %reduce-scatter.9.cloned.1.call-done = bf16[192,1152]{1,0:T(8,128)(2,1)} async-done(((bf16[768,1152]{1,0:T(8,128)(2,1)}), bf16[192,1152]{1,0:T(8,128)(2,1)}) %reduce-scatter.9.cloned.1.call-update) | async-done | bytes 442384
  643.8 44.4 %collective-permute-done.60 = bf16[512,1536]{1,0:T(8,128)(2,1)} collective-permute-done((bf16[512,1536]{1,0:T(8,128)(2,1)S(1)}, bf16[512,1536]{1,0:T(8,128)(2,1)}, u32[]{:S(2)}, u32[]{:S(2)}) %collective-permute-start.60) | collective-permute-done | bytes 1572896 | tf_op jit(solution)/shard_map/ppermute | solution.py:400
  704.7 8.6 %fusion.1 = bf16[2048,1536]{1,0:T(8,128)(2,1)} fusion(bf16[2048,1536]{1,0:T(8,128)(2,1)S(1)} %convolution_convert_fusion.2, bf16[512,1536]{1,0:T(8,128)(2,1)S(1)} %get-tuple-element.314, bf16[512,1536]{1,0:T(8,128)(2,1)S(1)} %copy-done.13, pred[2048,512]{1,0:T(32,128)(4,1)S(1)} %copy-done.21, pred[2048,512]{1,0:T(32,128)(4,1)S(1)} %copy-done.23), kind=kOutput, calls=%fused_computation.22 | convolution fusion | flops 6457131008 | bytes 17825792 | tf_op jit(solution)/shard_map/dot_general | solution.py:573
  716.9 23.7 %collective-permute-done.63 = bf16[512,1536]{1,0:T(8,128)(2,1)} collective-permute-done((bf16[512,1536]{1,0:T(8,128)(2,1)}, bf16[512,1536]{1,0:T(8,128)(2,1)}, u32[]{:S(2)}, u32[]{:S(2)}) %collective-permute-start.63) | collective-permute-done | bytes 1572896 | tf_op jit(solution)/shard_map/ppermute | solution.py:400
  743.9 8.5 %convolution_convert_fusion = bf16[2048,1536]{1,0:T(8,128)(2,1)} fusion(bf16[512,1536]{1,0:T(8,128)(2,1)S(1)} %get-tuple-element.311, bf16[512,1536]{1,0:T(8,128)(2,1)S(1)} %get-tuple-element.310, pred[2048,512]{1,0:T(32,128)(4,1)S(1)} %copy-done.17, pred[2048,512]{1,0:T(32,128)(4,1)S(1)} %copy-done.19), kind=kOutput, calls=%fused_computation.2 | convolution fusion | flops 6453985280 | bytes 11534336 | tf_op jit(solution)/shard_map/dot_general | solution.py:573
  752.4 9.1 %add.361 = bf16[2048,1536]{1,0:T(8,128)(2,1)} add(bf16[2048,1536]{1,0:T(8,128)(2,1)} %convolution_convert_fusion.1, bf16[2048,1536]{1,0:T(8,128)(2,1)} %convolution_convert_fusion) | non-fusion elementwise | flops 3145728 | bytes 18874368 | tf_op jit(solution)/shard_map/add | solution.py:677
  (426 shorter events, 336.6 us)
Async XLA Ops:
  7.2 478.6 %reduce-scatter.7.cloned.1.call-start = ((), (), s32[]{:S(2)}) async-start(), calls=%async_computation.2 | async-start | bytes 5308416
  50.9 43.8 %collective-permute-start.13 = (bf16[512,1536]{1,0:T(8,128)(2,1)}, bf16[512,1536]{1,0:T(8,128)(2,1)}, u32[]{:S(2)}, u32[]{:S(2)}) collective-permute-start(bf16[512,1536]{1,0:T(8,128)(2,1)} %fusion.20), channel_id=1, source_target_pairs={{0,8},{8,0},{1,9},{9,1},{2,10},{10,2},{3,11},{11,3},{4,12},{12,4},... | collective-permute-start | bytes 4718600 | tf_op jit(solution)/shard_map/ppermute | solution.py:373
  73.0 32.1 %collective-permute-start.14 = (bf16[192,1536]{1,0:T(8,128)(2,1)}, bf16[192,1536]{1,0:T(8,128)(2,1)}, u32[]{:S(2)}, u32[]{:S(2)}) collective-permute-start(bf16[192,1536]{1,0:T(8,128)(2,1)} %pad_maximum_fusion.7), channel_id=1, source_target_pairs={{0,0},{1,4},{2,8},{3,12},{4,1},{5,5},{6,9},{7,13},{8,2},{9,6},{10,... | collective-permute-start | bytes 1769480 | tf_op jit(solution)/shard_map/ppermute | solution.py:378
  128.5 39.6 %collective-permute-start.22 = (bf16[192,1536]{1,0:T(8,128)(2,1)}, bf16[192,1536]{1,0:T(8,128)(2,1)S(1)}, u32[]{:S(2)}, u32[]{:S(2)}) collective-permute-start(bf16[192,1536]{1,0:T(8,128)(2,1)} %collective-permute-done.14), channel_id=1, source_target_pairs={{0,16},{16,0},{1,17},{17,1},{2,18},{18,2},{3,19},{19,3},{4,20},{20... | collective-permute-start | bytes 1769480 | tf_op jit(solution)/shard_map/ppermute | solution.py:373
  168.1 46.1 %collective-permute-start.29 = (bf16[512,1536]{1,0:T(8,128)(2,1)S(1)}, bf16[512,1536]{1,0:T(8,128)(2,1)}, u32[]{:S(2)}, u32[]{:S(2)}) collective-permute-start(bf16[512,1536]{1,0:T(8,128)(2,1)S(1)} %pad_maximum_fusion.3), channel_id=1, source_target_pairs={{0,4},{4,0},{1,5},{5,1},{2,6},{6,2},{3,7},{7,3},{8,12},{12,8},{9,1... | collective-permute-start | bytes 4718600 | tf_op jit(solution)/shard_map/ppermute | solution.py:373
  169.5 36.0 %collective-permute-start.27 = (bf16[512,1536]{1,0:T(8,128)(2,1)S(1)}, bf16[512,1536]{1,0:T(8,128)(2,1)}, u32[]{:S(2)}, u32[]{:S(2)}) collective-permute-start(bf16[512,1536]{1,0:T(8,128)(2,1)S(1)} %pad_maximum_fusion.3), channel_id=1, source_target_pairs={{0,8},{8,0},{1,9},{9,1},{2,10},{10,2},{3,11},{11,3},{4,12},{12,4},... | collective-permute-start | bytes 4718600 | tf_op jit(solution)/shard_map/ppermute | solution.py:373
  170.1 31.6 %collective-permute-start.24 = (bf16[192,1536]{1,0:T(8,128)(2,1)}, bf16[192,1536]{1,0:T(8,128)(2,1)}, u32[]{:S(2)}, u32[]{:S(2)}) collective-permute-start(bf16[192,1536]{1,0:T(8,128)(2,1)} %collective-permute-done.20), channel_id=1, source_target_pairs={{2,3},{6,7},{10,11},{14,15},{18,19},{22,23},{26,27},{30,31}} | collective-permute-start | bytes 1769480 | tf_op jit(solution)/shard_map/ppermute | solution.py:399
  310.4 37.5 %collective-permute-start.35 = (bf16[512,1536]{1,0:T(8,128)(2,1)}, bf16[512,1536]{1,0:T(8,128)(2,1)S(1)}, u32[]{:S(2)}, u32[]{:S(2)}) collective-permute-start(bf16[512,1536]{1,0:T(8,128)(2,1)} %fusion.45), channel_id=1, source_target_pairs={{0,8},{8,0},{1,9},{9,1},{2,10},{10,2},{3,11},{11,3},{4,12},{12,4},... | collective-permute-start | bytes 4718600 | tf_op jit(solution)/shard_map/ppermute | solution.py:373
  317.7 324.8 %reduce-scatter.9.cloned.1.call-start = ((), (), s32[]{:S(2)}) async-start(), calls=%async_computation.3 | async-start | bytes 2211840
  381.8 57.4 %collective-permute-start.38 = (bf16[512,1536]{1,0:T(8,128)(2,1)S(1)}, bf16[512,1536]{1,0:T(8,128)(2,1)S(1)}, u32[]{:S(2)}, u32[]{:S(2)}) collective-permute-start(bf16[512,1536]{1,0:T(8,128)(2,1)S(1)} %pad_maximum_fusion.4), channel_id=1, source_target_pairs={{0,1},{1,2},{2,3},{4,5},{5,6},{6,7},{8,9},{9,10},{10,11},{12,13},{... | collective-permute-start | bytes 4718600 | tf_op jit(solution)/shard_map/ppermute | solution.py:399
  387.6 56.7 %collective-permute-start.39 = (bf16[512,1536]{1,0:T(8,128)(2,1)S(1)}, bf16[512,1536]{1,0:T(8,128)(2,1)}, u32[]{:S(2)}, u32[]{:S(2)}) collective-permute-start(bf16[512,1536]{1,0:T(8,128)(2,1)S(1)} %pad_maximum_fusion.4), channel_id=1, source_target_pairs={{1,0},{2,1},{3,2},{5,4},{6,5},{7,6},{9,8},{10,9},{11,10},{13,12},{... | collective-permute-start | bytes 4718600 | tf_op jit(solution)/shard_map/ppermute | solution.py:400
  401.5 46.4 %collective-permute-start.46 = (bf16[512,1536]{1,0:T(8,128)(2,1)S(1)}, bf16[512,1536]{1,0:T(8,128)(2,1)S(1)}, u32[]{:S(2)}, u32[]{:S(2)}) collective-permute-start(bf16[512,1536]{1,0:T(8,128)(2,1)S(1)} %fusion.48), channel_id=1, source_target_pairs={{0,4},{4,0},{1,5},{5,1},{2,6},{6,2},{3,7},{7,3},{8,12},{12,8},{9,1... | collective-permute-start | bytes 4718600 | tf_op jit(solution)/shard_map/ppermute | solution.py:373
  413.3 39.3 %collective-permute-start.43 = (bf16[512,256]{1,0:T(8,128)(2,1)S(1)}, bf16[512,256]{1,0:T(8,128)(2,1)S(1)}, u32[]{:S(2)}, u32[]{:S(2)}) collective-permute-start(bf16[512,256]{1,0:T(8,128)(2,1)S(1)} %add_convert_fusion.2), channel_id=1, source_target_pairs={{0,4},{4,0},{1,5},{5,1},{2,6},{6,2},{3,7},{7,3},{8,12},{12,8},{9,1... | collective-permute-start | bytes 786440 | tf_op jit(solution)/shard_map/ppermute | solution.py:373
  415.6 37.6 %collective-permute-start.45 = (bf16[512,256]{1,0:T(8,128)(2,1)S(1)}, bf16[512,256]{1,0:T(8,128)(2,1)}, u32[]{:S(2)}, u32[]{:S(2)}) collective-permute-start(bf16[512,256]{1,0:T(8,128)(2,1)S(1)} %collective-permute-done.44), channel_id=1, source_target_pairs={{0,4},{4,0},{1,5},{5,1},{2,6},{6,2},{3,7},{7,3},{8,12},{12,8},{9,1... | collective-permute-start | bytes 786440 | tf_op jit(solution)/shard_map/ppermute | solution.py:373
  439.2 34.4 %collective-permute-start.47 = (bf16[512,1536]{1,0:T(8,128)(2,1)}, bf16[512,1536]{1,0:T(8,128)(2,1)}, u32[]{:S(2)}, u32[]{:S(2)}) collective-permute-start(bf16[512,1536]{1,0:T(8,128)(2,1)} %fusion.46), channel_id=1, source_target_pairs={{0,8},{8,0},{1,9},{9,1},{2,10},{10,2},{3,11},{11,3},{4,12},{12,4},... | collective-permute-start | bytes 4718600 | tf_op jit(solution)/shard_map/ppermute | solution.py:373
  448.0 37.8 %collective-permute-start.49 = (bf16[512,1536]{1,0:T(8,128)(2,1)}, bf16[512,1536]{1,0:T(8,128)(2,1)}, u32[]{:S(2)}, u32[]{:S(2)}) collective-permute-start(bf16[512,1536]{1,0:T(8,128)(2,1)} %collective-permute-done.39), channel_id=1, source_target_pairs={{1,0},{2,1},{5,4},{6,5},{9,8},{10,9},{13,12},{14,13},{17,16},{18,1... | collective-permute-start | bytes 4718600 | tf_op jit(solution)/shard_map/ppermute | solution.py:400
  535.6 31.6 %collective-permute-start.61 = (bf16[768,1152]{1,0:T(8,128)(2,1)}, bf16[768,1152]{1,0:T(8,128)(2,1)S(1)}, u32[]{:S(2)}, u32[]{:S(2)}) collective-permute-start(bf16[768,1152]{1,0:T(8,128)(2,1)} %constant_dynamic-slice_fusion), channel_id=1, source_target_pairs={{0,16},{16,0},{1,17},{17,1},{2,18},{18,2},{3,19},{19,3},{4,20},{20... | collective-permute-start | bytes 5308424 | tf_op jit(solution)/shard_map/ppermute | solution.py:373
  539.8 39.4 %collective-permute-start.57 = (bf16[512,1536]{1,0:T(8,128)(2,1)}, bf16[512,1536]{1,0:T(8,128)(2,1)}, u32[]{:S(2)}, u32[]{:S(2)}) collective-permute-start(bf16[512,1536]{1,0:T(8,128)(2,1)} %pad_maximum_fusion.5), channel_id=1, source_target_pairs={{0,1},{1,2},{2,3},{4,5},{5,6},{6,7},{8,9},{9,10},{10,11},{12,13},{... | collective-permute-start | bytes 4718600 | tf_op jit(solution)/shard_map/ppermute | solution.py:399
  542.2 50.0 %collective-permute-start.59 = (bf16[512,1536]{1,0:T(8,128)(2,1)}, bf16[512,1536]{1,0:T(8,128)(2,1)S(1)}, u32[]{:S(2)}, u32[]{:S(2)}) collective-permute-start(bf16[512,1536]{1,0:T(8,128)(2,1)} %pad_maximum_fusion.5), channel_id=1, source_target_pairs={{1,0},{2,1},{3,2},{5,4},{6,5},{7,6},{9,8},{10,9},{11,10},{13,12},{... | collective-permute-start | bytes 4718600 | tf_op jit(solution)/shard_map/ppermute | solution.py:400
  575.1 118.6 %collective-permute-start.55 = (bf16[512,1536]{1,0:T(8,128)(2,1)}, bf16[512,1536]{1,0:T(8,128)(2,1)}, u32[]{:S(2)}, u32[]{:S(2)}) collective-permute-start(bf16[512,1536]{1,0:T(8,128)(2,1)} %collective-permute-done.48), channel_id=1, source_target_pairs={{2,3},{6,7},{10,11},{14,15},{18,19},{22,23},{26,27},{30,31}} | collective-permute-start | bytes 4718600 | tf_op jit(solution)/shard_map/ppermute | solution.py:399
  577.0 116.8 %collective-permute-start.56 = (bf16[512,1536]{1,0:T(8,128)(2,1)}, bf16[512,1536]{1,0:T(8,128)(2,1)}, u32[]{:S(2)}, u32[]{:S(2)}) collective-permute-start(bf16[512,1536]{1,0:T(8,128)(2,1)} %collective-permute-done.49), channel_id=1, source_target_pairs={{1,0},{5,4},{9,8},{13,12},{17,16},{21,20},{25,24},{29,28}} | collective-permute-start | bytes 4718600 | tf_op jit(solution)/shard_map/ppermute | solution.py:400
  579.2 64.6 %collective-permute-start.58 = (bf16[512,1536]{1,0:T(8,128)(2,1)}, bf16[512,1536]{1,0:T(8,128)(2,1)}, u32[]{:S(2)}, u32[]{:S(2)}) collective-permute-start(bf16[512,1536]{1,0:T(8,128)(2,1)} %collective-permute-done.57), channel_id=1, source_target_pairs={{1,2},{2,3},{5,6},{6,7},{9,10},{10,11},{13,14},{14,15},{17,18},{18... | collective-permute-start | bytes 4718600 | tf_op jit(solution)/shard_map/ppermute | solution.py:399
  592.2 96.0 %collective-permute-start.60 = (bf16[512,1536]{1,0:T(8,128)(2,1)S(1)}, bf16[512,1536]{1,0:T(8,128)(2,1)}, u32[]{:S(2)}, u32[]{:S(2)}) collective-permute-start(bf16[512,1536]{1,0:T(8,128)(2,1)S(1)} %collective-permute-done.59), channel_id=1, source_target_pairs={{1,0},{2,1},{5,4},{6,5},{9,8},{10,9},{13,12},{14,13},{17,16},{18,1... | collective-permute-start | bytes 4718600 | tf_op jit(solution)/shard_map/ppermute | solution.py:400
  692.5 48.1 %collective-permute-start.63 = (bf16[512,1536]{1,0:T(8,128)(2,1)}, bf16[512,1536]{1,0:T(8,128)(2,1)}, u32[]{:S(2)}, u32[]{:S(2)}) collective-permute-start(bf16[512,1536]{1,0:T(8,128)(2,1)} %collective-permute-done.60), channel_id=1, source_target_pairs={{1,0},{5,4},{9,8},{13,12},{17,16},{21,20},{25,24},{29,28}} | collective-permute-start | bytes 4718600 | tf_op jit(solution)/shard_map/ppermute | solution.py:400
  (109 other events, 1863.9 us)
Sparse Core Ops, SparseCore 0:
  317.8 120.7 reduce-scatter.6
  570.4 72.0 reduce-scatter.8

commit v8 on v7

--- a/solution.py
+++ b/solution.py
@@ -640,6 +640,7 @@
     out_two = line_step(out_one, 2)
     in_grad, both_grad, own_back = tie(in_grad, both_grad, own_back)
     beside, out_two = tie(beside, out_two)
+    out_three = line_step(out_two, 3)
     both_grad = crossed(both_grad)
     normed_back = own_back + beside.astype(F32) + contract_columns(own_shared, in_full[:, width + LANES :])
     norm_gain_grad = jnp.sum(normed_back * hidden * scale, axis=0)
@@ -662,18 +663,15 @@
     back_rows = exchanged(input_work.astype(BF16))
     small = summed(small, ("row",))
     small = jnp.concatenate([small[:8], summed(small[8:], ("core", "side"))], axis=0)
-    back_rows, out_two, small, both_grad, in_grad = tie(back_rows, out_two, small, both_grad, in_grad)
+    back_rows, out_three, small, both_grad, in_grad = tie(back_rows, out_three, small, both_grad, in_grad)
     in_grad = lax.psum_scatter(row_scattered(in_grad), "tensor", scatter_dimension=0, tiled=True)
     back_one = line_step((back_rows, back_rows), 1)
-    out_three = line_step(out_two, 3)
     back_two = line_step(back_one, 2)
-    back_two, in_grad = tie(back_two, in_grad)
     back_three = line_step(back_two, 3)
-    out_three, _ = tie(out_three, back_two)
     layer_out = settled([out_rows, slot_one(out_one)], (0, 1))
     layer_out = layer_out + settled([slot_two(out_one, out_two), slot_three(out_two, out_three)], (2, 3))
     input_grad = settled([back_rows, slot_one(back_one)], (0, 1))
-    layer_out, input_grad, back_three, small = tie(layer_out, input_grad, back_three, small)
+    layer_out, input_grad, back_three, small, in_grad = tie(layer_out, input_grad, back_three, small, in_grad)
     input_grad = input_grad + settled([slot_two(back_one, back_two), slot_three(back_two, back_three)], (2, 3))
     small = small + swap(small, "tensor", 1)
     small = small + swap(small, "tensor", 2)

time: 789 us -> 761 us (0.965)
  waiting for transfers between devices: 274 us -> 222 us
  starting transfers between devices: 121 us -> 135 us
    unnamed x4, waiting for transfers between devices: 38.9 us -> 0.05 us
    ppermute x38, waiting for transfers between devices: 94.5 us -> 62.9 us  [swap(): return lax.ppermute(v, axis, [(i, i ^ mask) for i in range(count)])]
    ppermute x12, waiting for transfers between devices: 23.1 us -> 43.7 us  [line_step(): lax.ppermute(left, 'tensor', [(i, i + 1) for i in range(j - 1, 3)])]
    ppermute x6, starting transfers between devices: 34.3 us -> 45 us  [crossed(): return lax.ppermute(v, ('side', 'core', 'tensor'), pairs)]
    unnamed x135 -> x155, local copies, waits for them, and re-layouts: 18.3 us -> 20.5 us
  transfers between devices with their start and end apart: 70 -> 70, of which waited for: 28 -> 27; matrix products, arithmetic and copies ran while one was open for 26% -> 29% of each run, Pallas kernels for 10% -> 11%
where the time goes in v8:
time: 761 us; the launch traced here: 748 us
  waiting for transfers between devices  222 us (29%)
  matrix products  148 us (19%)
  starting transfers between devices  135 us (18%)
  other arithmetic  91.3 us (12%)
  Pallas kernels  81.1 us (11%)
  local copies, waits for them, and re-layouts  48.4 us (6%)
  between operations  21.5 us (3%)
    ppermute x12, waiting for transfers between devices, line_step(): lax.ppermute(right, 'tensor', [(i + 1, i) for i in range(0, 4 - j)])  103 us
    ppermute x38, waiting for transfers between devices, swap(): return lax.ppermute(v, axis, [(i, i ^ mask) for i in range(count)])  62.9 us
    pallas_call x2, Pallas kernels, mixer_backward(): pl.pallas_call(functools.partial(backward_kernel, first_chunk), grid_spec...  55.3 us
    ppermute x38, starting transfers between devices, swap(): return lax.ppermute(v, axis, [(i, i ^ mask) for i in range(count)])  45.7 us
    ppermute x6, starting transfers between devices, crossed(): return lax.ppermute(v, ('side', 'core', 'tensor'), pairs)  45 us
    ppermute x12, waiting for transfers between devices, line_step(): lax.ppermute(left, 'tensor', [(i, i + 1) for i in range(j - 1, 3)])  43.7 us
    dot_general x4, matrix products, settled(): jnp.dot(where.astype(BF16), jnp.concatenate(held), preferred_element_type...  36.8 us
    dot_general x13, matrix products, contract_columns(): lax.dot_general(a, b, (((1,), (1,)), ((), ())), preferred_element_type=F32)  30.2 us
  transfers between devices with their start and end apart: 70, of which 27 were waited for; matrix products, arithmetic and copies ran while one was open for 29% of the time, Pallas kernels for 11%

profile of v8, /device:TPU:1, one launch (start us, length us, event | category | flops | bytes accessed | tf_op | source)
XLA Modules:
  0.0 747.5 jit_solution(8114529805272527580)
XLA Ops:
  73.1 10.0 %collective-permute-start.14 = (bf16[192,1536]{1,0:T(8,128)(2,1)S(1)}, bf16[192,1536]{1,0:T(8,128)(2,1)S(1)}, u32[]{:S(2)}, u32[]{:S(2)}) collective-permute-start(bf16[192,1536]{1,0:T(8,128)(2,1)S(1)} %copy-done.33), channel_id=1, source_target_pairs={{0,0},{1,4},{2,8},{3,12},{4,1},{5,5},{6,9},{7,13},{8,2},{9,6},{10,... | collective-permute-start | bytes 1769480 | tf_op jit(solution)/shard_map/ppermute | solution.py:378
  94.9 10.4 %collective-permute-start = (f32[8,768]{1,0:T(8,128)S(1)}, f32[8,768]{1,0:T(8,128)S(1)}, u32[]{:S(2)}, u32[]{:S(2)}) collective-permute-start(f32[8,768]{1,0:T(8,128)S(1)} %concatenate.77), channel_id=1, source_target_pairs={{0,0},{1,4},{2,8},{3,12},{4,1},{5,5},{6,9},{7,13},{8,2},{9,6},{10,... | collective-permute-start | bytes 73736 | tf_op jit(solution)/shard_map/ppermute | solution.py:378
  151.2 16.4 %fusion.124.proj_ref.proj_before_ref = f32[2048,1152]{1,0:T(8,128)} fusion(bf16[1536,1152]{1,0:T(8,128)(2,1)S(1)} %constant_dynamic-update-slice_fusion.12, bf16[512,1536]{1,0:T(8,128)(2,1)} %collective-permute-done.17, bf16[512,1536]{1,0:T(8,128)(2,1)} %collective-permute-done.13, bf16[512,1536]{1,0:T(8,128)(2,1)} %collective-permute-done.5, ...), kind=kOutput, calls=%fused_computation.273 | convolution fusion | flops 7272923136 | bytes 19267584 | tf_op jit(solution)/shard_map/dot_general | solution.py:575
  176.2 25.8 %mixer_forward.1 = (f32[2048,768]{1,0:T(8,128)}, bf16[16,128,768]{2,1,0:T(8,128)(2,1)}) custom-call(s32[4]{0:T(128)} %fusion.112.lens_ref, s32[16]{0:T(128)} %fusion.109.order_ref, f32[2048,1152]{1,0:T(8,128)} %fusion.124.proj_ref.proj_before_ref, f32[4,768]{1,0:T(4,128)} %slice.348.fw_ref, f32[1,768]{1,0:T(1,128)} %get-tuple-element.327.fb_ref, ...), custom_call_target="tpu_custom_call" | custom-call | flops 20000000000 | bytes 30000000 | tf_op jit(solution)/shard_map/mixer_forward/pallas_call | solution.py:293
  224.5 11.4 %fusion.71 = f32[2048,768]{1,0:T(8,128)S(1)} fusion(bf16[1536,1536]{1,0:T(8,128)(2,1)S(1)} %constant_dynamic-update-slice_fusion.4, bf16[512,1536]{1,0:T(8,128)(2,1)} %collective-permute-done.17, bf16[512,1536]{1,0:T(8,128)(2,1)} %collective-permute-done.13, bf16[512,1536]{1,0:T(8,128)(2,1)} %collective-permute-done.5, bf16[512,1536]{1,0:T(8,128)(2,1)} %fusion.20), kind=kOutput, calls=%fused_computation.117 | convolution fusion | flops 4857004032 | bytes 14942208 | tf_op jit(solution)/shard_map/dot_general | solution.py:587
  237.3 10.5 %fusion.65 = f32[2048,768]{1,0:T(8,128)S(1)} fusion(bf16[2048,1536]{1,0:T(8,128)(2,1)} %constant_dynamic-update-slice_fusion, bf16[1536,1536]{1,0:T(8,128)(2,1)} %copy-done.4), kind=kOutput, calls=%fused_computation.111 | convolution fusion | flops 4831838208 | bytes 14942208 | tf_op jit(solution)/shard_map/dot_general | solution.py:588
  261.6 21.8 %multiply_convert_fusion.1 = (bf16[2048,768]{1,0:T(8,128)(2,1)S(1)}, f32[2048,768]{1,0:T(8,128)}, f32[768]{0:T(1024)S(1)}, bf16[2048,768]{1,0:T(8,128)(2,1)S(1)}) fusion(f32[2048,768]{1,0:T(8,128)} %copy-done, f32[2048,768]{1,0:T(8,128)} %get-tuple-element.184.out_ref, f32[2048]{0:T(1024)S(1)} %bitcast.62, f32[2048,768]{1,0:T(8,128)} %get-tuple-element.295, ...), kind=kLoop, calls=%fused_computation.16 | loop fusion | flops 36175104 | bytes 37779456 | tf_op jit(solution)/shard_map/convert_element_type | solution.py:606
  286.3 8.1 %convolution_convert_fusion.5 = bf16[1536,768]{0,1:T(8,128)(2,1)S(1)} fusion(bf16[2048,1536]{1,0:T(8,128)(2,1)} %constant_dynamic-update-slice_fusion, bf16[2048,768]{1,0:T(8,128)(2,1)S(1)} %get-tuple-element.301), kind=kOutput, calls=%fused_computation.42 | convolution fusion | flops 4833017856 | bytes 11796480 | tf_op jit(solution)/shard_map/dot_general | solution.py:442
  321.6 27.8 %mixer_backward.2 = (bf16[2048,896]{1,0:T(8,128)(2,1)}, f32[2048,256]{1,0:T(8,128)}, f32[8,768]{1,0:T(8,128)}, f32[8,256]{1,0:T(8,128)}, f32[8,128]{1,0:T(8,128)...) custom-call(s32[4]{0:T(128)} %fusion.112.lens_ref, s32[16]{0:T(128)} %fusion.109.order_ref, ...), custom_call_target="tpu_custom_call" | custom-call | flops 20000000000 | bytes 30000000 | tf_op jit(solution)/shard_map/mixer_backward/pallas_call | solution.py:345
  353.0 27.5 %mixer_backward.3 = (bf16[2048,896]{1,0:T(8,128)(2,1)}, f32[2048,256]{1,0:T(8,128)}, f32[8,768]{1,0:T(8,128)}, f32[8,256]{1,0:T(8,128)}, f32[8,128]{1,0:T(8,128)...) custom-call(s32[4]{0:T(128)} %fusion.112.lens_ref, ...), custom_call_target="tpu_custom_call", output_to_operand_aliasing={{0}: (17, {}), {1}: (18, {})} | custom-call | flops 20000000000 | bytes 30000000 | tf_op jit(solution)/shard_map/mixer_backward/pallas_call | solution.py:345
  417.2 23.8 %collective-permute-done.38 = bf16[512,1536]{1,0:T(8,128)(2,1)S(1)} collective-permute-done((bf16[512,1536]{1,0:T(8,128)(2,1)S(1)}, bf16[512,1536]{1,0:T(8,128)(2,1)S(1)}, u32[]{:S(2)}, u32[]{:S(2)}) %collective-permute-start.38) | collective-permute-done | bytes 1572896 | tf_op jit(solution)/shard_map/ppermute | solution.py:399
  460.8 14.6 %convolution_convert_fusion.3 = bf16[1536,1152]{1,0:T(8,128)(2,1)} fusion(bf16[512,256]{1,0:T(8,128)(2,1)} %collective-permute-done.48, bf16[512,256]{1,0:T(8,128)(2,1)} %copy-done.63, bf16[512,256]{1,0:T(8,128)(2,1)} %copy-done.64, bf16[512,256]{1,0:T(8,128)(2,1)S(1)} %add_convert_fusion.2, bf16[2048,896]{1,0:T(8,128)(2,1)} %get-tuple-element.216, ...), kind=kOutput, calls=%fused_computation.5 | convolution fusion | flops 7298285568 | bytes 14548992 | tf_op jit(solution)/shard_map/dot_general | solution.py:442
  475.4 10.4 %collective-permute-done.42 = bf16[512,1536]{1,0:T(8,128)(2,1)} collective-permute-done((bf16[512,1536]{1,0:T(8,128)(2,1)}, bf16[512,1536]{1,0:T(8,128)(2,1)}, u32[]{:S(2)}, u32[]{:S(2)}) %collective-permute-start.42) | collective-permute-done | bytes 1572896 | tf_op jit(solution)/shard_map/ppermute | solution.py:400
  529.6 8.9 %collective-permute-done.52 = bf16[512,1536]{1,0:T(8,128)(2,1)} collective-permute-done((bf16[512,1536]{1,0:T(8,128)(2,1)}, bf16[512,1536]{1,0:T(8,128)(2,1)}, u32[]{:S(2)}, u32[]{:S(2)}) %collective-permute-start.52) | collective-permute-done | bytes 1572896 | tf_op jit(solution)/shard_map/ppermute | solution.py:400
  538.5 12.1 %collective-permute-done.56 = bf16[192,1536]{1,0:T(8,128)(2,1)} collective-permute-done((bf16[192,1536]{1,0:T(8,128)(2,1)}, bf16[192,1536]{1,0:T(8,128)(2,1)}, u32[]{:S(2)}, u32[]{:S(2)}) %collective-permute-start.56) | collective-permute-done | bytes 589856 | tf_op jit(solution)/shard_map/ppermute | solution.py:378
  564.7 8.5 %convolution_convert_fusion.2 = bf16[2048,1536]{1,0:T(8,128)(2,1)} fusion(bf16[512,1536]{1,0:T(8,128)(2,1)S(1)} %get-tuple-element.305, bf16[512,1536]{1,0:T(8,128)(2,1)S(1)} %get-tuple-element.304, pred[2048,512]{1,0:T(32,128)(4,1)S(1)} %get-tuple-element.344, pred[2048,512]{1,0:T(32,128)(4,1)S(1)} %copy-done.27), kind=kOutput, calls=%fused_computation.4 | convolution fusion | flops 6453985280 | bytes 11534336 | tf_op jit(solution)/shard_map/dot_general | solution.py:573
  573.2 15.8 %collective-permute-done.58 = bf16[512,1536]{1,0:T(8,128)(2,1)} collective-permute-done((bf16[512,1536]{1,0:T(8,128)(2,1)S(1)}, bf16[512,1536]{1,0:T(8,128)(2,1)}, u32[]{:S(2)}, u32[]{:S(2)}) %collective-permute-start.58) | collective-permute-done | bytes 1572896 | tf_op jit(solution)/shard_map/ppermute | solution.py:399
  600.0 11.2 %fusion.1 = bf16[2048,1536]{1,0:T(8,128)(2,1)} fusion(bf16[2048,1536]{1,0:T(8,128)(2,1)} %convolution_convert_fusion.2, bf16[512,1536]{1,0:T(8,128)(2,1)} %get-tuple-element.306, bf16[512,1536]{1,0:T(8,128)(2,1)S(1)} %copy-done.17, pred[2048,512]{1,0:T(32,128)(4,1)} %get-tuple-element.346, pred[2048,512]{1,0:T(32,128)(4,1)} %get-tuple-element.347), kind=kOutput, calls=%fused_computation.22 | convolution fusion | flops 6457131008 | bytes 17825792 | tf_op jit(solution)/shard_map/dot_general | solution.py:573
  615.4 43.2 %collective-permute-done.61 = bf16[512,1536]{1,0:T(8,128)(2,1)} collective-permute-done((bf16[512,1536]{1,0:T(8,128)(2,1)S(1)}, bf16[512,1536]{1,0:T(8,128)(2,1)}, u32[]{:S(2)}, u32[]{:S(2)}) %collective-permute-start.61) | collective-permute-done | bytes 1572896 | tf_op jit(solution)/shard_map/ppermute | solution.py:400
  659.9 8.5 %convolution_convert_fusion.1 = bf16[2048,1536]{1,0:T(8,128)(2,1)} fusion(bf16[512,1536]{1,0:T(8,128)(2,1)S(1)} %broadcast_select_fusion, bf16[512,1536]{1,0:T(8,128)(2,1)S(1)} %copy-done.19, pred[2048,512]{1,0:T(32,128)(4,1)S(1)} %copy-done.23, pred[2048,512]{1,0:T(32,128)(4,1)S(1)} %copy-done.24), kind=kOutput, calls=%fused_computation.3 | convolution fusion | flops 6453985280 | bytes 11534336 | tf_op jit(solution)/shard_map/dot_general | solution.py:573
  669.7 25.1 %collective-permute-done.62 = bf16[512,1536]{1,0:T(8,128)(2,1)} collective-permute-done((bf16[512,1536]{1,0:T(8,128)(2,1)}, bf16[512,1536]{1,0:T(8,128)(2,1)}, u32[]{:S(2)}, u32[]{:S(2)}) %collective-permute-start.62) | collective-permute-done | bytes 1572896 | tf_op jit(solution)/shard_map/ppermute | solution.py:400
  706.1 8.5 %convolution_convert_fusion = bf16[2048,1536]{1,0:T(8,128)(2,1)} fusion(bf16[512,1536]{1,0:T(8,128)(2,1)S(1)} %get-tuple-element.303, bf16[512,1536]{1,0:T(8,128)(2,1)S(1)} %get-tuple-element.302, pred[2048,512]{1,0:T(32,128)(4,1)S(1)} %copy-done.26, pred[2048,512]{1,0:T(32,128)(4,1)S(1)} %copy-done.28), kind=kOutput, calls=%fused_computation.2 | convolution fusion | flops 6453985280 | bytes 11534336 | tf_op jit(solution)/shard_map/dot_general | solution.py:573
  714.6 9.1 %add.361 = bf16[2048,1536]{1,0:T(8,128)(2,1)} add(bf16[2048,1536]{1,0:T(8,128)(2,1)} %convolution_convert_fusion.1, bf16[2048,1536]{1,0:T(8,128)(2,1)} %convolution_convert_fusion) | non-fusion elementwise | flops 3145728 | bytes 18874368 | tf_op jit(solution)/shard_map/add | solution.py:675
  723.7 9.3 %collective-permute-start.67 = (f32[8,768]{1,0:T(8,128)S(1)}, f32[8,768]{1,0:T(8,128)S(1)}, u32[]{:S(2)}, u32[]{:S(2)}) collective-permute-start(f32[8,768]{1,0:T(8,128)S(1)} %slice.382), channel_id=1, source_target_pairs={{0,0},{1,4},{2,8},{3,12},{4,1},{5,5},{6,9},{7,13},{8,2},{9,6},{10,... | collective-permute-start | bytes 73736 | tf_op jit(solution)/shard_map/ppermute | solution.py:378
  (446 shorter events, 347.3 us)
Async XLA Ops:
  7.2 486.2 %reduce-scatter.7.cloned.1.call-start = ((), (), s32[]{:S(2)}) async-start(), calls=%async_computation.2 | async-start | bytes 5308416
  51.0 43.9 %collective-permute-start.13 = (bf16[512,1536]{1,0:T(8,128)(2,1)}, bf16[512,1536]{1,0:T(8,128)(2,1)}, u32[]{:S(2)}, u32[]{:S(2)}) collective-permute-start(bf16[512,1536]{1,0:T(8,128)(2,1)} %fusion.20), channel_id=1, source_target_pairs={{0,8},{8,0},{1,9},{9,1},{2,10},{10,2},{3,11},{11,3},{4,12},{12,4},... | collective-permute-start | bytes 4718600 | tf_op jit(solution)/shard_map/ppermute | solution.py:373
  128.2 39.4 %collective-permute-start.22 = (bf16[192,1536]{1,0:T(8,128)(2,1)}, bf16[192,1536]{1,0:T(8,128)(2,1)S(1)}, u32[]{:S(2)}, u32[]{:S(2)}) collective-permute-start(bf16[192,1536]{1,0:T(8,128)(2,1)} %copy-done.31), channel_id=1, source_target_pairs={{0,16},{16,0},{1,17},{17,1},{2,18},{18,2},{3,19},{19,3},{4,20},{20... | collective-permute-start | bytes 1769480 | tf_op jit(solution)/shard_map/ppermute | solution.py:373
  167.7 45.9 %collective-permute-start.29 = (bf16[512,1536]{1,0:T(8,128)(2,1)S(1)}, bf16[512,1536]{1,0:T(8,128)(2,1)}, u32[]{:S(2)}, u32[]{:S(2)}) collective-permute-start(bf16[512,1536]{1,0:T(8,128)(2,1)S(1)} %pad_maximum_fusion.3), channel_id=1, source_target_pairs={{0,4},{4,0},{1,5},{5,1},{2,6},{6,2},{3,7},{7,3},{8,12},{12,8},{9,1... | collective-permute-start | bytes 4718600 | tf_op jit(solution)/shard_map/ppermute | solution.py:373
  168.6 36.5 %collective-permute-start.27 = (bf16[512,1536]{1,0:T(8,128)(2,1)S(1)}, bf16[512,1536]{1,0:T(8,128)(2,1)}, u32[]{:S(2)}, u32[]{:S(2)}) collective-permute-start(bf16[512,1536]{1,0:T(8,128)(2,1)S(1)} %pad_maximum_fusion.3), channel_id=1, source_target_pairs={{0,8},{8,0},{1,9},{9,1},{2,10},{10,2},{3,11},{11,3},{4,12},{12,4},... | collective-permute-start | bytes 4718600 | tf_op jit(solution)/shard_map/ppermute | solution.py:373
  311.9 37.5 %collective-permute-start.35 = (bf16[512,1536]{1,0:T(8,128)(2,1)}, bf16[512,1536]{1,0:T(8,128)(2,1)S(1)}, u32[]{:S(2)}, u32[]{:S(2)}) collective-permute-start(bf16[512,1536]{1,0:T(8,128)(2,1)} %fusion.45), channel_id=1, source_target_pairs={{0,8},{8,0},{1,9},{9,1},{2,10},{10,2},{3,11},{11,3},{4,12},{12,4},... | collective-permute-start | bytes 4718600 | tf_op jit(solution)/shard_map/ppermute | solution.py:373
  319.0 349.4 %reduce-scatter.9.cloned.1.call-start = ((), (), s32[]{:S(2)}) async-start(), calls=%async_computation.3 | async-start | bytes 2211840
  384.3 56.7 %collective-permute-start.38 = (bf16[512,1536]{1,0:T(8,128)(2,1)S(1)}, bf16[512,1536]{1,0:T(8,128)(2,1)S(1)}, u32[]{:S(2)}, u32[]{:S(2)}) collective-permute-start(bf16[512,1536]{1,0:T(8,128)(2,1)S(1)} %pad_maximum_fusion.4), channel_id=1, source_target_pairs={{0,1},{1,2},{2,3},{4,5},{5,6},{6,7},{8,9},{9,10},{10,11},{12,13},{... | collective-permute-start | bytes 4718600 | tf_op jit(solution)/shard_map/ppermute | solution.py:399
  389.5 56.7 %collective-permute-start.39 = (bf16[512,1536]{1,0:T(8,128)(2,1)S(1)}, bf16[512,1536]{1,0:T(8,128)(2,1)}, u32[]{:S(2)}, u32[]{:S(2)}) collective-permute-start(bf16[512,1536]{1,0:T(8,128)(2,1)S(1)} %pad_maximum_fusion.4), channel_id=1, source_target_pairs={{1,0},{2,1},{3,2},{5,4},{6,5},{7,6},{9,8},{10,9},{11,10},{13,12},{... | collective-permute-start | bytes 4718600 | tf_op jit(solution)/shard_map/ppermute | solution.py:400
  403.6 52.3 %collective-permute-start.49 = (bf16[512,1536]{1,0:T(8,128)(2,1)S(1)}, bf16[512,1536]{1,0:T(8,128)(2,1)S(1)}, u32[]{:S(2)}, u32[]{:S(2)}) collective-permute-start(bf16[512,1536]{1,0:T(8,128)(2,1)S(1)} %fusion.48), channel_id=1, source_target_pairs={{0,4},{4,0},{1,5},{5,1},{2,6},{6,2},{3,7},{7,3},{8,12},{12,8},{9,1... | collective-permute-start | bytes 4718600 | tf_op jit(solution)/shard_map/ppermute | solution.py:373
  414.8 45.3 %collective-permute-start.46 = (bf16[512,256]{1,0:T(8,128)(2,1)S(1)}, bf16[512,256]{1,0:T(8,128)(2,1)S(1)}, u32[]{:S(2)}, u32[]{:S(2)}) collective-permute-start(bf16[512,256]{1,0:T(8,128)(2,1)S(1)} %add_convert_fusion.2), channel_id=1, source_target_pairs={{0,4},{4,0},{1,5},{5,1},{2,6},{6,2},{3,7},{7,3},{8,12},{12,8},{9,1... | collective-permute-start | bytes 786440 | tf_op jit(solution)/shard_map/ppermute | solution.py:373
  417.2 43.7 %collective-permute-start.48 = (bf16[512,256]{1,0:T(8,128)(2,1)S(1)}, bf16[512,256]{1,0:T(8,128)(2,1)}, u32[]{:S(2)}, u32[]{:S(2)}) collective-permute-start(bf16[512,256]{1,0:T(8,128)(2,1)S(1)} %collective-permute-done.47), channel_id=1, source_target_pairs={{0,4},{4,0},{1,5},{5,1},{2,6},{6,2},{3,7},{7,3},{8,12},{12,8},{9,1... | collective-permute-start | bytes 786440 | tf_op jit(solution)/shard_map/ppermute | solution.py:373
  448.0 37.8 %collective-permute-start.42 = (bf16[512,1536]{1,0:T(8,128)(2,1)}, bf16[512,1536]{1,0:T(8,128)(2,1)}, u32[]{:S(2)}, u32[]{:S(2)}) collective-permute-start(bf16[512,1536]{1,0:T(8,128)(2,1)} %collective-permute-done.39), channel_id=1, source_target_pairs={{1,0},{2,1},{5,4},{6,5},{9,8},{10,9},{13,12},{14,13},{17,16},{18,1... | collective-permute-start | bytes 4718600 | tf_op jit(solution)/shard_map/ppermute | solution.py:400
  455.8 34.4 %collective-permute-start.40 = (bf16[512,1536]{1,0:T(8,128)(2,1)}, bf16[512,1536]{1,0:T(8,128)(2,1)}, u32[]{:S(2)}, u32[]{:S(2)}) collective-permute-start(bf16[512,1536]{1,0:T(8,128)(2,1)} %fusion.46), channel_id=1, source_target_pairs={{0,8},{8,0},{1,9},{9,1},{2,10},{10,2},{3,11},{11,3},{4,12},{12,4},... | collective-permute-start | bytes 4718600 | tf_op jit(solution)/shard_map/ppermute | solution.py:373
  490.2 39.4 %collective-permute-start.51 = (bf16[512,1536]{1,0:T(8,128)(2,1)}, bf16[512,1536]{1,0:T(8,128)(2,1)}, u32[]{:S(2)}, u32[]{:S(2)}) collective-permute-start(bf16[512,1536]{1,0:T(8,128)(2,1)} %collective-permute-done.41), channel_id=1, source_target_pairs={{2,3},{6,7},{10,11},{14,15},{18,19},{22,23},{26,27},{30,31}} | collective-permute-start | bytes 4718600 | tf_op jit(solution)/shard_map/ppermute | solution.py:399
  492.0 46.5 %collective-permute-start.52 = (bf16[512,1536]{1,0:T(8,128)(2,1)}, bf16[512,1536]{1,0:T(8,128)(2,1)}, u32[]{:S(2)}, u32[]{:S(2)}) collective-permute-start(bf16[512,1536]{1,0:T(8,128)(2,1)} %collective-permute-done.42), channel_id=1, source_target_pairs={{1,0},{5,4},{9,8},{13,12},{17,16},{21,20},{25,24},{29,28}} | collective-permute-start | bytes 4718600 | tf_op jit(solution)/shard_map/ppermute | solution.py:400
  510.7 39.8 %collective-permute-start.56 = (bf16[192,1536]{1,0:T(8,128)(2,1)}, bf16[192,1536]{1,0:T(8,128)(2,1)}, u32[]{:S(2)}, u32[]{:S(2)}) collective-permute-start(bf16[192,1536]{1,0:T(8,128)(2,1)} %copy.50), channel_id=1, source_target_pairs={{0,0},{1,4},{2,8},{3,12},{4,1},{5,5},{6,9},{7,13},{8,2},{9,6},{10,... | collective-permute-start | bytes 1769480 | tf_op jit(solution)/shard_map/ppermute | solution.py:378
  550.6 40.3 %collective-permute-start.57 = (bf16[512,1536]{1,0:T(8,128)(2,1)S(1)}, bf16[512,1536]{1,0:T(8,128)(2,1)S(1)}, u32[]{:S(2)}, u32[]{:S(2)}) collective-permute-start(bf16[512,1536]{1,0:T(8,128)(2,1)S(1)} %pad_maximum_fusion.5), channel_id=1, source_target_pairs={{1,0},{2,1},{3,2},{5,4},{6,5},{7,6},{9,8},{10,9},{11,10},{13,12},{... | collective-permute-start | bytes 4718600 | tf_op jit(solution)/shard_map/ppermute | solution.py:400
  551.8 37.2 %collective-permute-start.58 = (bf16[512,1536]{1,0:T(8,128)(2,1)S(1)}, bf16[512,1536]{1,0:T(8,128)(2,1)}, u32[]{:S(2)}, u32[]{:S(2)}) collective-permute-start(bf16[512,1536]{1,0:T(8,128)(2,1)S(1)} %pad_maximum_fusion.5), channel_id=1, source_target_pairs={{0,1},{1,2},{2,3},{4,5},{5,6},{6,7},{8,9},{9,10},{10,11},{12,13},{... | collective-permute-start | bytes 4718600 | tf_op jit(solution)/shard_map/ppermute | solution.py:399
  558.7 39.6 %collective-permute-start.63 = (bf16[768,1152]{1,0:T(8,128)(2,1)S(1)}, bf16[768,1152]{1,0:T(8,128)(2,1)S(1)}, u32[]{:S(2)}, u32[]{:S(2)}) collective-permute-start(bf16[768,1152]{1,0:T(8,128)(2,1)S(1)} %constant_dynamic-slice_fusion), channel_id=1, source_target_pairs={{0,16},{16,0},{1,17},{17,1},{2,18},{18,2},{3,19},{19,3},{4,20},{20... | collective-permute-start | bytes 5308424 | tf_op jit(solution)/shard_map/ppermute | solution.py:373
  590.8 67.8 %collective-permute-start.61 = (bf16[512,1536]{1,0:T(8,128)(2,1)S(1)}, bf16[512,1536]{1,0:T(8,128)(2,1)}, u32[]{:S(2)}, u32[]{:S(2)}) collective-permute-start(bf16[512,1536]{1,0:T(8,128)(2,1)S(1)} %collective-permute-done.57), channel_id=1, source_target_pairs={{1,0},{2,1},{5,4},{6,5},{9,8},{10,9},{13,12},{14,13},{17,16},{18,1... | collective-permute-start | bytes 4718600 | tf_op jit(solution)/shard_map/ppermute | solution.py:400
  613.5 56.2 %collective-permute-start.60 = (bf16[512,1536]{1,0:T(8,128)(2,1)}, bf16[512,1536]{1,0:T(8,128)(2,1)}, u32[]{:S(2)}, u32[]{:S(2)}) collective-permute-start(bf16[512,1536]{1,0:T(8,128)(2,1)} %collective-permute-done.59), channel_id=1, source_target_pairs={{2,3},{6,7},{10,11},{14,15},{18,19},{22,23},{26,27},{30,31}} | collective-permute-start | bytes 4718600 | tf_op jit(solution)/shard_map/ppermute | solution.py:399
  658.6 36.2 %collective-permute-start.62 = (bf16[512,1536]{1,0:T(8,128)(2,1)}, bf16[512,1536]{1,0:T(8,128)(2,1)}, u32[]{:S(2)}, u32[]{:S(2)}) collective-permute-start(bf16[512,1536]{1,0:T(8,128)(2,1)} %collective-permute-done.61), channel_id=1, source_target_pairs={{1,0},{5,4},{9,8},{13,12},{17,16},{21,20},{25,24},{29,28}} | collective-permute-start | bytes 4718600 | tf_op jit(solution)/shard_map/ppermute | solution.py:400
  695.1 41.6 %collective-permute-start.66 = (bf16[192,1152]{1,0:T(8,128)(2,1)S(1)}, bf16[192,1152]{1,0:T(8,128)(2,1)S(1)}, u32[]{:S(2)}, u32[]{:S(2)}) collective-permute-start(bf16[192,1152]{1,0:T(8,128)(2,1)S(1)} %copy.52), channel_id=1, source_target_pairs={{0,0},{1,4},{2,8},{3,12},{4,1},{5,5},{6,9},{7,13},{8,2},{9,6},{10,... | collective-permute-start | bytes 1327112 | tf_op jit(solution)/shard_map/ppermute | solution.py:378
  (119 other events, 2088.9 us)
Sparse Core Ops, SparseCore 0:
  319.1 120.6 reduce-scatter.6
  600.1 50.2 reduce-scatter.8
